TPU v7x, 32 devices: a whole 2x2x4 slice. The times are simulated.
32 devices in a mesh: rep: 8 (over z, x), space: 4 (over y, core).
Axes of the slice: x: 2, y: 2, z: 4, core: 2. Of those that a mesh axis runs over, the one named last changes fastest.
Arguments:
- positions: float32 [8, 3, 8, 4, 4, 128], P('rep', None, 'space'), may hold values from 0 to 1
- velocities: float32 [8, 3, 8, 4, 4, 128], P('rep', None, 'space'), may hold values from -12 to 12
- thermal_noise: float32 [8, 1, 3, 8, 4, 4, 128], P('rep', None, None, 'space'), may hold values from -6 to 6
- counts: int32 [8, 4, 4], P('space'), may hold values from 64 to 128, as said below
- pair_flags: int32 [13, 8, 4, 4], P(None, 'space'), may hold values 0 or 1
- exit_replica: int32 [8], replicated, may hold values from 0 to 7, each once
Outputs:
- quench_pos: float32 [8, 3, 8, 4, 4, 128], P('rep', None, 'space')
- quench_vel: float32 [8, 3, 8, 4, 4, 128], P('rep', None, 'space')
- dephase_pos: float32 [8, 3, 8, 4, 4, 128], P('rep', None, 'space')
- dephase_vel: float32 [8, 3, 8, 4, 4, 128], P('rep', None, 'space')
Inputs may be any that keep to these rules, and one draw needn't show every extreme that they name: `counts`: the cell with the lowest indices of every aligned slab of 2 planes along the first dimension holds 128 atoms. `exit_replica`: every replica appears exactly once.
All inputs are finite; a program needn't handle non-finite values. No bound on the sum of `pair_flags` on one device may be relied on, other than what follows from the above.
Results may differ from a plain program's by a relative error of at most 0.0003.
Values sent between devices are 32-bit elements; how exact they have to be, the bound alone decides.
No kernel may reach another device: no remote copies, remote signals or barrier semaphores. Data moves between devices by JAX's collectives and lax.ppermute only.
A program may use at most 128 MiB of HBM per device.

v0:
```python
import math

import jax
import jax.numpy as jnp
from jax import lax
from jax.sharding import PartitionSpec as P

QUENCH = 2


CUTOFF_SQ = 1.0
PAIR_A = 3.0
STEP_SIZE = 0.1
ALPHA_MIX = 0.25
EPSILON = 1e-06
FRICTION = math.exp(-0.2)
KICK_SCALE = math.sqrt(1.0 - FRICTION * FRICTION)
HALF_OFFSETS = (
    [(1, p, q) for p in (-1, 0, 1) for q in (-1, 0, 1)]
    + [(0, 1, q) for q in (-1, 0, 1)]
    + [(0, 0, 1)]
)


def with_halo(block, sides, width):
    for axis, dim in sides:
        count = lax.axis_size(axis)
        forward = [(i, i + 1) for i in range(count - 1)]
        forward.append((count - 1, 0))
        backward = [(target, source) for source, target in forward]
        low = lax.ppermute(
            lax.slice_in_dim(block, block.shape[dim] - width, None, axis=dim), axis, forward
        )
        high = lax.ppermute(lax.slice_in_dim(block, 0, width, axis=dim), axis, backward)
        block = jnp.concatenate([low, block, high], axis=dim)
    return block


def broadcast(value, axis, root):
    mine = lax.axis_index(axis) == root
    return lax.psum(jnp.where(mine, value, jnp.zeros_like(value)), axis)


def flag_lookup(ox, oy, oz):
    for index, entry in enumerate(HALF_OFFSETS):
        if entry == (ox, oy, oz):
            return (index, True)
        if entry == (-ox, -oy, -oz):
            return (index, False)
    return (0, True)


def plane_pass(pos_win, occ_win, flag_win, embed_win):
    slot_count = pos_win.shape[-1]
    center = pos_win[:, 1]
    occ_self = occ_win[1]
    diagonal = 1.0 - jnp.eye(slot_count, dtype=jnp.float32)
    if embed_win is None:
        result = jnp.zeros(occ_self.shape, jnp.float32)
    else:
        result = jnp.zeros(center.shape, jnp.float32)
        embed_self = embed_win[1]
    for ox in (-1, 0, 1):
        for oy in (-1, 0, 1):
            for oz in (-1, 0, 1):
                moved = (-oy, -oz)
                partner = jnp.roll(pos_win[:, 1 + ox], moved, axis=(1, 2))
                lattice = jnp.array([ox, oy, oz], dtype=jnp.float32)[:, None, None, None, None]
                displace = center[..., :, None] - partner[..., None, :] - lattice
                squared = jnp.sum(displace * displace, axis=0)
                occ_peer = jnp.roll(occ_win[1 + ox], moved, axis=(0, 1))
                weight = occ_self[..., :, None] * occ_peer[..., None, :]
                if ox == 0 and oy == 0 and (oz == 0):
                    weight = weight * diagonal
                else:
                    index, forward = flag_lookup(ox, oy, oz)
                    if forward:
                        flag = flag_win[index, 1]
                    else:
                        flag = jnp.roll(flag_win[index, 1 + ox], moved, axis=(0, 1))
                    weight = weight * flag[..., None, None]
                closeness = jnp.maximum(1.0 - squared / CUTOFF_SQ, 0.0)
                if embed_win is None:
                    result = (
                        result
                        + jnp.sum(weight * closeness * closeness * closeness, axis=-1) / slot_count
                    )
                else:
                    embed_peer = jnp.roll(embed_win[1 + ox], moved, axis=(0, 1))
                    slope = (
                        weight
                        * (
                            -4.0 * PAIR_A * closeness * closeness * closeness
                            - 3.0
                            * (embed_self[..., :, None] + embed_peer[..., None, :])
                            * closeness
                            * closeness
                        )
                        / slot_count
                    )
                    result = result - 2.0 * jnp.sum(slope[None] * displace, axis=-1)
    return result


def blocked(pos_win, occ_win, flag_win, embed_win):
    planes = pos_win.shape[1] - 2

    def one_plane(index):
        part_pos = lax.dynamic_slice_in_dim(pos_win, index, 3, 1)
        part_occ = lax.dynamic_slice_in_dim(occ_win, index, 3, 0)
        part_flag = lax.dynamic_slice_in_dim(flag_win, index, 3, 1)
        part_embed = None if embed_win is None else lax.dynamic_slice_in_dim(embed_win, index, 3, 0)
        return plane_pass(part_pos, part_occ, part_flag, part_embed)

    stacked = lax.map(one_plane, jnp.arange(planes, dtype=jnp.int32))
    if embed_win is None:
        return stacked
    return jnp.moveaxis(stacked, 0, 1)


def force_local(coords, occ_wide, flag_wide):
    pos_pad = with_halo(coords, (("space", 1),), 1)
    occ_pad = occ_wide[1:-1]
    flag_pad = flag_wide[:, 1:-1]
    density = blocked(pos_pad, occ_pad, flag_pad, None)
    embed = -1.0 / jnp.sqrt(1.0 + density)
    embed_pad = with_halo(embed, (("space", 0),), 1)
    return blocked(pos_pad, occ_pad, flag_pad, embed_pad)


def body(positions, velocities, thermal_noise, counts, pair_flags, exit_replica):
    start_pos = positions[0]
    slot_count = start_pos.shape[-1]
    tables = jnp.concatenate([counts[None], pair_flags], axis=0)
    rims = with_halo(tables, (("space", 1),), 2)
    occ_wide = (jnp.arange(slot_count, dtype=jnp.int32) < rims[0][..., None]).astype(jnp.float32)
    flag_wide = rims[1:].astype(jnp.float32)
    occupied = occ_wide[2:-2]
    start_vel = velocities[0] * occupied[None]
    coords, motion = (start_pos, start_vel)
    first_force = None
    for quench_step in range(QUENCH):
        forces = force_local(coords, occ_wide, flag_wide)
        if quench_step == 0:
            first_force = forces
        motion = motion + STEP_SIZE * forces
        vel_sq, force_sq = lax.psum((jnp.sum(motion * motion), jnp.sum(forces * forces)), "space")
        mixing = jnp.sqrt(vel_sq / (force_sq + EPSILON))
        motion = (1.0 - ALPHA_MIX) * motion + ALPHA_MIX * mixing * forces
        coords = coords + STEP_SIZE * motion
    quench_pos, quench_vel = (coords, motion)
    chosen = exit_replica[0]
    exit_pos, exit_vel, exit_force = (
        broadcast(start_pos, "rep", chosen),
        broadcast(start_vel, "rep", chosen),
        broadcast(first_force, "rep", chosen),
    )
    coords, motion, forces = (exit_pos, exit_vel, exit_force)
    noise_rep = thermal_noise[0]
    motion = motion + STEP_SIZE * forces
    motion = FRICTION * motion + KICK_SCALE * occupied[None] * noise_rep[0]
    coords = coords + STEP_SIZE * motion
    return (quench_pos[None], quench_vel[None], coords[None], motion[None])


def solution(mesh):
    placed = (
        P("rep", None, "space", None, None, None),
        P("rep", None, "space", None, None, None),
        P("rep", None, None, "space", None, None, None),
        P("space", None, None),
        P(None, "space", None, None),
        P(),
    )
    return jax.shard_map(
        body,
        mesh=mesh,
        in_specs=placed,
        out_specs=(
            P("rep", None, "space", None, None, None),
            P("rep", None, "space", None, None, None),
            P("rep", None, "space", None, None, None),
            P("rep", None, "space", None, None, None),
        ),
        check_vma=False,
    )
```

profile of v0, /device:TPU:0, one launch (start us, length us, event | category | flops | bytes accessed | tf_op | source)
XLA Modules:
  0.0 789.6 jit_solution(15408914594264077955)
XLA Ops:
  18.6 119.0 %while.44 = (s32[]{:T(128)}, f32[2,4,4,128]{3,2,1,0:T(4,128)}, s32[2]{0:T(128)}, f32[4,4,4,128]{3,2,1,0:T(4,128)S(1)}, f32[13,4,4,4]{3,2,1,0:T(4,128)S(1)}, /*in...) while((s32[]{:T(128)}, f32[2,4,4,128]{3,2,1,0:T(4,128)}, ...), condition=%wide.region_55.56_spmd.clone, body=%wide.region_0.55_spmd.sunk.clone.sunk | while | flops 134037800 | bytes 66400104 | solution.py:115
  25.7 11.8 %fusion.1086 = (f32[4,4,128,128]{3,2,1,0:T(8,128)}, f32[4,4,128,128]{3,2,1,0:T(8,128)}, f32[4,4,128,128]{3,2,1,0:T(8,128)}, f32[4,4,128,128]{3,2,1,0:T(8,128)}, ...) fusion(f32[3]{0:T(128)} %get-tuple-element.4464, ...), kind=kLoop, calls=%fused_computation.49.clone.1 | loop fusion | flops 28049408 | bytes 10731628 | tf_op jit(solution)/shard_map/while/body/eval_jaxpr/reduce_sum | solution.py:70
  51.4 9.0 %fusion.1082 = (f32[4,4,128,128]{3,2,1,0:T(8,128)S(1)}, f32[4,4,128,128]{3,2,1,0:T(8,128)S(1)}, f32[4,4,128,128]{3,2,1,0:T(8,128)S(1)}, f32[4,4,128,128]{3,2,1,0...) fusion(f32[3,4,4,128]{3,2,1,0:T(4,128)S(1)} %pad_maximum_fusion, ...), kind=kLoop, calls=%fused_computation.51.clone.1 | loop fusion | flops 28835840 | bytes 10756192 | tf_op jit(solution)/shard_map/while/body/eval_jaxpr/reduce_sum | solution.py:70
  85.2 11.8 %fusion.1086 = (f32[4,4,128,128]{3,2,1,0:T(8,128)}, f32[4,4,128,128]{3,2,1,0:T(8,128)}, f32[4,4,128,128]{3,2,1,0:T(8,128)}, f32[4,4,128,128]{3,2,1,0:T(8,128)}, ...) fusion(f32[3]{0:T(128)} %get-tuple-element.4464, ...), kind=kLoop, calls=%fused_computation.49.clone.1 | loop fusion | flops 28049408 | bytes 10731628 | tf_op jit(solution)/shard_map/while/body/eval_jaxpr/reduce_sum | solution.py:70
  110.9 9.0 %fusion.1082 = (f32[4,4,128,128]{3,2,1,0:T(8,128)S(1)}, f32[4,4,128,128]{3,2,1,0:T(8,128)S(1)}, f32[4,4,128,128]{3,2,1,0:T(8,128)S(1)}, f32[4,4,128,128]{3,2,1,0...) fusion(f32[3,4,4,128]{3,2,1,0:T(4,128)S(1)} %pad_maximum_fusion, ...), kind=kLoop, calls=%fused_computation.51.clone.1 | loop fusion | flops 28835840 | bytes 10756192 | tf_op jit(solution)/shard_map/while/body/eval_jaxpr/reduce_sum | solution.py:70
  142.7 214.0 %while.45 = (s32[]{:T(128)}, f32[2,3,4,4,128]{4,3,2,1,0:T(4,128)}, s32[2]{0:T(128)S(1)}, f32[4,4,4,128]{3,2,1,0:T(4,128)S(1)}, f32[13,4,4,4]{3,2,1,0:T(4,128)S(1...) while((s32[]{:T(128)}, f32[2,3,4,4,128]{4,3,2,1,0:T(4,128)}, ...), condition=%wide.region_111.112_spmd.clone, body=%wide.region_56.111_spmd.sunk.clone.sunk | while | flops 260892960 | bytes 136181376 | solution.py:115
  166.6 10.8 %multiply_reduce_fusion.126 = (f32[4,4,128,128]{3,2,1,0:T(8,128)}, f32[4,4,128,128]{3,2,1,0:T(8,128)}, f32[4,4,128,128]{3,2,1,0:T(8,128)}, f32[4,4,128,128]{3,2,...) fusion(f32[3,4,4,128]{3,2,1,0:T(4,128)S(1)} %pad_maximum_fusion, ...), kind=kLoop, calls=%fused_computation.512.clone.1 | loop fusion | flops 28835840 | bytes 10756192 | tf_op jit(solution)/shard_map/while/body/eval_jaxpr/reduce_sum | solution.py:70
  200.1 7.8 multiply_reduce_fusion.132
  210.7 7.8 multiply_reduce_fusion.131
  234.6 7.0 multiply_reduce_fusion.129
  242.3 7.7 multiply_reduce_fusion.130
  259.6 10.8 %multiply_reduce_fusion.126 = (f32[4,4,128,128]{3,2,1,0:T(8,128)}, f32[4,4,128,128]{3,2,1,0:T(8,128)}, f32[4,4,128,128]{3,2,1,0:T(8,128)}, f32[4,4,128,128]{3,2,...) fusion(f32[3,4,4,128]{3,2,1,0:T(4,128)S(1)} %pad_maximum_fusion, ...), kind=kLoop, calls=%fused_computation.512.clone.1 | loop fusion | flops 28835840 | bytes 10756192 | tf_op jit(solution)/shard_map/while/body/eval_jaxpr/reduce_sum | solution.py:70
  293.1 7.8 multiply_reduce_fusion.132
  303.7 7.8 multiply_reduce_fusion.131
  335.3 7.7 multiply_reduce_fusion.130
  360.3 8.6 %all-reduce.2 = (f32[]{:T(128)}, f32[]{:T(128)}) all-reduce(f32[]{:T(128)} %get-tuple-element.2206, f32[]{:T(128)} %multiply_reduce_fusion.108), channel_id=1, replica_groups=mesh['rep'=8,'space'=4] {'space'}, use_global_device_ids=true, to_apply=%region_113.114 | all-reduce | flops 2 | bytes 16 | tf_op jit(solution)/shard_map/psum | solution.py:147
  376.3 119.6 %while.46 = (s32[]{:T(128)}, f32[2,4,4,128]{3,2,1,0:T(4,128)}, s32[2]{0:T(128)}, f32[4,4,4,128]{3,2,1,0:T(4,128)S(1)}, f32[13,4,4,4]{3,2,1,0:T(4,128)S(1)}, /*in...) while((s32[]{:T(128)}, f32[2,4,4,128]{3,2,1,0:T(4,128)}, ...), condition=%wide.region_171.172_spmd.clone, body=%wide.region_116.171_spmd.sunk.clone.sunk | while | flops 134037800 | bytes 66400104 | solution.py:115
  383.6 11.8 %fusion.1198 = (f32[4,4,128,128]{3,2,1,0:T(8,128)}, f32[4,4,128,128]{3,2,1,0:T(8,128)}, f32[4,4,128,128]{3,2,1,0:T(8,128)}, f32[4,4,128,128]{3,2,1,0:T(8,128)}, ...) fusion(f32[3]{0:T(128)} %get-tuple-element.4737, ...), kind=kLoop, calls=%fused_computation.1150.clone.1 | loop fusion | flops 28049408 | bytes 10731628 | tf_op jit(solution)/shard_map/while/body/eval_jaxpr/reduce_sum | solution.py:70
  409.4 9.0 %fusion.1194 = (f32[4,4,128,128]{3,2,1,0:T(8,128)S(1)}, f32[4,4,128,128]{3,2,1,0:T(8,128)S(1)}, f32[4,4,128,128]{3,2,1,0:T(8,128)S(1)}, f32[4,4,128,128]{3,2,1,0...) fusion(f32[3,4,4,128]{3,2,1,0:T(4,128)S(1)} %pad_maximum_fusion, ...), kind=kLoop, calls=%fused_computation.1152.clone.1 | loop fusion | flops 28835840 | bytes 10756192 | tf_op jit(solution)/shard_map/while/body/eval_jaxpr/reduce_sum | solution.py:70
  443.4 11.8 %fusion.1198 = (f32[4,4,128,128]{3,2,1,0:T(8,128)}, f32[4,4,128,128]{3,2,1,0:T(8,128)}, f32[4,4,128,128]{3,2,1,0:T(8,128)}, f32[4,4,128,128]{3,2,1,0:T(8,128)}, ...) fusion(f32[3]{0:T(128)} %get-tuple-element.4737, ...), kind=kLoop, calls=%fused_computation.1150.clone.1 | loop fusion | flops 28049408 | bytes 10731628 | tf_op jit(solution)/shard_map/while/body/eval_jaxpr/reduce_sum | solution.py:70
  469.2 9.0 %fusion.1194 = (f32[4,4,128,128]{3,2,1,0:T(8,128)S(1)}, f32[4,4,128,128]{3,2,1,0:T(8,128)S(1)}, f32[4,4,128,128]{3,2,1,0:T(8,128)S(1)}, f32[4,4,128,128]{3,2,1,0...) fusion(f32[3,4,4,128]{3,2,1,0:T(4,128)S(1)} %pad_maximum_fusion, ...), kind=kLoop, calls=%fused_computation.1152.clone.1 | loop fusion | flops 28835840 | bytes 10756192 | tf_op jit(solution)/shard_map/while/body/eval_jaxpr/reduce_sum | solution.py:70
  501.2 203.7 %while.47 = (s32[]{:T(128)}, f32[2,3,4,4,128]{4,3,2,1,0:T(4,128)}, s32[2]{0:T(128)S(1)}, f32[4,4,4,128]{3,2,1,0:T(4,128)S(1)}, f32[13,4,4,4]{3,2,1,0:T(4,128)S(1...) while((s32[]{:T(128)}, f32[2,3,4,4,128]{4,3,2,1,0:T(4,128)}, ...), condition=%wide.region_227.228_spmd.clone, body=%wide.region_172.227_spmd.sunk.clone.sunk | while | flops 260892960 | bytes 136181376 | solution.py:115
  525.2 10.8 %multiply_reduce_fusion.134 = (f32[4,4,128,128]{3,2,1,0:T(8,128)}, f32[4,4,128,128]{3,2,1,0:T(8,128)}, f32[4,4,128,128]{3,2,1,0:T(8,128)}, f32[4,4,128,128]{3,2,...) fusion(f32[3,4,4,128]{3,2,1,0:T(4,128)S(1)} %pad_maximum_fusion, ...), kind=kLoop, calls=%fused_computation.1613.clone.1 | loop fusion | flops 28835840 | bytes 10756192 | tf_op jit(solution)/shard_map/while/body/eval_jaxpr/reduce_sum | solution.py:70
  558.6 7.8 multiply_reduce_fusion.140
  569.3 7.8 multiply_reduce_fusion.139
  600.9 7.7 multiply_reduce_fusion.138
  618.1 10.8 %multiply_reduce_fusion.134 = (f32[4,4,128,128]{3,2,1,0:T(8,128)}, f32[4,4,128,128]{3,2,1,0:T(8,128)}, f32[4,4,128,128]{3,2,1,0:T(8,128)}, f32[4,4,128,128]{3,2,...) fusion(f32[3,4,4,128]{3,2,1,0:T(4,128)S(1)} %pad_maximum_fusion, ...), kind=kLoop, calls=%fused_computation.1613.clone.1 | loop fusion | flops 28835840 | bytes 10756192 | tf_op jit(solution)/shard_map/while/body/eval_jaxpr/reduce_sum | solution.py:70
  651.5 7.8 multiply_reduce_fusion.140
  662.2 7.8 multiply_reduce_fusion.139
  693.8 7.7 multiply_reduce_fusion.138
  707.8 7.9 all-reduce.1
  718.5 62.3 %all-reduce.5.cloned.1.call-done = (f32[3,2,4,4,128]{4,3,2,1,0:T(4,128)}, f32[3,2,4,4,128]{4,3,2,1,0:T(4,128)}, f32[3,2,4,4,128]{4,3,2,1,0:T(4,128)}) async-done(((f32[3,2,4,4,128]{4,3,2,1,0:T(4,128)}, f32[3,2,4,4,128]{4,3,2,1,0:T(4,128)}, f32[3,2,4,4,128]{4,3,2,1,0:T(4,128)}), (f32[3,2,4,4,128]{4,3,2,1,0:T(4,128)}, f32[3,2,4,4,128]{4,3,2,1,0:T(4,128)}, ...) | async-done | bytes 147472 | tf_op jit(solution)/shard_map/psum | solution.py:41
  (2107 shorter events, 391.9 us)
Async XLA Ops:
  7.2 773.6 %all-reduce.5.cloned.1.call-start = ((), (), s32[]{:S(2)}) async-start(), calls=%async_computation | async-start | bytes 294912 | tf_op jit(solution)/shard_map/psum | solution.py:41
  8.8 5.7 collective-permute-start
  9.3 5.2 collective-permute-start.1
  12.1 4.5 collective-permute-start.2
  12.7 3.9 collective-permute-start.3
  21.8 28.3 %copy-start.58 = (f32[3,1,4,128]{3,2,1,0:T(4,128)}, f32[3,1,4,128]{3,2,1,0:T(4,128)S(1)}, u32[]{:S(2)}) copy-start(f32[3,1,4,128]{3,2,1,0:T(4,128)S(1)} %get-tuple-element.3382) | copy-start | bytes 18436 | tf_op jit(solution)/shard_map/while
  81.3 28.3 %copy-start.58 = (f32[3,1,4,128]{3,2,1,0:T(4,128)}, f32[3,1,4,128]{3,2,1,0:T(4,128)S(1)}, u32[]{:S(2)}) copy-start(f32[3,1,4,128]{3,2,1,0:T(4,128)S(1)} %get-tuple-element.3382) | copy-start | bytes 18436 | tf_op jit(solution)/shard_map/while
  138.3 3.1 collective-permute-start.4
  139.5 2.0 collective-permute-start.5
  164.9 12.5 %copy-start.8 = (f32[3,4,4,128]{3,2,1,0:T(4,128)}, f32[3,4,4,128]{3,2,1,0:T(4,128)S(1)}, u32[]{:S(2)}) copy-start(f32[3,4,4,128]{3,2,1,0:T(4,128)S(1)} %pad_maximum_fusion.654) | copy-start | bytes 73732 | tf_op jit(solution)/shard_map/while
  165.1 12.4 %copy-start.12 = (f32[3,4,4,128]{3,2,1,0:T(4,128)}, f32[3,4,4,128]{3,2,1,0:T(4,128)S(1)}, u32[]{:S(2)}) copy-start(f32[3,4,4,128]{3,2,1,0:T(4,128)S(1)} %pad_maximum_fusion.653) | copy-start | bytes 73732 | tf_op jit(solution)/shard_map/while
  165.1 12.4 %copy-start.16 = (f32[3,4,4,128]{3,2,1,0:T(4,128)}, f32[3,4,4,128]{3,2,1,0:T(4,128)S(1)}, u32[]{:S(2)}) copy-start(f32[3,4,4,128]{3,2,1,0:T(4,128)S(1)} %pad_maximum_fusion.652) | copy-start | bytes 73732 | tf_op jit(solution)/shard_map/while
  165.1 12.3 %copy-start.28 = (f32[3,4,4,128]{3,2,1,0:T(4,128)}, f32[3,4,4,128]{3,2,1,0:T(4,128)S(1)}, u32[]{:S(2)}) copy-start(f32[3,4,4,128]{3,2,1,0:T(4,128)S(1)} %pad_maximum_fusion.650) | copy-start | bytes 73732 | tf_op jit(solution)/shard_map/while
  165.1 12.3 %copy-start.32 = (f32[3,4,4,128]{3,2,1,0:T(4,128)}, f32[3,4,4,128]{3,2,1,0:T(4,128)S(1)}, u32[]{:S(2)}) copy-start(f32[3,4,4,128]{3,2,1,0:T(4,128)S(1)} %pad_maximum_fusion.648) | copy-start | bytes 73732 | tf_op jit(solution)/shard_map/while
  257.9 12.5 %copy-start.8 = (f32[3,4,4,128]{3,2,1,0:T(4,128)}, f32[3,4,4,128]{3,2,1,0:T(4,128)S(1)}, u32[]{:S(2)}) copy-start(f32[3,4,4,128]{3,2,1,0:T(4,128)S(1)} %pad_maximum_fusion.654) | copy-start | bytes 73732 | tf_op jit(solution)/shard_map/while
  258.0 12.4 %copy-start.12 = (f32[3,4,4,128]{3,2,1,0:T(4,128)}, f32[3,4,4,128]{3,2,1,0:T(4,128)S(1)}, u32[]{:S(2)}) copy-start(f32[3,4,4,128]{3,2,1,0:T(4,128)S(1)} %pad_maximum_fusion.653) | copy-start | bytes 73732 | tf_op jit(solution)/shard_map/while
  258.1 12.4 %copy-start.16 = (f32[3,4,4,128]{3,2,1,0:T(4,128)}, f32[3,4,4,128]{3,2,1,0:T(4,128)S(1)}, u32[]{:S(2)}) copy-start(f32[3,4,4,128]{3,2,1,0:T(4,128)S(1)} %pad_maximum_fusion.652) | copy-start | bytes 73732 | tf_op jit(solution)/shard_map/while
  258.1 12.3 %copy-start.28 = (f32[3,4,4,128]{3,2,1,0:T(4,128)}, f32[3,4,4,128]{3,2,1,0:T(4,128)S(1)}, u32[]{:S(2)}) copy-start(f32[3,4,4,128]{3,2,1,0:T(4,128)S(1)} %pad_maximum_fusion.650) | copy-start | bytes 73732 | tf_op jit(solution)/shard_map/while
  371.8 3.3 collective-permute-start.6
  371.8 3.3 collective-permute-start.7
  379.7 28.4 %copy-start.59 = (f32[3,1,4,128]{3,2,1,0:T(4,128)}, f32[3,1,4,128]{3,2,1,0:T(4,128)S(1)}, u32[]{:S(2)}) copy-start(f32[3,1,4,128]{3,2,1,0:T(4,128)S(1)} %get-tuple-element.3885) | copy-start | bytes 18436 | tf_op jit(solution)/shard_map/while
  439.5 28.4 %copy-start.59 = (f32[3,1,4,128]{3,2,1,0:T(4,128)}, f32[3,1,4,128]{3,2,1,0:T(4,128)S(1)}, u32[]{:S(2)}) copy-start(f32[3,1,4,128]{3,2,1,0:T(4,128)S(1)} %get-tuple-element.3885) | copy-start | bytes 18436 | tf_op jit(solution)/shard_map/while
  496.6 3.3 collective-permute-start.8
  498.4 1.5 collective-permute-start.9
  523.5 12.5 %copy-start.10 = (f32[3,4,4,128]{3,2,1,0:T(4,128)}, f32[3,4,4,128]{3,2,1,0:T(4,128)S(1)}, u32[]{:S(2)}) copy-start(f32[3,4,4,128]{3,2,1,0:T(4,128)S(1)} %pad_maximum_fusion.792) | copy-start | bytes 73732 | tf_op jit(solution)/shard_map/while
  523.7 12.4 %copy-start.14 = (f32[3,4,4,128]{3,2,1,0:T(4,128)}, f32[3,4,4,128]{3,2,1,0:T(4,128)S(1)}, u32[]{:S(2)}) copy-start(f32[3,4,4,128]{3,2,1,0:T(4,128)S(1)} %pad_maximum_fusion.791) | copy-start | bytes 73732 | tf_op jit(solution)/shard_map/while
  523.7 12.4 %copy-start.18 = (f32[3,4,4,128]{3,2,1,0:T(4,128)}, f32[3,4,4,128]{3,2,1,0:T(4,128)S(1)}, u32[]{:S(2)}) copy-start(f32[3,4,4,128]{3,2,1,0:T(4,128)S(1)} %pad_maximum_fusion.790) | copy-start | bytes 73732 | tf_op jit(solution)/shard_map/while
  523.7 12.3 %copy-start.30 = (f32[3,4,4,128]{3,2,1,0:T(4,128)}, f32[3,4,4,128]{3,2,1,0:T(4,128)S(1)}, u32[]{:S(2)}) copy-start(f32[3,4,4,128]{3,2,1,0:T(4,128)S(1)} %pad_maximum_fusion.788) | copy-start | bytes 73732 | tf_op jit(solution)/shard_map/while
  616.4 12.5 %copy-start.10 = (f32[3,4,4,128]{3,2,1,0:T(4,128)}, f32[3,4,4,128]{3,2,1,0:T(4,128)S(1)}, u32[]{:S(2)}) copy-start(f32[3,4,4,128]{3,2,1,0:T(4,128)S(1)} %pad_maximum_fusion.792) | copy-start | bytes 73732 | tf_op jit(solution)/shard_map/while
  616.5 12.4 %copy-start.14 = (f32[3,4,4,128]{3,2,1,0:T(4,128)}, f32[3,4,4,128]{3,2,1,0:T(4,128)S(1)}, u32[]{:S(2)}) copy-start(f32[3,4,4,128]{3,2,1,0:T(4,128)S(1)} %pad_maximum_fusion.791) | copy-start | bytes 73732 | tf_op jit(solution)/shard_map/while
  616.6 12.4 %copy-start.18 = (f32[3,4,4,128]{3,2,1,0:T(4,128)}, f32[3,4,4,128]{3,2,1,0:T(4,128)S(1)}, u32[]{:S(2)}) copy-start(f32[3,4,4,128]{3,2,1,0:T(4,128)S(1)} %pad_maximum_fusion.790) | copy-start | bytes 73732 | tf_op jit(solution)/shard_map/while
  616.6 12.3 %copy-start.30 = (f32[3,4,4,128]{3,2,1,0:T(4,128)}, f32[3,4,4,128]{3,2,1,0:T(4,128)S(1)}, u32[]{:S(2)}) copy-start(f32[3,4,4,128]{3,2,1,0:T(4,128)S(1)} %pad_maximum_fusion.788) | copy-start | bytes 73732 | tf_op jit(solution)/shard_map/while
  (449 other events, 2197.5 us)
Sparse Core Ops, SparseCore 0:
  707.9 72.8 all-reduce.4
where the time goes:
time: 803 us; the launch traced here: 790 us
  other arithmetic  545 us (68%)
  loops' own time  74.1 us (9%)
  waiting for transfers between devices  63.9 us (8%)
  local copies, waits for them, and re-layouts  63 us (8%)
  between operations  17.8 us (2%)
  blocking collectives  16.4 us (2%)
  starting transfers between devices  9.72 us (1%)
    reduce_sum x28, other arithmetic, plane_pass(): result = result - 2.0 * jnp.sum(slope[None] * displace, axis=-1)  186 us
    reduce_sum x16, other arithmetic, plane_pass(): squared = jnp.sum(displace * displace, axis=0)  151 us
    another operation x4, loops' own time, blocked(): stacked = lax.map(one_plane, jnp.arange(planes, dtype=jnp.int32))  74.1 us
    div x36, other arithmetic, plane_pass(): weight * (-4.0 * PAIR_A * closeness * closeness * closeness - 3.0 * (embe...  71.5 us
    psum x1, waiting for transfers between devices, broadcast(): return lax.psum(jnp.where(mine, value, jnp.zeros_like(value)), axis)  62.3 us
    reduce_sum x20, other arithmetic, plane_pass(): jnp.sum(weight * closeness * closeness * closeness, axis=-1) / slot_count  55.2 us
    concatenate x256, other arithmetic, plane_pass(): partner = jnp.roll(pos_win[:, 1 + ox], moved, axis=(1, 2))  25.6 us
    concatenate x104, other arithmetic, plane_pass(): flag = jnp.roll(flag_win[index, 1 + ox], moved, axis=(0, 1))  20 us
  transfers between devices with their start and end apart: 11, of which 2 were waited for; matrix products, arithmetic and copies ran while one was open for 1% of the time, Pallas kernels for 0%

commit v1 on v0

v1 whole, which is shorter than its diff:
```python
import functools
import math

import jax
import jax.numpy as jnp
from jax import lax
from jax.experimental import pallas as pl
from jax.experimental.pallas import tpu as pltpu
from jax.sharding import PartitionSpec as P

QUENCH = 2
STEP_SIZE = 0.1
ALPHA_MIX = 0.25
EPSILON = 1e-06
FRICTION = math.exp(-0.2)
KICK_SCALE = math.sqrt(1.0 - FRICTION * FRICTION)
HALF_OFFSETS = (
    [(1, p, q) for p in (-1, 0, 1) for q in (-1, 0, 1)]
    + [(0, 1, q) for q in (-1, 0, 1)]
    + [(0, 0, 1)]
)
OFFSETS = [(i, j, k) for i in (-1, 0, 1) for j in (-1, 0, 1) for k in (-1, 0, 1)]
FAR = 1.0e6
BF = jnp.bfloat16
F32 = jnp.float32
KDIM = 64


def ring(axis, shift):
    count = lax.axis_size(axis)
    return [(i, (i + shift) % count) for i in range(count)]


def flag_of(offset):
    for index, entry in enumerate(HALF_OFFSETS):
        if entry == offset:
            return index, True
        if entry == tuple(-v for v in offset):
            return index, False
    return None


def split3(value):
    high = value.astype(BF).astype(F32)
    rest = value - high
    mid = rest.astype(BF).astype(F32)
    return high, mid, (rest - mid).astype(BF).astype(F32)


def wrap(index, size):
    index = jnp.where(index < 0, index + size, index)
    return jnp.where(index >= size, index - size, index)


def build_list(dims, cnt_dummy, flags, flags_lo, list_ref):
    planes, gy, gz = dims
    ey, ez = gy + 2, gz + 2
    dummy = (planes + 2) * ey * ez

    def row(y, _):
        for p in range(planes):
            for z in range(gz):
                cell = (p * gy + y) * gz + z
                for slot, (ox, oy, oz) in enumerate(OFFSETS):
                    ext = ((p + 1 + ox) * ey + (y + 1 + oy)) * ez + (z + 1 + oz)
                    found = flag_of((ox, oy, oz))
                    if found is None:
                        list_ref[cell * 27 + slot] = ext
                        continue
                    index, forward = found
                    if forward:
                        flag = flags[index, p, y, z]
                    else:
                        jy, jz = wrap(y + oy, gy), (z + oz) % gz
                        if p + ox < 0:
                            flag = flags_lo[index, 0, jy, jz]
                        else:
                            flag = flags[index, p + ox, jy, jz]
                    list_ref[cell * 27 + slot] = jnp.where(flag > 0, ext, dummy)
        return 0

    lax.fori_loop(0, gy, row, 0)


def build_partners(dims, pos, cnt, emb, lhs_ref, yb_ref, sel_ref):
    planes, gy, gz = dims
    ey, ez = gy + 2, gz + 2
    slots = lhs_ref.shape[1]
    rows = lax.broadcasted_iota(jnp.int32, (8, slots), 0)
    lane = lax.broadcasted_iota(jnp.int32, (8, slots), 1)

    def one(j, which, at, y, z, by, bz):
        full = (8, slots)
        raw = [
            jnp.broadcast_to(pos[which][k, at, by, pl.ds(bz, 1), :], full) for k in range(3)
        ]
        xx = raw[0] + (j - 0.5 - (planes + 1) / 2)
        yy = raw[1] + ((y - 0.5 - (gy + 1) / 2) if isinstance(y, int) else (y.astype(F32) - 0.5 - (gy + 1) / 2))
        zz = raw[2] + (z - 0.5 - (gz + 1) / 2)
        norm = xx * xx + yy * yy + zz * zz
        norm = jnp.where(lane < cnt[which][at, by, bz], norm, norm + FAR)
        value = jnp.where(rows == 0, xx, jnp.where(rows == 1, yy, zz))
        value = jnp.where(rows == 3, norm, value)
        value = jnp.where(rows >= 4, 1.0, value)
        if emb is not None:
            e = jnp.broadcast_to(emb[which][at, by, pl.ds(bz, 1), :], full) * 0.25
            value = jnp.where(rows == 6, e, value)
        h, m, l = split3(value)
        return jnp.concatenate([h, h, h, m, m, m, l, l], axis=0)

    for j in range(planes + 2):
        which, at = (0, 0) if j == 0 else ((2, 0) if j == planes + 1 else (1, j - 1))

        def line(y, _):
            by = wrap(y - 1, gy)
            for z in range(ez):
                bz = (z - 1) % gz
                tall = one(j, which, at, y, z, by, bz)
                ext = (j * ey + y) * ez + z
                lhs_ref[ext] = tall.T.astype(BF)
            return 0

        lax.fori_loop(0, ey, line, 0)
        if yb_ref is not None:

            def broad(y, _):
                for z in range(gz):
                    out = jnp.concatenate(
                        split3(
                            jnp.concatenate(
                                [pos[which][k, at, y, pl.ds(z, 1), :] for k in range(3)]
                                + [jnp.zeros((5, slots), F32)],
                                axis=0,
                            )
                        ),
                        axis=0,
                    )
                    tall = out.T.astype(BF)
                    wide = jnp.dot(tall, sel_ref[...], preferred_element_type=F32)
                    cell = (j * gy + y) * gz + z
                    for k in range(3):
                        yb_ref[cell, k] = wide[:, k * slots : (k + 1) * slots]
                return 0

            lax.fori_loop(0, gy, broad, 0)
    dummy = (planes + 2) * ey * ez
    value = jnp.where(rows == 3, FAR, jnp.where(rows >= 4, 1.0, 0.0))
    h, m, l = split3(value)
    lhs_ref[dummy] = jnp.concatenate([h, h, h, m, m, m, l, l], axis=0).T.astype(BF)


def build_center(dims, p, y, z, x3, count, e_row):
    planes, gy, gz = dims
    slots = x3[0].shape[-1]
    full = (8, slots)
    rows = lax.broadcasted_iota(jnp.int32, full, 0)
    lane = lax.broadcasted_iota(jnp.int32, full, 1)
    xx = jnp.broadcast_to(x3[0], full) + (p + 0.5 - (planes + 1) / 2)
    yy = jnp.broadcast_to(x3[1], full) + (y.astype(F32) + 0.5 - (gy + 1) / 2)
    zz = jnp.broadcast_to(x3[2], full) + (z.astype(F32) + 0.5 - (gz + 1) / 2)
    one = 1.0 - (xx * xx + yy * yy + zz * zz)
    one = jnp.where(lane < count, one, one - FAR)
    value = jnp.where(rows == 0, xx, jnp.where(rows == 1, yy, zz)) * 2.0
    value = jnp.where(rows == 4, one, value)
    if e_row is not None:
        value = jnp.where(rows == 5, jnp.broadcast_to(e_row, full) * 0.25, value)
    parts = split3(value)
    us, ws = [], []
    for block in range(8):
        part = parts[block % 3]
        keep = rows < 3
        if block < 3:
            keep = keep | (rows == 4)
        u = jnp.where(keep, part, 0.0)
        if block % 3 == 0:
            u = jnp.where(rows == 3, -1.0, u)
        us.append(u)
        if e_row is not None:
            w = u
            if block < 3:
                w = jnp.where(rows == 5, part, w)
            if block % 3 == 0:
                w = jnp.where(rows == 6, 1.0, w)
            ws.append(w)
    right = jnp.concatenate(us, axis=0).astype(BF)
    if e_row is None:
        return right
    return jnp.concatenate([right, jnp.concatenate(ws, axis=0).astype(BF)], axis=1)


def density_kernel(dims, first, *refs):
    if first:
        (p0, p1, p2, c0, c1, c2, fl, fl_lo, emb_ref, list_ref, lhs_ref) = refs
        build_list(dims, None, fl, fl_lo, list_ref)
    else:
        (p0, p1, p2, c0, c1, c2, list_ref, emb_ref, lhs_ref) = refs
    planes, gy, gz = dims
    slots = lhs_ref.shape[1]
    build_partners(dims, (p0, p1, p2), (c0, c1, c2), None, lhs_ref, None, None)
    lane = lax.broadcasted_iota(jnp.int32, (1, slots), 1)
    for p in range(planes):

        def cell_step(i, _):
            y, z = i // gz, i % gz
            x3 = [p1[k, p, y, pl.ds(z, 1), :] for k in range(3)]
            count = c1[p, y, z]
            right = build_center(dims, p, y, z, x3, count, None)
            cell = p * gy * gz + i
            acc = [jnp.zeros((8, slots), F32) for _ in range(4)]
            for slot in range(27):
                u = jnp.dot(lhs_ref[list_ref[cell * 27 + slot]], right, preferred_element_type=F32)
                for r in range(slots // 8):
                    t = jnp.maximum(u[r * 8 : r * 8 + 8], 0.0)
                    acc[r % 4] = acc[r % 4] + t * t * t
            total = jnp.sum((acc[0] + acc[1]) + (acc[2] + acc[3]), axis=0, keepdims=True)
            total = total - jnp.where(lane < count, 1.0, 0.0)
            emb_ref[p, y, pl.ds(z, 1), :] = -lax.rsqrt(1.0 + total / slots)
            return 0

        lax.fori_loop(0, gy * gz, cell_step, 0)


def force_kernel(dims, *refs):
    (p0, p1, p2, c0, c1, c2, e0, e1, e2, vel, list_ref, sel_ref, f_ref, v_ref, s_ref, lhs_ref, yb_ref) = refs
    planes, gy, gz = dims
    slots = lhs_ref.shape[1]
    build_partners(dims, (p0, p1, p2), (c0, c1, c2), (e0, e1, e2), lhs_ref, yb_ref, sel_ref)
    lane = lax.broadcasted_iota(jnp.int32, (1, slots), 1)
    sums = (jnp.zeros((1, slots), F32), jnp.zeros((1, slots), F32))
    for p in range(planes):

        def cell_step(i, sums):
            y, z = i // gz, i % gz
            x3 = [p1[k, p, y, pl.ds(z, 1), :] for k in range(3)]
            count = c1[p, y, z]
            right = build_center(dims, p, y, z, x3, count, e1[p, y, pl.ds(z, 1), :])
            cell = p * gy * gz + i
            zero = jnp.zeros((8, slots), F32)
            s0, s1, extra = zero, [zero] * 3, [zero] * 3
            for slot, offset in enumerate(OFFSETS):
                both = jnp.dot(lhs_ref[list_ref[cell * 27 + slot]], right, preferred_element_type=F32)
                base = ((p + 1 + offset[0]) * gy + wrap(y + offset[1], gy)) * gz + wrap(z + offset[2], gz)
                part = None
                for r in range(slots // 8):
                    here = slice(r * 8, r * 8 + 8)
                    t = jnp.maximum(both[here, :slots], 0.0)
                    g = t * t * both[here, slots:]
                    part = g if part is None else part + g
                    for k in range(3):
                        s1[k] = s1[k] + g * yb_ref[base, k, here, :]
                s0 = s0 + part
                for k in range(3):
                    if offset[k] == 1:
                        extra[k] = extra[k] + part
                    elif offset[k] == -1:
                        extra[k] = extra[k] - part
            total = jnp.sum(s0, axis=0, keepdims=True)
            ff, vv = sums
            for k in range(3):
                f = (24.0 / slots) * (
                    x3[k] * total - jnp.sum(s1[k] + extra[k], axis=0, keepdims=True)
                )
                f_ref[k, p, y, pl.ds(z, 1), :] = f
                v = jnp.where(lane < count, vel[k, p, y, pl.ds(z, 1), :], 0.0) + STEP_SIZE * f
                v_ref[k, p, y, pl.ds(z, 1), :] = v
                ff = ff + f * f
                vv = vv + v * v
            return ff, vv

        sums = lax.fori_loop(0, gy * gz, cell_step, sums)
    s_ref[...] = jnp.concatenate([sums[0], sums[1], jnp.zeros((6, slots), F32)], axis=0)


def body(positions, velocities, thermal_noise, counts, pair_flags, exit_replica):
    start_pos = positions[0]
    start_vel = velocities[0]
    planes, gy, gz, slots = start_pos.shape[1:]
    dims = (planes, gy, gz)
    up, down = ring("space", 1), ring("space", -1)
    vmem = pl.BlockSpec(memory_space=pltpu.VMEM)
    smem = pl.BlockSpec(memory_space=pltpu.SMEM)
    params = pltpu.CompilerParams(vmem_limit_bytes=56 * 2**20)
    ext = (planes + 2) * (gy + 2) * (gz + 2) + 1
    entries = planes * gy * gz * 27
    cells = planes * gy * gz
    pairs = cells * 27 * slots * slots

    def halo(block, dim):
        low = lax.ppermute(lax.slice_in_dim(block, planes - 1, planes, axis=dim), "space", up)
        high = lax.ppermute(lax.slice_in_dim(block, 0, 1, axis=dim), "space", down)
        return low, high

    count_lo, count_hi = halo(counts, 0)
    flags_lo = lax.ppermute(lax.slice_in_dim(pair_flags, planes - 1, planes, axis=1), "space", up)
    column = jnp.arange(24)[:, None]
    pick = ((column % 8) == (jnp.arange(3 * slots)[None, :] // slots)).astype(BF)
    lhs_scratch = pltpu.VMEM((ext, slots, KDIM), BF)
    emb_shape = jax.ShapeDtypeStruct((planes, gy, gz, slots), F32)
    vec_shape = jax.ShapeDtypeStruct((3, planes, gy, gz, slots), F32)

    coords, motion = start_pos, start_vel
    blocks = None
    pushed = None
    for quench_step in range(QUENCH):
        low, high = halo(coords, 1)
        args = [low, coords, high, count_lo, counts, count_hi]
        specs = [vmem] * 3 + [smem] * 3
        cost = pl.CostEstimate(flops=pairs * 10, bytes_accessed=2**20, transcendentals=0)
        if quench_step == 0:
            embed, blocks = pl.pallas_call(
                functools.partial(density_kernel, dims, True),
                out_shape=(emb_shape, jax.ShapeDtypeStruct((entries,), jnp.int32)),
                in_specs=specs + [smem, smem],
                out_specs=(vmem, smem),
                scratch_shapes=[lhs_scratch],
                compiler_params=params,
                cost_estimate=cost,
                name="density_first",
            )(*args, pair_flags, flags_lo)
        else:
            embed = pl.pallas_call(
                functools.partial(density_kernel, dims, False),
                out_shape=emb_shape,
                in_specs=specs + [smem],
                out_specs=vmem,
                scratch_shapes=[lhs_scratch],
                compiler_params=params,
                cost_estimate=cost,
                name="density_next",
            )(*args, blocks)
        embed_lo, embed_hi = halo(embed, 0)
        forces, pushed_vel, sums = pl.pallas_call(
            functools.partial(force_kernel, dims),
            out_shape=(vec_shape, vec_shape, jax.ShapeDtypeStruct((8, slots), F32)),
            in_specs=specs + [vmem] * 4 + [smem, vmem],
            out_specs=(vmem, vmem, vmem),
            scratch_shapes=[
                lhs_scratch,
                pltpu.VMEM(((planes + 2) * gy * gz, 3, slots, slots), F32),
            ],
            compiler_params=params,
            cost_estimate=pl.CostEstimate(
                flops=pairs * 25, bytes_accessed=2**20, transcendentals=0
            ),
            name="force",
        )(*args, embed_lo, embed, embed_hi, motion, blocks, pick)
        if quench_step == 0:
            pushed = pushed_vel
        total = sums
        for shift in range(1, lax.axis_size("space")):
            total = total + lax.ppermute(sums, "space", ring("space", shift))
        force_sq, vel_sq = jnp.sum(total[0]), jnp.sum(total[1])
        mixing = jnp.sqrt(vel_sq / (force_sq + EPSILON))
        motion = (1.0 - ALPHA_MIX) * pushed_vel + ALPHA_MIX * mixing * forces
        coords = coords + STEP_SIZE * motion

    chosen = exit_replica[0]
    held = jnp.concatenate([start_pos, pushed], axis=0)
    replicas = lax.axis_size("rep")
    me = lax.axis_index("rep")
    if replicas & (replicas - 1) == 0:
        stride = 1
        while stride < replicas:
            other = lax.ppermute(held, "rep", [(i, i ^ stride) for i in range(replicas)])
            mine = ((me ^ chosen) >> (stride.bit_length() - 1)) & 1 == 0
            held = jnp.where(mine, held, other)
            stride *= 2
    else:
        final = held
        for shift in range(1, replicas):
            other = lax.ppermute(held, "rep", ring("rep", shift))
            final = jnp.where((me - shift) % replicas == chosen, other, final)
        held = final
    exit_pos, exit_push = held[:3], held[3:]
    occupied = (jnp.arange(slots, dtype=jnp.int32) < counts[..., None]).astype(F32)
    drift = FRICTION * exit_push + KICK_SCALE * occupied[None] * thermal_noise[0, 0]
    place = exit_pos + STEP_SIZE * drift
    return coords[None], motion[None], place[None], drift[None]


def solution(mesh):
    vector = P("rep", None, "space", None, None, None)
    placed = (
        vector,
        vector,
        P("rep", None, None, "space", None, None, None),
        P("space", None, None),
        P(None, "space", None, None),
        P(),
    )
    return jax.shard_map(
        body, mesh=mesh, in_specs=placed, out_specs=(vector,) * 4, check_vma=False
    )
```

time: 803 us -> 168 us (0.21); the launches traced: 790 us -> 168 us
  other arithmetic: 545 us -> 5.55 us
  Pallas kernels: 0 us -> 114 us
  loops' own time: 74.1 us -> 0 us
  local copies, waits for them, and re-layouts: 63 us -> 8.22 us
  waiting for transfers between devices: 63.9 us -> 22.1 us
  blocking collectives: 16.4 us -> 0 us
  between operations: 17.8 us -> 3.52 us
    reduce_sum x67 -> x2, other arithmetic: 396 us -> 1.2 us  [body(): force_sq, vel_sq = (jnp.sum(total[0]), jnp.sum(total[1]))]
    pallas_call x0 -> x4, Pallas kernels: none -> 114 us  [the longest x2 73.3 us: body(): pl.pallas_call(functools.partial(force_kernel, dims), out_shape=(vec_shap...]
    another operation x4 -> x0, loops' own time: 74.1 us -> none  [blocked(): stacked = lax.map(one_plane, jnp.arange(planes, dtype=jnp.int32))]
    div x38 -> x0, other arithmetic: 73 us -> none  [the longest x36 71.5 us: plane_pass(): weight * (-4.0 * PAIR_A * closeness * closeness * closeness - 3.0 * (embe...]
    concatenate x758 -> x1, other arithmetic: 64.4 us -> 0.02 us  [body(): held = jnp.concatenate([start_pos, pushed], axis=0)]
    psum x1 -> x0, waiting for transfers between devices: 62.3 us -> none  [broadcast(): return lax.psum(jnp.where(mine, value, jnp.zeros_like(value)), axis)]
    slice x238 -> x7, local copies, waits for them, and re-layouts: 37.5 us -> 2.98 us  [the longest x5 2.17 us: halo(): high = lax.ppermute(lax.slice_in_dim(block, 0, 1, axis=dim), 'space', down)]
    ppermute x10 -> x20, waiting for transfers between devices: 1.57 us -> 22.1 us  [the longest x3 7.63 us: body(): lax.ppermute(held, 'rep', [(i, i ^ stride) for i in range(replicas)])]
  transfers between devices with their start and end apart: 11 -> 20, of which waited for: 2 -> 17; matrix products, arithmetic and copies ran while one was open for 1% -> 2% of each run, Pallas kernels for 0% -> 0%
where the time goes in v1:
time: 168 us
  Pallas kernels  114 us (68%)
  waiting for transfers between devices  22.1 us (13%)
  starting transfers between devices  14.4 us (9%)
  local copies, waits for them, and re-layouts  8.22 us (5%)
  other arithmetic  5.55 us (3%)
  between operations  3.52 us (2%)
    pallas_call x2, Pallas kernels, body(): pl.pallas_call(functools.partial(force_kernel, dims), out_shape=(vec_shap...  73.3 us
    pallas_call x1, Pallas kernels, body(): pl.pallas_call(functools.partial(density_kernel, dims, True), out_shape=(...  21.9 us
    pallas_call x1, Pallas kernels, body(): pl.pallas_call(functools.partial(density_kernel, dims, False), out_shape=...  18.6 us
    ppermute x3, waiting for transfers between devices, body(): lax.ppermute(held, 'rep', [(i, i ^ stride) for i in range(replicas)])  7.63 us
    ppermute x5, waiting for transfers between devices, halo(): lax.ppermute(lax.slice_in_dim(block, planes - 1, planes, axis=dim), 'spac...  6.87 us
    ppermute x3, starting transfers between devices, body(): lax.ppermute(held, 'rep', [(i, i ^ stride) for i in range(replicas)])  5.85 us
    unnamed x47, local copies, waits for them, and re-layouts  5.24 us
    ppermute x5, starting transfers between devices, halo(): high = lax.ppermute(lax.slice_in_dim(block, 0, 1, axis=dim), 'space', down)  4.77 us
  transfers between devices with their start and end apart: 20, of which 17 were waited for; matrix products, arithmetic and copies ran while one was open for 2% of the time, Pallas kernels for 0%

profile of v1, /device:TPU:0, one launch (start us, length us, event | category | flops | bytes accessed | tf_op | source)
XLA Modules:
  0.0 167.6 jit_solution(4728704758265305283)
XLA Ops:
  0.6 0.7 fusion.12
  1.4 2.4 %collective-permute-start.3 = (s32[1,4,4]{2,1,0:T(4,128)S(1)}, s32[1,4,4]{2,1,0:T(4,128)S(1)}, u32[]{:S(2)}, u32[]{:S(2)}) collective-permute-start(s32[1,4,4]{2,1,0:T(4,128)S(1)} %get-tuple-element.38), channel_id=1, source_target_pairs={{0,3},{1,0},{2,1},{3,2},{4,7},{5,4},{6,5},{7,6},{8,11},{9,8},{10,9... | collective-permute-start | bytes 200 | tf_op jit(solution)/shard_map/ppermute | solution.py:290
  3.8 0.7 slice.58
  4.6 0.7 collective-permute-start.4
  5.3 1.2 collective-permute-start.1
  6.5 0.7 copy.11.refs_6_
  8.0 1.7 %collective-permute-done.refs_0_ = f32[3,1,4,4,128]{4,3,2,1,0:T(4,128)S(1)} collective-permute-done((f32[3,1,4,4,128]{4,3,2,1,0:T(4,128)S(1)}, f32[3,1,4,4,128]{4,3,2,1,0:T(4,128)S(1)}, u32[]{:S(2)}, u32[]{:S(2)}) %collective-permute-start) | collective-permute-done | bytes 24608 | tf_op jit(solution)/shard_map/ppermute | solution.py:289
  10.4 21.9 %density_first.1 = (f32[2,4,4,128]{3,2,1,0:T(4,128)}, s32[864]{0:T(1024)}) custom-call(f32[3,1,4,4,128]{4,3,2,1,0:T(4,128)} %copy-done.15, f32[3,2,4,4,128]{4,3,2,1,0:T(4,128)} %bitcast.27, f32[3,1,4,4,128]{4,3,2,1,0:T(4,128)} %copy-done.14, s32[1,4,4]{2,1,0:T(4,128)} %copy-done.21, s32[2,4,4]{2,1,0:T(4,128)} %refs_4_.7, s32[1,4,4]{2,1,0:T(4,128)} %copy-done.20, ...), custom_call_target="tpu_custom_call" | custom-call | flops 141557760 | bytes 1048576 | tf_op jit(solution)/shard_map/density_first/pallas_call | solution.py:310
  32.3 0.7 fusion.11
  33.6 0.7 compare_convert_fusion.refs_11_
  34.3 0.7 collective-permute-done.6.refs_8_
  35.0 1.7 %collective-permute-done.5.refs_6_ = f32[1,4,4,128]{3,2,1,0:T(4,128)S(1)} collective-permute-done((f32[1,4,4,128]{3,2,1,0:T(4,128)S(1)}, f32[1,4,4,128]{3,2,1,0:T(4,128)S(1)}, u32[]{:S(2)}, u32[]{:S(2)}) %collective-permute-start.5) | collective-permute-done | bytes 8224 | tf_op jit(solution)/shard_map/ppermute | solution.py:289
  37.3 36.7 %force.2 = (f32[3,2,4,4,128]{4,3,2,1,0:T(4,128)}, f32[3,2,4,4,128]{4,3,2,1,0:T(4,128)}, f32[8,128]{1,0:T(8,128)}) custom-call(f32[3,1,4,4,128]{4,3,2,1,0:T(4,128)} %copy-done.15, f32[3,2,4,4,128]{4,3,2,1,0:T(4,128)} %bitcast.28, f32[3,1,4,4,128]{4,3,2,1,0:T(4,128)} %copy-done.14, s32[1,4,4]{2,1,0:T(4,128)} %copy-done.21, s32[2,4,4]{2,1,0:T(4,128)} %refs_4_.7, ...), custom_call_target="tpu_custom_call" | custom-call | flops 353894400 | bytes 1048576 | tf_op jit(solution)/shard_map/force/pallas_call | solution.py:332
  73.9 1.1 collective-permute-start.8
  75.5 2.3 %collective-permute-done.8 = f32[8,128]{1,0:T(8,128)S(1)} collective-permute-done((f32[8,128]{1,0:T(8,128)}, f32[8,128]{1,0:T(8,128)S(1)}, u32[]{:S(2)}, u32[]{:S(2)}) %collective-permute-start.8) | collective-permute-done | bytes 4128 | tf_op jit(solution)/shard_map/ppermute | solution.py:351
  78.3 0.7 add_add_fusion.1
  80.9 1.5 multiply_add_fusion.1
  83.5 1.0 collective-permute-done.11.refs_2_
  84.5 1.7 %collective-permute-done.10.refs_0_ = f32[3,1,4,4,128]{4,3,2,1,0:T(4,128)S(1)} collective-permute-done((f32[3,1,4,4,128]{4,3,2,1,0:T(4,128)S(1)}, f32[3,1,4,4,128]{4,3,2,1,0:T(4,128)S(1)}, u32[]{:S(2)}, u32[]{:S(2)}) %collective-permute-start.10) | collective-permute-done | bytes 24608 | tf_op jit(solution)/shard_map/ppermute | solution.py:289
  86.9 18.6 %density_next.1.refs_7_ = f32[2,4,4,128]{3,2,1,0:T(4,128)} custom-call(f32[3,1,4,4,128]{4,3,2,1,0:T(4,128)} %copy-done.13, f32[3,2,4,4,128]{4,3,2,1,0:T(4,128)} %copy-done.3, f32[3,1,4,4,128]{4,3,2,1,0:T(4,128)} %copy-done.12, s32[1,4,4]{2,1,0:T(4,128)} %copy-done.21, s32[2,4,4]{2,1,0:T(4,128)} %refs_4_.7, s32[1,4,4]{2,1,0:T(4,128)} %copy-done.20, ...), custom_call_target="tpu_custom_call" | custom-call | flops 141557760 | bytes 1048576 | tf_op jit(solution)/shard_map/density_next/pallas_call | solution.py:321
  105.5 0.7 fusion.10
  108.2 1.7 %collective-permute-done.12.refs_6_ = f32[1,4,4,128]{3,2,1,0:T(4,128)S(1)} collective-permute-done((f32[1,4,4,128]{3,2,1,0:T(4,128)S(1)}, f32[1,4,4,128]{3,2,1,0:T(4,128)S(1)}, u32[]{:S(2)}, u32[]{:S(2)}) %collective-permute-start.12) | collective-permute-done | bytes 8224 | tf_op jit(solution)/shard_map/ppermute | solution.py:289
  110.5 36.6 %force.3 = (f32[3,2,4,4,128]{4,3,2,1,0:T(4,128)}, f32[3,2,4,4,128]{4,3,2,1,0:T(4,128)}, f32[8,128]{1,0:T(8,128)}) custom-call(f32[3,1,4,4,128]{4,3,2,1,0:T(4,128)} %copy-done.13, f32[3,2,4,4,128]{4,3,2,1,0:T(4,128)} %copy-done.3, f32[3,1,4,4,128]{4,3,2,1,0:T(4,128)} %copy-done.12, s32[1,4,4]{2,1,0:T(4,128)} %copy-done.21, s32[2,4,4]{2,1,0:T(4,128)} %refs_4_.7, ...), custom_call_target="tpu_custom_call" | custom-call | flops 353894400 | bytes 1048576 | tf_op jit(solution)/shard_map/force/pallas_call | solution.py:332
  147.2 1.1 collective-permute-start.15
  148.4 1.5 collective-permute-start.17
  150.0 1.1 collective-permute-done.15
  151.5 2.7 %collective-permute-done.17 = f32[6,2,4,4,128]{4,3,2,1,0:T(4,128)S(1)} collective-permute-done((f32[6,2,4,4,128]{4,3,2,1,0:T(4,128)S(1)}, f32[6,2,4,4,128]{4,3,2,1,0:T(4,128)S(1)}, u32[]{:S(2)}, u32[]{:S(2)}) %collective-permute-start.17) | collective-permute-done | bytes 98336 | tf_op jit(solution)/shard_map/ppermute | solution.py:364
  154.2 1.6 collective-permute-start.18
  157.8 1.3 collective-permute-done.18
  159.1 2.7 %collective-permute-start.19 = (f32[6,2,4,4,128]{4,3,2,1,0:T(4,128)S(1)}, f32[6,2,4,4,128]{4,3,2,1,0:T(4,128)S(1)}, u32[]{:S(2)}, u32[]{:S(2)}) collective-permute-start(f32[6,2,4,4,128]{4,3,2,1,0:T(4,128)S(1)} %bitcast.33), channel_id=1, source_target_pairs={{0,16},{4,20},{8,24},{12,28},{16,0},{20,4},{24,8},{28,12},{1,17},{... | collective-permute-start | bytes 294920 | tf_op jit(solution)/shard_map/ppermute | solution.py:364
  162.4 3.7 %collective-permute-done.19 = f32[6,2,4,4,128]{4,3,2,1,0:T(4,128)S(1)} collective-permute-done((f32[6,2,4,4,128]{4,3,2,1,0:T(4,128)S(1)}, f32[6,2,4,4,128]{4,3,2,1,0:T(4,128)S(1)}, u32[]{:S(2)}, u32[]{:S(2)}) %collective-permute-start.19) | collective-permute-done | bytes 98336 | tf_op jit(solution)/shard_map/ppermute | solution.py:364
  166.1 0.8 copy-done.5
  (81 shorter events, 11.1 us)
Async XLA Ops:
  0.6 4.7 %copy-start = (f32[1,3,2,4,4,128]{5,4,3,2,1,0:T(4,128)S(1)}, f32[1,3,2,4,4,128]{5,4,3,2,1,0:T(4,128)}, u32[]{:S(2)}) copy-start(f32[1,3,2,4,4,128]{5,4,3,2,1,0:T(4,128)} %param.6) | copy-start | bytes 147460
  1.4 5.9 %collective-permute-start.3 = (s32[1,4,4]{2,1,0:T(4,128)S(1)}, s32[1,4,4]{2,1,0:T(4,128)S(1)}, u32[]{:S(2)}, u32[]{:S(2)}) collective-permute-start(s32[1,4,4]{2,1,0:T(4,128)S(1)} %get-tuple-element.38), channel_id=1, source_target_pairs={{0,3},{1,0},{2,1},{3,2},{4,7},{5,4},{6,5},{7,6},{8,11},{9,8},{10,9... | collective-permute-start | bytes 200 | tf_op jit(solution)/shard_map/ppermute | solution.py:290
  3.8 3.5 %collective-permute-start.2 = (s32[1,4,4]{2,1,0:T(4,128)S(1)}, s32[1,4,4]{2,1,0:T(4,128)S(1)}, u32[]{:S(2)}, u32[]{:S(2)}) collective-permute-start(s32[1,4,4]{2,1,0:T(4,128)S(1)} %get-tuple-element.39), channel_id=1, source_target_pairs={{0,1},{1,2},{2,3},{3,0},{4,5},{5,6},{6,7},{7,4},{8,9},{9,10},{10,1... | collective-permute-start | bytes 200 | tf_op jit(solution)/shard_map/ppermute | solution.py:289
  4.6 3.3 %collective-permute-start.4 = (s32[13,1,4,4]{3,2,1,0:T(4,128)S(1)}, s32[13,1,4,4]{3,2,1,0:T(4,128)S(1)}, u32[]{:S(2)}, u32[]{:S(2)}) collective-permute-start(s32[13,1,4,4]{3,2,1,0:T(4,128)S(1)} %copy.10), channel_id=1, source_target_pairs={{0,1},{1,2},{2,3},{3,0},{4,5},{5,6},{6,7},{7,4},{8,9},{9,10},{10,1... | collective-permute-start | bytes 2504 | tf_op jit(solution)/shard_map/ppermute | solution.py:294
  5.3 2.7 %collective-permute-start.1 = (f32[3,1,4,4,128]{4,3,2,1,0:T(4,128)S(1)}, f32[3,1,4,4,128]{4,3,2,1,0:T(4,128)S(1)}, u32[]{:S(2)}, u32[]{:S(2)}) collective-permute-start(f32[3,1,4,4,128]{4,3,2,1,0:T(4,128)S(1)} %get-tuple-element.32), channel_id=1, source_target_pairs={{0,3},{1,0},{2,1},{3,2},{4,7},{5,4},{6,5},{7,6},{8,11},{9,8},{10,9... | collective-permute-start | bytes 73736 | tf_op jit(solution)/shard_map/ppermute | solution.py:290
  6.5 3.3 %collective-permute-start = (f32[3,1,4,4,128]{4,3,2,1,0:T(4,128)S(1)}, f32[3,1,4,4,128]{4,3,2,1,0:T(4,128)S(1)}, u32[]{:S(2)}, u32[]{:S(2)}) collective-permute-start(f32[3,1,4,4,128]{4,3,2,1,0:T(4,128)S(1)} %get-tuple-element.33), channel_id=1, source_target_pairs={{0,1},{1,2},{2,3},{3,0},{4,5},{5,6},{6,7},{7,4},{8,9},{9,10},{10,1... | collective-permute-start | bytes 73736 | tf_op jit(solution)/shard_map/ppermute | solution.py:289
  7.3 2.5 %copy-start.20 = (s32[1,4,4]{2,1,0:T(4,128)}, s32[1,4,4]{2,1,0:T(4,128)S(1)}, u32[]{:S(2)}) copy-start(s32[1,4,4]{2,1,0:T(4,128)S(1)} %collective-permute-done.3.refs_5_) | copy-start | bytes 196
  7.3 2.5 %copy-start.21 = (s32[1,4,4]{2,1,0:T(4,128)}, s32[1,4,4]{2,1,0:T(4,128)S(1)}, u32[]{:S(2)}) copy-start(s32[1,4,4]{2,1,0:T(4,128)S(1)} %collective-permute-done.2.refs_3_) | copy-start | bytes 196
  7.9 1.8 %copy-start.11 = (s32[13,1,4,4]{3,2,1,0:T(4,128)}, s32[13,1,4,4]{3,2,1,0:T(4,128)S(1)}, u32[]{:S(2)}) copy-start(s32[13,1,4,4]{3,2,1,0:T(4,128)S(1)} %collective-permute-done.4.refs_7_) | copy-start | bytes 2500
  8.0 1.7 %copy-start.14 = (f32[3,1,4,4,128]{4,3,2,1,0:T(4,128)}, f32[3,1,4,4,128]{4,3,2,1,0:T(4,128)S(1)}, u32[]{:S(2)}) copy-start(f32[3,1,4,4,128]{4,3,2,1,0:T(4,128)S(1)} %collective-permute-done.1.refs_2_) | copy-start | bytes 73732
  33.0 2.0 %collective-permute-start.6 = (f32[1,4,4,128]{3,2,1,0:T(4,128)S(1)}, f32[1,4,4,128]{3,2,1,0:T(4,128)S(1)}, u32[]{:S(2)}, u32[]{:S(2)}) collective-permute-start(f32[1,4,4,128]{3,2,1,0:T(4,128)S(1)} %get-tuple-element.36), channel_id=1, source_target_pairs={{0,3},{1,0},{2,1},{3,2},{4,7},{5,4},{6,5},{7,6},{8,11},{9,8},{10,9... | collective-permute-start | bytes 24584 | tf_op jit(solution)/shard_map/ppermute | solution.py:290
  33.6 3.1 %collective-permute-start.5 = (f32[1,4,4,128]{3,2,1,0:T(4,128)S(1)}, f32[1,4,4,128]{3,2,1,0:T(4,128)S(1)}, u32[]{:S(2)}, u32[]{:S(2)}) collective-permute-start(f32[1,4,4,128]{3,2,1,0:T(4,128)S(1)} %get-tuple-element.37), channel_id=1, source_target_pairs={{0,1},{1,2},{2,3},{3,0},{4,5},{5,6},{6,7},{7,4},{8,9},{9,10},{10,1... | collective-permute-start | bytes 24584 | tf_op jit(solution)/shard_map/ppermute | solution.py:289
  37.3 43.6 %copy-start.1 = (f32[1,3,2,4,4,128]{5,4,3,2,1,0:T(4,128)S(1)}, f32[1,3,2,4,4,128]{5,4,3,2,1,0:T(4,128)}, u32[]{:S(2)}) copy-start(f32[1,3,2,4,4,128]{5,4,3,2,1,0:T(4,128)} %param.6) | copy-start | bytes 147460
  73.9 1.5 collective-permute-start.9
  73.9 3.9 %collective-permute-start.8 = (f32[8,128]{1,0:T(8,128)}, f32[8,128]{1,0:T(8,128)S(1)}, u32[]{:S(2)}, u32[]{:S(2)}) collective-permute-start(f32[8,128]{1,0:T(8,128)} %get-tuple-element.15), channel_id=1, source_target_pairs={{0,2},{1,3},{2,0},{3,1},{4,6},{5,7},{6,4},{7,5},{8,10},{9,11},{10,... | collective-permute-start | bytes 12296 | tf_op jit(solution)/shard_map/ppermute | solution.py:351
  75.0 3.2 %collective-permute-start.7 = (f32[8,128]{1,0:T(8,128)}, f32[8,128]{1,0:T(8,128)S(1)}, u32[]{:S(2)}, u32[]{:S(2)}) collective-permute-start(f32[8,128]{1,0:T(8,128)} %get-tuple-element.15), channel_id=1, source_target_pairs={{0,1},{1,2},{2,3},{3,0},{4,5},{5,6},{6,7},{7,4},{8,9},{9,10},{10,1... | collective-permute-start | bytes 12296 | tf_op jit(solution)/shard_map/ppermute | solution.py:351
  83.0 1.5 collective-permute-start.11
  83.0 3.3 %collective-permute-start.10 = (f32[3,1,4,4,128]{4,3,2,1,0:T(4,128)S(1)}, f32[3,1,4,4,128]{4,3,2,1,0:T(4,128)S(1)}, u32[]{:S(2)}, u32[]{:S(2)}) collective-permute-start(f32[3,1,4,4,128]{4,3,2,1,0:T(4,128)S(1)} %get-tuple-element.31), channel_id=1, source_target_pairs={{0,1},{1,2},{2,3},{3,0},{4,5},{5,6},{6,7},{7,4},{8,9},{9,10},{10,1... | collective-permute-start | bytes 73736 | tf_op jit(solution)/shard_map/ppermute | solution.py:289
  84.5 1.7 %copy-start.12 = (f32[3,1,4,4,128]{4,3,2,1,0:T(4,128)}, f32[3,1,4,4,128]{4,3,2,1,0:T(4,128)S(1)}, u32[]{:S(2)}) copy-start(f32[3,1,4,4,128]{4,3,2,1,0:T(4,128)S(1)} %collective-permute-done.11.refs_2_) | copy-start | bytes 73732
  106.2 2.0 %collective-permute-start.13 = (f32[1,4,4,128]{3,2,1,0:T(4,128)S(1)}, f32[1,4,4,128]{3,2,1,0:T(4,128)S(1)}, u32[]{:S(2)}, u32[]{:S(2)}) collective-permute-start(f32[1,4,4,128]{3,2,1,0:T(4,128)S(1)} %get-tuple-element.34), channel_id=1, source_target_pairs={{0,3},{1,0},{2,1},{3,2},{4,7},{5,4},{6,5},{7,6},{8,11},{9,8},{10,9... | collective-permute-start | bytes 24584 | tf_op jit(solution)/shard_map/ppermute | solution.py:290
  106.8 3.1 %collective-permute-start.12 = (f32[1,4,4,128]{3,2,1,0:T(4,128)S(1)}, f32[1,4,4,128]{3,2,1,0:T(4,128)S(1)}, u32[]{:S(2)}, u32[]{:S(2)}) collective-permute-start(f32[1,4,4,128]{3,2,1,0:T(4,128)S(1)} %get-tuple-element.35), channel_id=1, source_target_pairs={{0,1},{1,2},{2,3},{3,0},{4,5},{5,6},{6,7},{7,4},{8,9},{9,10},{10,1... | collective-permute-start | bytes 24584 | tf_op jit(solution)/shard_map/ppermute | solution.py:289
  110.5 37.9 %copy-start.2 = (f32[3,2,4,4,128]{4,3,2,1,0:T(4,128)S(1)}, f32[3,2,4,4,128]{4,3,2,1,0:T(4,128)}, u32[]{:S(2)}) copy-start(f32[3,2,4,4,128]{4,3,2,1,0:T(4,128)} %get-tuple-element.14) | copy-start | bytes 147460
  147.1 4.4 %copy-start.10 = (f32[8,128]{1,0:T(8,128)S(1)}, f32[8,128]{1,0:T(8,128)}, u32[]{:S(2)}) copy-start(f32[8,128]{1,0:T(8,128)} %get-tuple-element.18) | copy-start | bytes 12292
  147.1 2.9 %collective-permute-start.16 = (f32[8,128]{1,0:T(8,128)}, f32[8,128]{1,0:T(8,128)S(1)}, u32[]{:S(2)}, u32[]{:S(2)}) collective-permute-start(f32[8,128]{1,0:T(8,128)} %get-tuple-element.18), channel_id=1, source_target_pairs={{0,3},{1,0},{2,1},{3,2},{4,7},{5,4},{6,5},{7,6},{8,11},{9,8},{10,9... | collective-permute-start | bytes 12296 | tf_op jit(solution)/shard_map/ppermute | solution.py:351
  147.2 3.9 %collective-permute-start.15 = (f32[8,128]{1,0:T(8,128)}, f32[8,128]{1,0:T(8,128)S(1)}, u32[]{:S(2)}, u32[]{:S(2)}) collective-permute-start(f32[8,128]{1,0:T(8,128)} %get-tuple-element.18), channel_id=1, source_target_pairs={{0,2},{1,3},{2,0},{3,1},{4,6},{5,7},{6,4},{7,5},{8,10},{9,11},{10,... | collective-permute-start | bytes 12296 | tf_op jit(solution)/shard_map/ppermute | solution.py:351
  148.2 3.2 %collective-permute-start.14 = (f32[8,128]{1,0:T(8,128)}, f32[8,128]{1,0:T(8,128)S(1)}, u32[]{:S(2)}, u32[]{:S(2)}) collective-permute-start(f32[8,128]{1,0:T(8,128)} %get-tuple-element.18), channel_id=1, source_target_pairs={{0,1},{1,2},{2,3},{3,0},{4,5},{5,6},{6,7},{7,4},{8,9},{9,10},{10,1... | collective-permute-start | bytes 12296 | tf_op jit(solution)/shard_map/ppermute | solution.py:351
  148.4 5.7 %collective-permute-start.17 = (f32[6,2,4,4,128]{4,3,2,1,0:T(4,128)S(1)}, f32[6,2,4,4,128]{4,3,2,1,0:T(4,128)S(1)}, u32[]{:S(2)}, u32[]{:S(2)}) collective-permute-start(f32[6,2,4,4,128]{4,3,2,1,0:T(4,128)S(1)} %pad_maximum_fusion), channel_id=1, source_target_pairs={{0,4},{4,0},{8,12},{12,8},{16,20},{20,16},{24,28},{28,24},{1,5},{5... | collective-permute-start | bytes 294920 | tf_op jit(solution)/shard_map/ppermute | solution.py:364
  154.2 4.9 %collective-permute-start.18 = (f32[6,2,4,4,128]{4,3,2,1,0:T(4,128)S(1)}, f32[6,2,4,4,128]{4,3,2,1,0:T(4,128)S(1)}, u32[]{:S(2)}, u32[]{:S(2)}) collective-permute-start(f32[6,2,4,4,128]{4,3,2,1,0:T(4,128)S(1)} %broadcast_select_fusion), channel_id=1, source_target_pairs={{0,8},{4,12},{8,0},{12,4},{16,24},{20,28},{24,16},{28,20},{1,9},{5... | collective-permute-start | bytes 294920 | tf_op jit(solution)/shard_map/ppermute | solution.py:364
  159.1 2.7 %copy-start.4 = (f32[3,2,4,4,128]{4,3,2,1,0:T(4,128)S(1)}, f32[3,2,4,4,128]{4,3,2,1,0:T(4,128)}, u32[]{:S(2)}) copy-start(f32[3,2,4,4,128]{4,3,2,1,0:T(4,128)} %copy-done.3) | copy-start | bytes 147460
  159.1 2.7 %copy-start.6 = (f32[3,2,4,4,128]{4,3,2,1,0:T(4,128)S(1)}, f32[3,2,4,4,128]{4,3,2,1,0:T(4,128)}, u32[]{:S(2)}) copy-start(f32[3,2,4,4,128]{4,3,2,1,0:T(4,128)} %get-tuple-element.19) | copy-start | bytes 147460
  159.1 2.7 %copy-start.7 = (f32[3,2,4,4,128]{4,3,2,1,0:T(4,128)S(1)}, f32[3,2,4,4,128]{4,3,2,1,0:T(4,128)}, u32[]{:S(2)}) copy-start(f32[3,2,4,4,128]{4,3,2,1,0:T(4,128)} %get-tuple-element.17) | copy-start | bytes 147460
  159.1 7.0 %collective-permute-start.19 = (f32[6,2,4,4,128]{4,3,2,1,0:T(4,128)S(1)}, f32[6,2,4,4,128]{4,3,2,1,0:T(4,128)S(1)}, u32[]{:S(2)}, u32[]{:S(2)}) collective-permute-start(f32[6,2,4,4,128]{4,3,2,1,0:T(4,128)S(1)} %bitcast.33), channel_id=1, source_target_pairs={{0,16},{4,20},{8,24},{12,28},{16,0},{20,4},{24,8},{28,12},{1,17},{... | collective-permute-start | bytes 294920 | tf_op jit(solution)/shard_map/ppermute | solution.py:364
  (11 other events, 10.4 us)

commit v2 on v1

--- a/solution.py
+++ b/solution.py
@@ -7,6 +7,7 @@
 from jax.experimental import pallas as pl
 from jax.experimental.pallas import tpu as pltpu
 from jax.sharding import PartitionSpec as P
+
 
 QUENCH = 2
 STEP_SIZE = 0.1
@@ -52,7 +53,7 @@
     return jnp.where(index >= size, index - size, index)
 
 
-def build_list(dims, cnt_dummy, flags, flags_lo, list_ref):
+def build_list(dims, flags, flags_lo, list_ref):
     planes, gy, gz = dims
     ey, ez = gy + 2, gz + 2
     dummy = (planes + 2) * ey * ez
@@ -82,7 +83,7 @@
     lax.fori_loop(0, gy, row, 0)
 
 
-def build_partners(dims, pos, cnt, emb, lhs_ref, yb_ref, sel_ref):
+def build_partners(dims, pos, cnt, emb, lhs_ref, yb_ref):
     planes, gy, gz = dims
     ey, ez = gy + 2, gz + 2
     slots = lhs_ref.shape[1]
@@ -122,6 +123,8 @@
 
         lax.fori_loop(0, ey, line, 0)
         if yb_ref is not None:
+            col = lax.broadcasted_iota(jnp.int32, (24, 3 * slots), 0) % 8
+            pick = (col == lax.broadcasted_iota(jnp.int32, (24, 3 * slots), 1) // slots).astype(F32).astype(BF)
 
             def broad(y, _):
                 for z in range(gz):
@@ -136,7 +139,7 @@
                         axis=0,
                     )
                     tall = out.T.astype(BF)
-                    wide = jnp.dot(tall, sel_ref[...], preferred_element_type=F32)
+                    wide = jnp.dot(tall, pick, preferred_element_type=F32)
                     cell = (j * gy + y) * gz + z
                     for k in range(3):
                         yb_ref[cell, k] = wide[:, k * slots : (k + 1) * slots]
@@ -188,15 +191,45 @@
     return jnp.concatenate([right, jnp.concatenate(ws, axis=0).astype(BF)], axis=1)
 
 
+def mix_factor(sum_refs):
+    total = sum_refs[0][...]
+    for ref in sum_refs[1:]:
+        total = total + ref[...]
+    force_sq = jnp.sum(total[0:1], axis=1, keepdims=True)
+    vel_sq = jnp.sum(total[1:2], axis=1, keepdims=True)
+    return jnp.sqrt(vel_sq / (force_sq + EPSILON))
+
+
+def quench_update(dims, mix, x_ref, f_of, v_of, planes, x_out, v_out):
+    gy, _ = dims[1:]
+    for k in range(3):
+        for p in range(planes):
+            for y in range(gy):
+                v = (1.0 - ALPHA_MIX) * v_of(k, p, y) + ALPHA_MIX * mix * f_of(k, p, y)
+                if v_out is not None:
+                    v_out[k, p, y] = v
+                x_out[k, p, y] = x_ref[k, p, y] + STEP_SIZE * v
+
+
 def density_kernel(dims, first, *refs):
+    planes, gy, gz = dims
     if first:
-        (p0, p1, p2, c0, c1, c2, fl, fl_lo, emb_ref, list_ref, lhs_ref) = refs
-        build_list(dims, None, fl, fl_lo, list_ref)
+        (p0, p1, p2, c0, c1, c2, fl, fl_lo, emb_ref, lo_ref, hi_ref, list_ref, lhs_ref) = refs
+        build_list(dims, fl, fl_lo, list_ref)
     else:
-        (p0, p1, p2, c0, c1, c2, list_ref, emb_ref, lhs_ref) = refs
-    planes, gy, gz = dims
+        (q0, q1, q2, c0, c1, c2, list_ref, f_ref, v_ref, b0, b2) = refs[:11]
+        sum_refs = refs[11:-8]
+        (emb_ref, lo_ref, hi_ref, p0, p1, p2, v_out, lhs_ref) = refs[-8:]
+        mix = mix_factor(sum_refs)
+        quench_update(
+            dims, mix, q1, lambda k, p, y: f_ref[k, p, y], lambda k, p, y: v_ref[k, p, y], planes, p1, v_out
+        )
+        for q, b, out in ((q0, b0, p0), (q2, b2, p2)):
+            quench_update(
+                dims, mix, q, lambda k, p, y, b=b: b[k, p, y], lambda k, p, y, b=b: b[k + 3, p, y], 1, out, None
+            )
     slots = lhs_ref.shape[1]
-    build_partners(dims, (p0, p1, p2), (c0, c1, c2), None, lhs_ref, None, None)
+    build_partners(dims, (p0, p1, p2), (c0, c1, c2), None, lhs_ref, None)
     lane = lax.broadcasted_iota(jnp.int32, (1, slots), 1)
     for p in range(planes):
 
@@ -214,17 +247,25 @@
                     acc[r % 4] = acc[r % 4] + t * t * t
             total = jnp.sum((acc[0] + acc[1]) + (acc[2] + acc[3]), axis=0, keepdims=True)
             total = total - jnp.where(lane < count, 1.0, 0.0)
-            emb_ref[p, y, pl.ds(z, 1), :] = -lax.rsqrt(1.0 + total / slots)
+            emb = -lax.rsqrt(1.0 + total / slots)
+            emb_ref[p, y, pl.ds(z, 1), :] = emb
+            if p == 0:
+                lo_ref[0, y, pl.ds(z, 1), :] = emb
+            if p == planes - 1:
+                hi_ref[0, y, pl.ds(z, 1), :] = emb
             return 0
 
         lax.fori_loop(0, gy * gz, cell_step, 0)
 
 
 def force_kernel(dims, *refs):
-    (p0, p1, p2, c0, c1, c2, e0, e1, e2, vel, list_ref, sel_ref, f_ref, v_ref, s_ref, lhs_ref, yb_ref) = refs
+    (p0, p1, p2, c0, c1, c2, e0, e1, e2, vel, list_ref) = refs[:11]
+    (f_ref, v_ref, s_ref) = refs[11:14]
+    edges = refs[14:-2]
+    (lhs_ref, yb_ref) = refs[-2:]
     planes, gy, gz = dims
     slots = lhs_ref.shape[1]
-    build_partners(dims, (p0, p1, p2), (c0, c1, c2), (e0, e1, e2), lhs_ref, yb_ref, sel_ref)
+    build_partners(dims, (p0, p1, p2), (c0, c1, c2), (e0, e1, e2), lhs_ref, yb_ref)
     lane = lax.broadcasted_iota(jnp.int32, (1, slots), 1)
     sums = (jnp.zeros((1, slots), F32), jnp.zeros((1, slots), F32))
     for p in range(planes):
@@ -263,12 +304,58 @@
                 f_ref[k, p, y, pl.ds(z, 1), :] = f
                 v = jnp.where(lane < count, vel[k, p, y, pl.ds(z, 1), :], 0.0) + STEP_SIZE * f
                 v_ref[k, p, y, pl.ds(z, 1), :] = v
+                if edges and p == 0:
+                    edges[0][k, 0, y, pl.ds(z, 1), :] = f
+                    edges[0][k + 3, 0, y, pl.ds(z, 1), :] = v
+                if edges and p == planes - 1:
+                    edges[1][k, 0, y, pl.ds(z, 1), :] = f
+                    edges[1][k + 3, 0, y, pl.ds(z, 1), :] = v
                 ff = ff + f * f
                 vv = vv + v * v
             return ff, vv
 
         sums = lax.fori_loop(0, gy * gz, cell_step, sums)
     s_ref[...] = jnp.concatenate([sums[0], sums[1], jnp.zeros((6, slots), F32)], axis=0)
+
+
+def finish_kernel(dims, radix, *refs):
+    (x_ref, f_ref, v_ref, noise, cnt, pick) = refs[:6]
+    options = refs[6 : 6 + radix]
+    sum_refs = refs[6 + radix : -4]
+    (xq, vq, xd, vd) = refs[-4:]
+    planes, gy, gz = dims
+    slots = x_ref.shape[-1]
+    mix = mix_factor(sum_refs)
+    quench_update(
+        dims, mix, x_ref, lambda k, p, y: f_ref[k, p, y], lambda k, p, y: v_ref[k, p, y], planes, xq, vq
+    )
+    lane = lax.broadcasted_iota(jnp.int32, (gz, slots), 1)
+    line = lax.broadcasted_iota(jnp.int32, (gz, slots), 0)
+    take = pick[0]
+    for p in range(planes):
+        for y in range(gy):
+            limit = jnp.zeros((gz, slots), jnp.int32)
+            for z in range(gz):
+                limit = jnp.where(line == z, cnt[p, y, z], limit)
+            occupied = (lane < limit).astype(F32)
+            for k in range(3):
+                place, push = options[0][k, p, y], options[0][k + 3, p, y]
+                for index in range(1, radix):
+                    place = jnp.where(take == index, options[index][k, p, y], place)
+                    push = jnp.where(take == index, options[index][k + 3, p, y], push)
+                v = FRICTION * push + KICK_SCALE * occupied * noise[k, p, y]
+                vd[k, p, y] = v
+                xd[k, p, y] = place + STEP_SIZE * v
+
+
+def exit_hops(count):
+    hops, stride = [], 1
+    while stride < count:
+        left = count // stride
+        radix = next(r for r in (4, 2, 3, 5, 7, left) if left % r == 0)
+        hops.append((stride, radix))
+        stride *= radix
+    return hops
 
 
 def body(positions, velocities, thermal_noise, counts, pair_flags, exit_replica):
@@ -277,105 +364,112 @@
     planes, gy, gz, slots = start_pos.shape[1:]
     dims = (planes, gy, gz)
     up, down = ring("space", 1), ring("space", -1)
+    space = lax.axis_size("space")
     vmem = pl.BlockSpec(memory_space=pltpu.VMEM)
     smem = pl.BlockSpec(memory_space=pltpu.SMEM)
-    params = pltpu.CompilerParams(vmem_limit_bytes=56 * 2**20)
     ext = (planes + 2) * (gy + 2) * (gz + 2) + 1
     entries = planes * gy * gz * 27
-    cells = planes * gy * gz
-    pairs = cells * 27 * slots * slots
-
-    def halo(block, dim):
-        low = lax.ppermute(lax.slice_in_dim(block, planes - 1, planes, axis=dim), "space", up)
-        high = lax.ppermute(lax.slice_in_dim(block, 0, 1, axis=dim), "space", down)
-        return low, high
-
-    count_lo, count_hi = halo(counts, 0)
+    pairs = planes * gy * gz * 27 * slots * slots
+
+    def shaped(*shape):
+        return jax.ShapeDtypeStruct(shape, F32)
+
+    def planes_of(block, dim):
+        return lax.slice_in_dim(block, 0, 1, axis=dim), lax.slice_in_dim(block, planes - 1, planes, axis=dim)
+
+    def halo(first, last):
+        return lax.ppermute(last, "space", up), lax.ppermute(first, "space", down)
+
     flags_lo = lax.ppermute(lax.slice_in_dim(pair_flags, planes - 1, planes, axis=1), "space", up)
-    column = jnp.arange(24)[:, None]
-    pick = ((column % 8) == (jnp.arange(3 * slots)[None, :] // slots)).astype(BF)
+    count_lo, count_hi = halo(*planes_of(counts, 0))
+    pos_lo, pos_hi = halo(*planes_of(start_pos, 1))
     lhs_scratch = pltpu.VMEM((ext, slots, KDIM), BF)
-    emb_shape = jax.ShapeDtypeStruct((planes, gy, gz, slots), F32)
-    vec_shape = jax.ShapeDtypeStruct((3, planes, gy, gz, slots), F32)
-
-    coords, motion = start_pos, start_vel
-    blocks = None
-    pushed = None
+    emb_shape = [shaped(planes, gy, gz, slots), shaped(1, gy, gz, slots), shaped(1, gy, gz, slots)]
+    vec, edge = shaped(3, planes, gy, gz, slots), shaped(3, 1, gy, gz, slots)
+    pack = shaped(6, 1, gy, gz, slots)
+    number = [smem] * 3
+    cost_d = pl.CostEstimate(flops=pairs * 10, bytes_accessed=2**20, transcendentals=0)
+    cost_f = pl.CostEstimate(flops=pairs * 25, bytes_accessed=2**20, transcendentals=0)
+
+    held, hops = None, exit_hops(lax.axis_size("rep"))
+    me, chosen = lax.axis_index("rep"), exit_replica[0]
+
+    def hop(index, held):
+        stride, radix = hops[index]
+        digit, root = (me // stride) % radix, (chosen // stride) % radix
+        options = [held]
+        for turn in range(1, radix):
+            pairs = []
+            for i in range(lax.axis_size("rep")):
+                at = (i // stride) % radix
+                pairs.append((i, i + (((at + turn) % radix) - at) * stride))
+            options.append(lax.ppermute(held, "rep", pairs))
+        return options, (digit - root) % radix
+
+    motion = start_vel
+    coords = (pos_lo, start_pos, pos_hi)
     for quench_step in range(QUENCH):
-        low, high = halo(coords, 1)
-        args = [low, coords, high, count_lo, counts, count_hi]
-        specs = [vmem] * 3 + [smem] * 3
-        cost = pl.CostEstimate(flops=pairs * 10, bytes_accessed=2**20, transcendentals=0)
+        args = [*coords, count_lo, counts, count_hi]
+        specs = [vmem] * 3 + number
         if quench_step == 0:
-            embed, blocks = pl.pallas_call(
+            emb, emb_first, emb_last, blocks = pl.pallas_call(
                 functools.partial(density_kernel, dims, True),
-                out_shape=(emb_shape, jax.ShapeDtypeStruct((entries,), jnp.int32)),
+                out_shape=(*emb_shape, jax.ShapeDtypeStruct((entries,), jnp.int32)),
                 in_specs=specs + [smem, smem],
-                out_specs=(vmem, smem),
+                out_specs=(vmem, vmem, vmem, smem),
                 scratch_shapes=[lhs_scratch],
-                compiler_params=params,
-                cost_estimate=cost,
+                compiler_params=pltpu.CompilerParams(vmem_limit_bytes=12 * 2**20),
+                cost_estimate=cost_d,
                 name="density_first",
             )(*args, pair_flags, flags_lo)
         else:
-            embed = pl.pallas_call(
+            emb, emb_first, emb_last, *coords, motion = pl.pallas_call(
                 functools.partial(density_kernel, dims, False),
-                out_shape=emb_shape,
-                in_specs=specs + [smem],
-                out_specs=vmem,
+                out_shape=(*emb_shape, edge, vec, edge, vec),
+                in_specs=specs + [smem] + [vmem] * (4 + space),
+                out_specs=(vmem,) * 7,
                 scratch_shapes=[lhs_scratch],
-                compiler_params=params,
-                cost_estimate=cost,
+                compiler_params=pltpu.CompilerParams(vmem_limit_bytes=12 * 2**20),
+                cost_estimate=cost_d,
                 name="density_next",
-            )(*args, blocks)
-        embed_lo, embed_hi = halo(embed, 0)
-        forces, pushed_vel, sums = pl.pallas_call(
+            )(*args, blocks, forces, pushed, *packs, *sums)
+            args = [*coords, count_lo, counts, count_hi]
+        emb_lo, emb_hi = halo(emb_first, emb_last)
+        last = quench_step == QUENCH - 1
+        forces, pushed, part, *edges = pl.pallas_call(
             functools.partial(force_kernel, dims),
-            out_shape=(vec_shape, vec_shape, jax.ShapeDtypeStruct((8, slots), F32)),
-            in_specs=specs + [vmem] * 4 + [smem, vmem],
-            out_specs=(vmem, vmem, vmem),
+            out_shape=(vec, vec, shaped(8, slots), *(() if last else (pack, pack))),
+            in_specs=specs + [vmem] * 4 + [smem],
+            out_specs=(vmem,) * (3 if last else 5),
             scratch_shapes=[
                 lhs_scratch,
                 pltpu.VMEM(((planes + 2) * gy * gz, 3, slots, slots), F32),
             ],
-            compiler_params=params,
-            cost_estimate=pl.CostEstimate(
-                flops=pairs * 25, bytes_accessed=2**20, transcendentals=0
-            ),
+            compiler_params=pltpu.CompilerParams(vmem_limit_bytes=26 * 2**20),
+            cost_estimate=cost_f,
             name="force",
-        )(*args, embed_lo, embed, embed_hi, motion, blocks, pick)
+        )(*args, emb_lo, emb, emb_hi, motion, blocks)
+        sums = [part] + [lax.ppermute(part, "space", ring("space", s)) for s in range(1, space)]
+        if not last:
+            packs = halo(*edges)
         if quench_step == 0:
-            pushed = pushed_vel
-        total = sums
-        for shift in range(1, lax.axis_size("space")):
-            total = total + lax.ppermute(sums, "space", ring("space", shift))
-        force_sq, vel_sq = jnp.sum(total[0]), jnp.sum(total[1])
-        mixing = jnp.sqrt(vel_sq / (force_sq + EPSILON))
-        motion = (1.0 - ALPHA_MIX) * pushed_vel + ALPHA_MIX * mixing * forces
-        coords = coords + STEP_SIZE * motion
-
-    chosen = exit_replica[0]
-    held = jnp.concatenate([start_pos, pushed], axis=0)
-    replicas = lax.axis_size("rep")
-    me = lax.axis_index("rep")
-    if replicas & (replicas - 1) == 0:
-        stride = 1
-        while stride < replicas:
-            other = lax.ppermute(held, "rep", [(i, i ^ stride) for i in range(replicas)])
-            mine = ((me ^ chosen) >> (stride.bit_length() - 1)) & 1 == 0
-            held = jnp.where(mine, held, other)
-            stride *= 2
-    else:
-        final = held
-        for shift in range(1, replicas):
-            other = lax.ppermute(held, "rep", ring("rep", shift))
-            final = jnp.where((me - shift) % replicas == chosen, other, final)
-        held = final
-    exit_pos, exit_push = held[:3], held[3:]
-    occupied = (jnp.arange(slots, dtype=jnp.int32) < counts[..., None]).astype(F32)
-    drift = FRICTION * exit_push + KICK_SCALE * occupied[None] * thermal_noise[0, 0]
-    place = exit_pos + STEP_SIZE * drift
-    return coords[None], motion[None], place[None], drift[None]
+            held = jnp.concatenate([start_pos, pushed], axis=0)
+            for index in range(len(hops) - 1):
+                options, pick = hop(index, held)
+                held = options[0]
+                for turn in range(1, len(options)):
+                    held = jnp.where(pick == turn, options[turn], held)
+            options, pick = hop(len(hops) - 1, held)
+
+    quench_pos, quench_vel, place, drift = pl.pallas_call(
+        functools.partial(finish_kernel, dims, len(options)),
+        out_shape=(vec,) * 4,
+        in_specs=[vmem] * 4 + [smem] * 2 + [vmem] * (len(options) + space),
+        out_specs=(vmem,) * 4,
+        compiler_params=pltpu.CompilerParams(vmem_limit_bytes=12 * 2**20),
+        name="finish",
+    )(coords[1], forces, pushed, thermal_noise[0, 0], counts, pick[None], *options, *sums)
+    return quench_pos[None], quench_vel[None], place[None], drift[None]
 
 
 def solution(mesh):
@@ -388,6 +482,4 @@
         P(None, "space", None, None),
         P(),
     )
-    return jax.shard_map(
-        body, mesh=mesh, in_specs=placed, out_specs=(vector,) * 4, check_vma=False
-    )
+    return jax.shard_map(body, mesh=mesh, in_specs=placed, out_specs=(vector,) * 4, check_vma=False)

time: 168 us -> 148 us (0.88)
  waiting for transfers between devices: 22.1 us -> 13.1 us
  local copies, waits for them, and re-layouts: 8.22 us -> 1.7 us
  starting transfers between devices: 14.4 us -> 20.4 us
  other arithmetic: 5.55 us -> 0.08 us
  Pallas kernels: 114 us -> 111 us
  between operations: 3.52 us -> 0.96 us
    ppermute x19 -> x20, waiting for transfers between devices: 21.5 us -> 13.1 us  [the longest x6 5.87 us: body(): lax.ppermute(part, 'space', ring('space', s))]
    ppermute x19 -> x20, starting transfers between devices: 13.7 us -> 19 us  [the longest x10 9.7 us: halo(): return (lax.ppermute(last, 'space', up), lax.ppermute(first, 'space', down))]
    unnamed x47 -> x13, local copies, waits for them, and re-layouts: 5.24 us -> 0.82 us
    add x3 -> x0, other arithmetic: 2.17 us -> none  [the longest x1 1.48 us: body(): coords = coords + STEP_SIZE * motion]
    pallas_call x2 -> x3, Pallas kernels: 73.3 us -> 72 us  [the longest x2 70.6 us: body(): pl.pallas_call(functools.partial(force_kernel, dims), out_shape=(vec, vec...]
  transfers between devices with their start and end apart: 20 -> 21, of which waited for: 17 -> 12; matrix products, arithmetic and copies ran while one was open for 2% -> 0% of each run, Pallas kernels for 0% -> 36%
where the time goes in v2:
time: 148 us
  Pallas kernels  111 us (75%)
  starting transfers between devices  20.4 us (14%)
  waiting for transfers between devices  13.1 us (9%)
  local copies, waits for them, and re-layouts  1.7 us (1%)
    pallas_call x2, Pallas kernels, body(): pl.pallas_call(functools.partial(force_kernel, dims), out_shape=(vec, vec...  70.6 us
    pallas_call x1, Pallas kernels, body(): pl.pallas_call(functools.partial(density_kernel, dims, True), out_shape=(...  21.5 us
    pallas_call x1, Pallas kernels, body(): pl.pallas_call(functools.partial(density_kernel, dims, False), out_shape=...  17.9 us
    ppermute x10, starting transfers between devices, halo(): return (lax.ppermute(last, 'space', up), lax.ppermute(first, 'space', down))  9.7 us
    ppermute x4, starting transfers between devices, hop(): options.append(lax.ppermute(held, 'rep', pairs))  6.24 us
    ppermute x6, waiting for transfers between devices, body(): lax.ppermute(part, 'space', ring('space', s))  5.87 us
    ppermute x10, waiting for transfers between devices, halo(): return (lax.ppermute(last, 'space', up), lax.ppermute(first, 'space', down))  3.9 us
    ppermute x4, waiting for transfers between devices, hop(): options.append(lax.ppermute(held, 'rep', pairs))  3.32 us
  transfers between devices with their start and end apart: 21, of which 12 were waited for; matrix products, arithmetic and copies ran while one was open for 0% of the time, Pallas kernels for 36%

profile of v2, /device:TPU:0, one launch (start us, length us, event | category | flops | bytes accessed | tf_op | source)
XLA Modules:
  0.0 147.6 jit_solution(1028656566555156534)
XLA Ops:
  0.6 0.8 fusion
  1.9 2.0 %collective-permute-start.1 = (f32[3,1,4,4,128]{4,3,2,1,0:T(4,128)S(1)}, f32[3,1,4,4,128]{4,3,2,1,0:T(4,128)S(1)}, u32[]{:S(2)}, u32[]{:S(2)}) collective-permute-start(f32[3,1,4,4,128]{4,3,2,1,0:T(4,128)S(1)} %get-tuple-element.50), channel_id=1, source_target_pairs={{0,3},{1,0},{2,1},{3,2},{4,7},{5,4},{6,5},{7,6},{8,11},{9,8},{10,9... | collective-permute-start | bytes 73736 | tf_op jit(solution)/shard_map/ppermute | solution.py:381
  4.0 1.4 collective-permute-start.4
  5.4 1.1 collective-permute-start.2
  6.4 0.7 collective-permute-start.3
  7.3 1.1 collective-permute-done.2.refs_3_
  8.5 21.5 %density_first.1 = (f32[2,4,4,128]{3,2,1,0:T(4,128)S(1)}, f32[1,4,4,128]{3,2,1,0:T(4,128)S(1)}, f32[1,4,4,128]{3,2,1,0:T(4,128)S(1)}, s32[864]{0:T(1024)S(1)}) custom-call(f32[3,1,4,4,128]{4,3,2,1,0:T(4,128)S(1)} %collective-permute-done.refs_0_, f32[3,2,4,4,128]{4,3,2,1,0:T(4,128)S(1)} %bitcast.11, f32[3,1,4,4,128]{4,3,2,1,0:T(4,128)S(1)} %collective-permute-done.1.refs_2_, ...), custom_call_target="tpu_custom_call" | custom-call | flops 141557760 | bytes 1048576 | tf_op jit(solution)/shard_map/density_first/pallas_call | solution.py:415
  29.9 1.6 %collective-permute-start.5 = (f32[1,4,4,128]{3,2,1,0:T(4,128)S(1)}, f32[1,4,4,128]{3,2,1,0:T(4,128)S(1)}, u32[]{:S(2)}, u32[]{:S(2)}) collective-permute-start(f32[1,4,4,128]{3,2,1,0:T(4,128)S(1)} %get-tuple-element.28), channel_id=1, source_target_pairs={{0,1},{1,2},{2,3},{3,0},{4,5},{5,6},{6,7},{7,4},{8,9},{9,10},{10,1... | collective-permute-start | bytes 24584 | tf_op jit(solution)/shard_map/ppermute | solution.py:381
  31.8 1.3 collective-permute-done.5.refs_6_
  33.1 35.4 %force.2 = (f32[3,2,4,4,128]{4,3,2,1,0:T(4,128)S(1)}, f32[3,2,4,4,128]{4,3,2,1,0:T(4,128)S(1)}, f32[8,128]{1,0:T(8,128)S(1)}, f32[6,1,4,4,128]{4,3,2,1,0:T(4,128)S(1)}, f32[6,1,4,4,128]{4,3,2,1,0:T(4,128)S(1)}) custom-call(f32[3,1,4,4,128]{4,3,2,1,0:T(4,128)S(1)} %collective-permute-done.refs_0_, f32[3,2,4,4,128]{4,3,2,1,0:T(4,128)S(1)} %bitcast.12, ...), custom_call_target="tpu_custom_call" | custom-call | flops 353894400 | bytes 1048576 | tf_op jit(solution)/shard_map/force/pallas_call | solution.py:439
  68.5 2.5 %collective-permute-start.14 = (f32[6,2,4,4,128]{4,3,2,1,0:T(4,128)S(1)}, f32[6,2,4,4,128]{4,3,2,1,0:T(4,128)S(1)}, u32[]{:S(2)}, u32[]{:S(2)}) collective-permute-start(f32[6,2,4,4,128]{4,3,2,1,0:T(4,128)S(1)} %pad_maximum_fusion), channel_id=1, source_target_pairs={{0,12},{4,0},{8,4},{12,8},{16,28},{20,16},{24,20},{28,24},{1,13},{... | collective-permute-start | bytes 294920 | tf_op jit(solution)/shard_map/ppermute | solution.py:406
  71.0 0.5 collective-permute-start.15
  71.5 0.6 collective-permute-start.16
  72.1 0.7 copy-done.5
  73.0 0.7 collective-permute-start.7
  73.7 1.0 collective-permute-start.8
  74.8 2.0 %collective-permute-done.15 = f32[6,2,4,4,128]{4,3,2,1,0:T(4,128)S(1)} collective-permute-done((f32[6,2,4,4,128]{4,3,2,1,0:T(4,128)S(1)}, f32[6,2,4,4,128]{4,3,2,1,0:T(4,128)S(1)}, u32[]{:S(2)}, u32[]{:S(2)}) %collective-permute-start.15) | collective-permute-done | bytes 98336 | tf_op jit(solution)/shard_map/ppermute | solution.py:406
  76.8 1.3 collective-permute-done.16
  78.1 2.6 %collective-permute-start.17 = (f32[6,2,4,4,128]{4,3,2,1,0:T(4,128)S(1)}, f32[6,2,4,4,128]{4,3,2,1,0:T(4,128)S(1)}, u32[]{:S(2)}, u32[]{:S(2)}) collective-permute-start(f32[6,2,4,4,128]{4,3,2,1,0:T(4,128)S(1)} %select_select_fusion.refs_6_), channel_id=1, source_target_pairs={{0,16},{4,20},{8,24},{12,28},{16,0},{20,4},{24,8},{28,12},{1,17},{... | collective-permute-start | bytes 294920 | tf_op jit(solution)/shard_map/ppermute | solution.py:406
  80.8 0.6 collective-permute-start.10
  81.3 2.5 %collective-permute-done.9.refs_12_ = f32[8,128]{1,0:T(8,128)S(1)} collective-permute-done((f32[8,128]{1,0:T(8,128)S(1)}, f32[8,128]{1,0:T(8,128)S(1)}, u32[]{:S(2)}, u32[]{:S(2)}) %collective-permute-start.9) | collective-permute-done | bytes 4128 | tf_op jit(solution)/shard_map/ppermute | solution.py:452
  83.8 0.6 collective-permute-done.10.refs_13_
  84.4 0.8 collective-permute-done.11.refs_14_
  85.1 17.9 %density_next.1 = (f32[2,4,4,128]{3,2,1,0:T(4,128)S(1)}, f32[1,4,4,128]{3,2,1,0:T(4,128)S(1)}, f32[1,4,4,128]{3,2,1,0:T(4,128)S(1)}, f32[3,1,4,4,128]{4,3,2,1,0:...) custom-call(f32[3,1,4,4,128]{4,3,2,1,0:T(4,128)S(1)} %collective-per, ...), custom_call_target="tpu_custom_call" | custom-call | flops 141557760 | bytes 1048576 | tf_op jit(solution)/shard_map/density_next/pallas_call | solution.py:426
  103.1 1.0 collective-permute-start.12
  104.0 0.8 collective-permute-start.13
  104.9 1.3 collective-permute-done.12.refs_6_
  106.3 35.2 %force.3 = (f32[3,2,4,4,128]{4,3,2,1,0:T(4,128)S(1)}, f32[3,2,4,4,128]{4,3,2,1,0:T(4,128)S(1)}, f32[8,128]{1,0:T(8,128)S(1)}) custom-call(f32[3,1,4,4,128]{4,3,2,1,0:T(4,128)S(1)} %get-tuple-element.37.refs_0_, f32[3,2,4,4,128]{4,3,2,1,0:T(4,128)S(1)} %get-tuple-element.36.refs_1_.refs_0_, f32[3,1,4,4,128]{4,3,2,1,0:T(4,128)S(1)} %get-tuple-element.38.refs_2_, ...), custom_call_target="tpu_custom_call" | custom-call | flops 353894400 | bytes 1048576 | tf_op jit(solution)/shard_map/force/pallas_call | solution.py:439
  141.5 1.1 collective-permute-start.18
  142.5 1.1 collective-permute-start.19
  144.6 1.6 %collective-permute-done.19.refs_10_ = f32[8,128]{1,0:T(8,128)S(1)} collective-permute-done((f32[8,128]{1,0:T(8,128)S(1)}, f32[8,128]{1,0:T(8,128)S(1)}, u32[]{:S(2)}, u32[]{:S(2)}) %collective-permute-start.19) | collective-permute-done | bytes 4128 | tf_op jit(solution)/shard_map/ppermute | solution.py:452
  146.2 1.4 finish.1
  (35 shorter events, 2.1 us)
Async XLA Ops:
  1.4 7.0 %collective-permute-start = (f32[3,1,4,4,128]{4,3,2,1,0:T(4,128)S(1)}, f32[3,1,4,4,128]{4,3,2,1,0:T(4,128)S(1)}, u32[]{:S(2)}, u32[]{:S(2)}) collective-permute-start(f32[3,1,4,4,128]{4,3,2,1,0:T(4,128)S(1)} %get-tuple-element.51), channel_id=1, source_target_pairs={{0,1},{1,2},{2,3},{3,0},{4,5},{5,6},{6,7},{7,4},{8,9},{9,10},{10,1... | collective-permute-start | bytes 73736 | tf_op jit(solution)/shard_map/ppermute | solution.py:381
  1.9 2.0 %slice-start = ((s32[13,2,4,4]{0,3,2,1:T(4,128)}), s32[13,1,4,4]{0,3,2,1:T(4,128)S(1)}, s32[]{:S(2)}) async-start(s32[13,2,4,4]{0,3,2,1:T(4,128)} %param.10), calls=%async_computation | async-start | bytes 16384 | tf_op jit(solution)/shard_map/slice | solution.py:383
  1.9 6.6 %collective-permute-start.1 = (f32[3,1,4,4,128]{4,3,2,1,0:T(4,128)S(1)}, f32[3,1,4,4,128]{4,3,2,1,0:T(4,128)S(1)}, u32[]{:S(2)}, u32[]{:S(2)}) collective-permute-start(f32[3,1,4,4,128]{4,3,2,1,0:T(4,128)S(1)} %get-tuple-element.50), channel_id=1, source_target_pairs={{0,3},{1,0},{2,1},{3,2},{4,7},{5,4},{6,5},{7,6},{8,11},{9,8},{10,9... | collective-permute-start | bytes 73736 | tf_op jit(solution)/shard_map/ppermute | solution.py:381
  3.9 1.5 %copy-start.2 = (s32[2,4,4]{2,1,0:T(4,128)S(1)}, s32[2,4,4]{2,1,0:T(4,128)}, u32[]{:S(2)}) copy-start(s32[2,4,4]{2,1,0:T(4,128)} %refs_4_.9) | copy-start | bytes 388
  3.9 3.2 %copy-start.4 = (s32[13,2,4,4]{0,3,2,1:T(4,128)S(1)}, s32[13,2,4,4]{0,3,2,1:T(4,128)}, u32[]{:S(2)}) copy-start(s32[13,2,4,4]{0,3,2,1:T(4,128)} %param.10) | copy-start | bytes 4996
  4.0 4.4 %copy-start = (f32[1,3,2,4,4,128]{5,4,3,2,1,0:T(4,128)S(1)}, f32[1,3,2,4,4,128]{5,4,3,2,1,0:T(4,128)}, u32[]{:S(2)}) copy-start(f32[1,3,2,4,4,128]{5,4,3,2,1,0:T(4,128)} %param.6) | copy-start | bytes 147460
  4.0 4.4 %collective-permute-start.4 = (s32[13,1,4,4]{3,2,1,0:T(4,128)S(1)}, s32[13,1,4,4]{3,2,1,0:T(4,128)S(1)}, u32[]{:S(2)}, u32[]{:S(2)}) collective-permute-start(s32[13,1,4,4]{3,2,1,0:T(4,128)S(1)} %copy.10), channel_id=1, source_target_pairs={{0,1},{1,2},{2,3},{3,0},{4,5},{5,6},{6,7},{7,4},{8,9},{9,10},{10,1... | collective-permute-start | bytes 2504 | tf_op jit(solution)/shard_map/ppermute | solution.py:383
  5.4 3.0 %collective-permute-start.2 = (s32[1,4,4]{2,1,0:T(4,128)S(1)}, s32[1,4,4]{2,1,0:T(4,128)S(1)}, u32[]{:S(2)}, u32[]{:S(2)}) collective-permute-start(s32[1,4,4]{2,1,0:T(4,128)S(1)} %get-tuple-element.53), channel_id=1, source_target_pairs={{0,1},{1,2},{2,3},{3,0},{4,5},{5,6},{6,7},{7,4},{8,9},{9,10},{10,1... | collective-permute-start | bytes 200 | tf_op jit(solution)/shard_map/ppermute | solution.py:381
  6.4 2.0 %collective-permute-start.3 = (s32[1,4,4]{2,1,0:T(4,128)S(1)}, s32[1,4,4]{2,1,0:T(4,128)S(1)}, u32[]{:S(2)}, u32[]{:S(2)}) collective-permute-start(s32[1,4,4]{2,1,0:T(4,128)S(1)} %get-tuple-element.52), channel_id=1, source_target_pairs={{0,3},{1,0},{2,1},{3,2},{4,7},{5,4},{6,5},{7,6},{8,11},{9,8},{10,9... | collective-permute-start | bytes 200 | tf_op jit(solution)/shard_map/ppermute | solution.py:381
  7.3 25.9 %copy-start.3 = (f32[1,3,2,4,4,128]{5,4,3,2,1,0:T(4,128)S(1)}, f32[1,3,2,4,4,128]{5,4,3,2,1,0:T(4,128)}, u32[]{:S(2)}) copy-start(f32[1,3,2,4,4,128]{5,4,3,2,1,0:T(4,128)} %param.7) | copy-start | bytes 147460
  29.9 3.1 %collective-permute-start.5 = (f32[1,4,4,128]{3,2,1,0:T(4,128)S(1)}, f32[1,4,4,128]{3,2,1,0:T(4,128)S(1)}, u32[]{:S(2)}, u32[]{:S(2)}) collective-permute-start(f32[1,4,4,128]{3,2,1,0:T(4,128)S(1)} %get-tuple-element.28), channel_id=1, source_target_pairs={{0,1},{1,2},{2,3},{3,0},{4,5},{5,6},{6,7},{7,4},{8,9},{9,10},{10,1... | collective-permute-start | bytes 24584 | tf_op jit(solution)/shard_map/ppermute | solution.py:381
  31.5 1.6 %collective-permute-start.6 = (f32[1,4,4,128]{3,2,1,0:T(4,128)S(1)}, f32[1,4,4,128]{3,2,1,0:T(4,128)S(1)}, u32[]{:S(2)}, u32[]{:S(2)}) collective-permute-start(f32[1,4,4,128]{3,2,1,0:T(4,128)S(1)} %get-tuple-element.30), channel_id=1, source_target_pairs={{0,3},{1,0},{2,1},{3,2},{4,7},{5,4},{6,5},{7,6},{8,11},{9,8},{10,9... | collective-permute-start | bytes 24584 | tf_op jit(solution)/shard_map/ppermute | solution.py:381
  68.5 6.2 %collective-permute-start.14 = (f32[6,2,4,4,128]{4,3,2,1,0:T(4,128)S(1)}, f32[6,2,4,4,128]{4,3,2,1,0:T(4,128)S(1)}, u32[]{:S(2)}, u32[]{:S(2)}) collective-permute-start(f32[6,2,4,4,128]{4,3,2,1,0:T(4,128)S(1)} %pad_maximum_fusion), channel_id=1, source_target_pairs={{0,12},{4,0},{8,4},{12,8},{16,28},{20,16},{24,20},{28,24},{1,13},{... | collective-permute-start | bytes 294920 | tf_op jit(solution)/shard_map/ppermute | solution.py:406
  71.0 5.7 %collective-permute-start.15 = (f32[6,2,4,4,128]{4,3,2,1,0:T(4,128)S(1)}, f32[6,2,4,4,128]{4,3,2,1,0:T(4,128)S(1)}, u32[]{:S(2)}, u32[]{:S(2)}) collective-permute-start(f32[6,2,4,4,128]{4,3,2,1,0:T(4,128)S(1)} %pad_maximum_fusion), channel_id=1, source_target_pairs={{0,8},{4,12},{8,0},{12,4},{16,24},{20,28},{24,16},{28,20},{1,9},{5... | collective-permute-start | bytes 294920 | tf_op jit(solution)/shard_map/ppermute | solution.py:406
  71.5 6.5 %collective-permute-start.16 = (f32[6,2,4,4,128]{4,3,2,1,0:T(4,128)S(1)}, f32[6,2,4,4,128]{4,3,2,1,0:T(4,128)S(1)}, u32[]{:S(2)}, u32[]{:S(2)}) collective-permute-start(f32[6,2,4,4,128]{4,3,2,1,0:T(4,128)S(1)} %pad_maximum_fusion), channel_id=1, source_target_pairs={{0,4},{4,8},{8,12},{12,0},{16,20},{20,24},{24,28},{28,16},{1,5},{5... | collective-permute-start | bytes 294920 | tf_op jit(solution)/shard_map/ppermute | solution.py:406
  72.1 0.7 copy-start.5
  73.0 12.2 %collective-permute-start.7 = (f32[6,1,4,4,128]{4,3,2,1,0:T(4,128)S(1)}, f32[6,1,4,4,128]{4,3,2,1,0:T(4,128)S(1)}, u32[]{:S(2)}, u32[]{:S(2)}) collective-permute-start(f32[6,1,4,4,128]{4,3,2,1,0:T(4,128)S(1)} %get-tuple-element.33), channel_id=1, source_target_pairs={{0,1},{1,2},{2,3},{3,0},{4,5},{5,6},{6,7},{7,4},{8,9},{9,10},{10,1... | collective-permute-start | bytes 147464 | tf_op jit(solution)/shard_map/ppermute | solution.py:381
  73.7 11.4 %collective-permute-start.8 = (f32[6,1,4,4,128]{4,3,2,1,0:T(4,128)S(1)}, f32[6,1,4,4,128]{4,3,2,1,0:T(4,128)S(1)}, u32[]{:S(2)}, u32[]{:S(2)}) collective-permute-start(f32[6,1,4,4,128]{4,3,2,1,0:T(4,128)S(1)} %get-tuple-element.34), channel_id=1, source_target_pairs={{0,3},{1,0},{2,1},{3,2},{4,7},{5,4},{6,5},{7,6},{8,11},{9,8},{10,9... | collective-permute-start | bytes 147464 | tf_op jit(solution)/shard_map/ppermute | solution.py:381
  78.1 68.0 %collective-permute-start.17 = (f32[6,2,4,4,128]{4,3,2,1,0:T(4,128)S(1)}, f32[6,2,4,4,128]{4,3,2,1,0:T(4,128)S(1)}, u32[]{:S(2)}, u32[]{:S(2)}) collective-permute-start(f32[6,2,4,4,128]{4,3,2,1,0:T(4,128)S(1)} %select_select_fusion.refs_6_), channel_id=1, source_target_pairs={{0,16},{4,20},{8,24},{12,28},{16,0},{20,4},{24,8},{28,12},{1,17},{... | collective-permute-start | bytes 294920 | tf_op jit(solution)/shard_map/ppermute | solution.py:406
  80.8 3.0 %collective-permute-start.9 = (f32[8,128]{1,0:T(8,128)S(1)}, f32[8,128]{1,0:T(8,128)S(1)}, u32[]{:S(2)}, u32[]{:S(2)}) collective-permute-start(f32[8,128]{1,0:T(8,128)S(1)} %get-tuple-element.35.refs_11_), channel_id=1, source_target_pairs={{0,1},{1,2},{2,3},{3,0},{4,5},{5,6},{6,7},{7,4},{8,9},{9,10},{10,1... | collective-permute-start | bytes 12296 | tf_op jit(solution)/shard_map/ppermute | solution.py:452
  80.8 3.6 %collective-permute-start.10 = (f32[8,128]{1,0:T(8,128)S(1)}, f32[8,128]{1,0:T(8,128)S(1)}, u32[]{:S(2)}, u32[]{:S(2)}) collective-permute-start(f32[8,128]{1,0:T(8,128)S(1)} %get-tuple-element.35.refs_11_), channel_id=1, source_target_pairs={{0,2},{1,3},{2,0},{3,1},{4,6},{5,7},{6,4},{7,5},{8,10},{9,11},{10,... | collective-permute-start | bytes 12296 | tf_op jit(solution)/shard_map/ppermute | solution.py:452
  83.8 1.3 collective-permute-start.11
  103.1 3.1 %collective-permute-start.12 = (f32[1,4,4,128]{3,2,1,0:T(4,128)S(1)}, f32[1,4,4,128]{3,2,1,0:T(4,128)S(1)}, u32[]{:S(2)}, u32[]{:S(2)}) collective-permute-start(f32[1,4,4,128]{3,2,1,0:T(4,128)S(1)} %get-tuple-element.39), channel_id=1, source_target_pairs={{0,1},{1,2},{2,3},{3,0},{4,5},{5,6},{6,7},{7,4},{8,9},{9,10},{10,1... | collective-permute-start | bytes 24584 | tf_op jit(solution)/shard_map/ppermute | solution.py:381
  104.0 2.2 %collective-permute-start.13 = (f32[1,4,4,128]{3,2,1,0:T(4,128)S(1)}, f32[1,4,4,128]{3,2,1,0:T(4,128)S(1)}, u32[]{:S(2)}, u32[]{:S(2)}) collective-permute-start(f32[1,4,4,128]{3,2,1,0:T(4,128)S(1)} %get-tuple-element.41), channel_id=1, source_target_pairs={{0,3},{1,0},{2,1},{3,2},{4,7},{5,4},{6,5},{7,6},{8,11},{9,8},{10,9... | collective-permute-start | bytes 24584 | tf_op jit(solution)/shard_map/ppermute | solution.py:381
  141.5 3.1 %collective-permute-start.18 = (f32[8,128]{1,0:T(8,128)S(1)}, f32[8,128]{1,0:T(8,128)S(1)}, u32[]{:S(2)}, u32[]{:S(2)}) collective-permute-start(f32[8,128]{1,0:T(8,128)S(1)} %get-tuple-element.45.refs_8_), channel_id=1, source_target_pairs={{0,1},{1,2},{2,3},{3,0},{4,5},{5,6},{6,7},{7,4},{8,9},{9,10},{10,1... | collective-permute-start | bytes 12296 | tf_op jit(solution)/shard_map/ppermute | solution.py:452
  142.5 3.6 %collective-permute-start.19 = (f32[8,128]{1,0:T(8,128)S(1)}, f32[8,128]{1,0:T(8,128)S(1)}, u32[]{:S(2)}, u32[]{:S(2)}) collective-permute-start(f32[8,128]{1,0:T(8,128)S(1)} %get-tuple-element.45.refs_8_), channel_id=1, source_target_pairs={{0,2},{1,3},{2,0},{3,1},{4,6},{5,7},{6,4},{7,5},{8,10},{9,11},{10,... | collective-permute-start | bytes 12296 | tf_op jit(solution)/shard_map/ppermute | solution.py:452
  143.6 2.5 %collective-permute-start.20 = (f32[8,128]{1,0:T(8,128)S(1)}, f32[8,128]{1,0:T(8,128)S(1)}, u32[]{:S(2)}, u32[]{:S(2)}) collective-permute-start(f32[8,128]{1,0:T(8,128)S(1)} %get-tuple-element.45.refs_8_), channel_id=1, source_target_pairs={{0,3},{1,0},{2,1},{3,2},{4,7},{5,4},{6,5},{7,6},{8,11},{9,8},{10,9... | collective-permute-start | bytes 12296 | tf_op jit(solution)/shard_map/ppermute | solution.py:452
  144.0 2.2 %copy-start.1 = (f32[1,1,3,2,4,4,128]{6,5,4,3,2,1,0:T(4,128)S(1)}, f32[1,1,3,2,4,4,128]{6,5,4,3,2,1,0:T(4,128)}, u32[]{:S(2)}) copy-start(f32[1,1,3,2,4,4,128]{6,5,4,3,2,1,0:T(4,128)} %param.8) | copy-start | bytes 147460

commit v3 on v2

--- a/solution.py
+++ b/solution.py
@@ -3,6 +3,7 @@
 
 import jax
 import jax.numpy as jnp
+import numpy as np
 from jax import lax
 from jax.experimental import pallas as pl
 from jax.experimental.pallas import tpu as pltpu
@@ -25,6 +26,9 @@
 BF = jnp.bfloat16
 F32 = jnp.float32
 KDIM = 64
+TILE = 32
+ITEM = 12
+GROUP = 4
 
 
 def ring(axis, shift):
@@ -53,50 +57,110 @@
     return jnp.where(index >= size, index - size, index)
 
 
-def build_list(dims, flags, flags_lo, list_ref):
+def list_sizes(dims, slots):
+    cells = math.prod(dims)
+    most = cells * (-(-27 * (slots // TILE) // ITEM))
+    head = 8
+    return head, most + 2 * GROUP, head + (most + 2 * GROUP) * (ITEM + 1) + 2 * ITEM
+
+
+def build_list(dims, slots, cnt, flags, flags_lo, list_ref):
     planes, gy, gz = dims
     ey, ez = gy + 2, gz + 2
-    dummy = (planes + 2) * ey * ez
-
-    def row(y, _):
-        for p in range(planes):
+    per = slots // TILE
+    dummy = (planes + 2) * ey * ez * per
+    head, items, _ = list_sizes(dims, slots)
+    tiles = head + items
+    bound = -(-27 * per // ITEM)
+
+    def count_at(j, y, z):
+        which, at = (0, 0) if j == 0 else ((2, 0) if j == planes + 1 else (1, j - 1))
+        return cnt[which][at, y, z]
+
+    def cell_list(p, y, z, item):
+        at = item * ITEM
+        for ox, oy, oz in OFFSETS:
+            ext = ((p + 1 + ox) * ey + (y + 1 + oy)) * ez + (z + 1 + oz)
+            jy, jz = wrap(y + oy, gy), (z + oz) % gz
+            number = (count_at(p + 1 + ox, jy, jz) + (TILE - 1)) // TILE
+            found = flag_of((ox, oy, oz))
+            if found is not None:
+                index, forward = found
+                if forward:
+                    flag = flags[index, p, y, z]
+                elif p + ox < 0:
+                    flag = flags_lo[index, 0, jy, jz]
+                else:
+                    flag = flags[index, p + ox, jy, jz]
+                number = number * flag
+            for t in range(per):
+                list_ref[tiles + at + t] = ext * per + t
+            at = at + number
+        for t in range(ITEM):
+            list_ref[tiles + at + t] = dummy
+        for t in range(bound):
+            list_ref[head + item + t] = (p * gy + y) * gz + z
+        return (at + (ITEM - 1)) // ITEM
+
+    item = 0
+    for p in range(planes):
+
+        def row(y, item):
             for z in range(gz):
-                cell = (p * gy + y) * gz + z
-                for slot, (ox, oy, oz) in enumerate(OFFSETS):
-                    ext = ((p + 1 + ox) * ey + (y + 1 + oy)) * ez + (z + 1 + oz)
-                    found = flag_of((ox, oy, oz))
-                    if found is None:
-                        list_ref[cell * 27 + slot] = ext
-                        continue
-                    index, forward = found
-                    if forward:
-                        flag = flags[index, p, y, z]
-                    else:
-                        jy, jz = wrap(y + oy, gy), (z + oz) % gz
-                        if p + ox < 0:
-                            flag = flags_lo[index, 0, jy, jz]
-                        else:
-                            flag = flags[index, p + ox, jy, jz]
-                    list_ref[cell * 27 + slot] = jnp.where(flag > 0, ext, dummy)
+                item = cell_list(p, y, z, item)
+            return item
+
+        item = lax.fori_loop(0, gy, row, item)
+    list_ref[0] = (item + (GROUP - 1)) // GROUP * GROUP
+
+    def rest(i, _):
+        list_ref[head + item + i] = planes * gy * gz - 1
+        for t in range(ITEM):
+            list_ref[tiles + (item + i) * ITEM + t] = dummy
         return 0
 
-    lax.fori_loop(0, gy, row, 0)
-
-
-def build_partners(dims, pos, cnt, emb, lhs_ref, yb_ref):
+    lax.fori_loop(0, 2 * GROUP - 1, rest, 0)
+
+
+def build_partners(dims, pos, cnt, emb, lhs_ref, wide_refs, *accs):
     planes, gy, gz = dims
     ey, ez = gy + 2, gz + 2
     slots = lhs_ref.shape[1]
-    rows = lax.broadcasted_iota(jnp.int32, (8, slots), 0)
-    lane = lax.broadcasted_iota(jnp.int32, (8, slots), 1)
+    full = (8, slots)
+    rows = lax.broadcasted_iota(jnp.int32, full, 0)
+    lane = lax.broadcasted_iota(jnp.int32, full, 1)
+    blank = jnp.zeros((slots - KDIM, slots), F32)
+
+    def store(ext, value):
+        h, m, l = split3(value)
+        tall = jnp.concatenate([h, h, h, m, m, m, l, l, blank], axis=0).T.astype(BF)
+        lhs_ref[ext] = tall
+        return tall
+
+    if wide_refs is not None:
+        row = lax.broadcasted_iota(jnp.int32, (2 * slots, 2 * slots), 0)
+        col = lax.broadcasted_iota(jnp.int32, (2 * slots, 2 * slots), 1) // slots
+        used = (row < 8) | ((row >= 24) & (row < 32)) | ((row >= 48) & (row < 56))
+        side = jnp.zeros((slots, slots), BF)
+        wide_x, wide_y, wide_z = wide_refs
+        acc_xy, acc_z = accs[:gz], accs[gz:]
+        for m, base in enumerate((0, 2)):
+            pick = jnp.where(used & (row % 8 == col + base) & (col + base < 3), 1.0, 0.0)
+            pltpu.matmul_push_rhs(pick.astype(BF), staging_register=0, mxu_index=m)
+        for m in range(2):
+            for index, acc in enumerate((acc_xy, acc_z)[m]):
+                pltpu.matmul_acc_lhs(
+                    acc,
+                    jnp.zeros((slots, 2 * slots), BF),
+                    load_staged_rhs=0 if index == 0 else None,
+                )
 
     def one(j, which, at, y, z, by, bz):
-        full = (8, slots)
         raw = [
             jnp.broadcast_to(pos[which][k, at, by, pl.ds(bz, 1), :], full) for k in range(3)
         ]
         xx = raw[0] + (j - 0.5 - (planes + 1) / 2)
-        yy = raw[1] + ((y - 0.5 - (gy + 1) / 2) if isinstance(y, int) else (y.astype(F32) - 0.5 - (gy + 1) / 2))
+        yy = raw[1] + (jnp.asarray(y).astype(F32) - 0.5 - (gy + 1) / 2)
         zz = raw[2] + (z - 0.5 - (gz + 1) / 2)
         norm = xx * xx + yy * yy + zz * zz
         norm = jnp.where(lane < cnt[which][at, by, bz], norm, norm + FAR)
@@ -106,50 +170,54 @@
         if emb is not None:
             e = jnp.broadcast_to(emb[which][at, by, pl.ds(bz, 1), :], full) * 0.25
             value = jnp.where(rows == 6, e, value)
-        h, m, l = split3(value)
-        return jnp.concatenate([h, h, h, m, m, m, l, l], axis=0)
-
+        return store((j * ey + y) * ez + z, value)
+
+    def put(spot):
+        at_x, at_y, at_z = spot
+        for z in range(gz):
+            both = pltpu.matmul_pop(acc_xy[z])
+            wide_x[at_x + z] = both[:, :slots]
+            wide_y[at_y + z] = both[:, slots:]
+        for z in range(ez):
+            wide_z[at_z + z] = pltpu.matmul_pop(acc_z[z])[:, :slots]
+
+    spot = (jnp.int32(0),) * 3
     for j in range(planes + 2):
         which, at = (0, 0) if j == 0 else ((2, 0) if j == planes + 1 else (1, j - 1))
 
-        def line(y, _):
+        def line(y, spot):
             by = wrap(y - 1, gy)
+            talls = [one(j, which, at, y, z, by, (z - 1) % gz) for z in range(ez)]
+            if wide_refs is None:
+                return spot
+            put(spot)
             for z in range(ez):
-                bz = (z - 1) % gz
-                tall = one(j, which, at, y, z, by, bz)
-                ext = (j * ey + y) * ez + z
-                lhs_ref[ext] = tall.T.astype(BF)
-            return 0
-
-        lax.fori_loop(0, ey, line, 0)
-        if yb_ref is not None:
-            col = lax.broadcasted_iota(jnp.int32, (24, 3 * slots), 0) % 8
-            pick = (col == lax.broadcasted_iota(jnp.int32, (24, 3 * slots), 1) // slots).astype(F32).astype(BF)
-
-            def broad(y, _):
-                for z in range(gz):
-                    out = jnp.concatenate(
-                        split3(
-                            jnp.concatenate(
-                                [pos[which][k, at, y, pl.ds(z, 1), :] for k in range(3)]
-                                + [jnp.zeros((5, slots), F32)],
-                                axis=0,
-                            )
-                        ),
-                        axis=0,
-                    )
-                    tall = out.T.astype(BF)
-                    wide = jnp.dot(tall, pick, preferred_element_type=F32)
-                    cell = (j * gy + y) * gz + z
-                    for k in range(3):
-                        yb_ref[cell, k] = wide[:, k * slots : (k + 1) * slots]
-                return 0
-
-            lax.fori_loop(0, gy, broad, 0)
-    dummy = (planes + 2) * ey * ez
-    value = jnp.where(rows == 3, FAR, jnp.where(rows >= 4, 1.0, 0.0))
-    h, m, l = split3(value)
-    lhs_ref[dummy] = jnp.concatenate([h, h, h, m, m, m, l, l], axis=0).T.astype(BF)
+                left = jnp.concatenate([talls[z], side], axis=1)
+                if 1 <= z <= gz:
+                    pltpu.matmul_acc_lhs(acc_xy[z - 1], left)
+                pltpu.matmul_acc_lhs(acc_z[z], left)
+            return ((j * gy + by) * gz, (j * ey + y) * gz, (j * gy + by) * ez)
+
+        spot = lax.fori_loop(0, ey, line, spot)
+    if wide_refs is not None:
+        put(spot)
+    store((planes + 2) * ey * ez, jnp.where(rows == 3, FAR, jnp.where(rows >= 4, 1.0, 0.0)))
+
+
+def wide_table(dims, slots):
+    planes, gy, gz = dims
+    ey, ez = gy + 2, gz + 2
+    per = slots // TILE
+    table = np.zeros(((planes + 2) * ey * ez + 1) * per, np.int32)
+    for j in range(planes + 2):
+        for y in range(ey):
+            for z in range(ez):
+                by, bz = (y - 1) % gy, (z - 1) % gz
+                where = ((j * gy + by) * gz + bz, (j * ey + y) * gz + bz, (j * gy + by) * ez + z)
+                for t in range(per):
+                    x0, y0, z0 = (w * per + t for w in where)
+                    table[((j * ey + y) * ez + z) * per + t] = x0 | (y0 << 10) | (z0 << 20)
+    return table
 
 
 def build_center(dims, p, y, z, x3, count, e_row):
@@ -214,12 +282,12 @@
 def density_kernel(dims, first, *refs):
     planes, gy, gz = dims
     if first:
-        (p0, p1, p2, c0, c1, c2, fl, fl_lo, emb_ref, lo_ref, hi_ref, list_ref, lhs_ref) = refs
-        build_list(dims, fl, fl_lo, list_ref)
+        (p0, p1, p2, c0, c1, c2, fl, fl_lo, emb_ref, lo_ref, hi_ref, list_ref, lhs_ref, right_ref, res_ref) = refs
+        build_list(dims, lhs_ref.shape[1], (c0, c1, c2), fl, fl_lo, list_ref)
     else:
         (q0, q1, q2, c0, c1, c2, list_ref, f_ref, v_ref, b0, b2) = refs[:11]
-        sum_refs = refs[11:-8]
-        (emb_ref, lo_ref, hi_ref, p0, p1, p2, v_out, lhs_ref) = refs[-8:]
+        sum_refs = refs[11:-10]
+        (emb_ref, lo_ref, hi_ref, p0, p1, p2, v_out, lhs_ref, right_ref, res_ref) = refs[-10:]
         mix = mix_factor(sum_refs)
         quench_update(
             dims, mix, q1, lambda k, p, y: f_ref[k, p, y], lambda k, p, y: v_ref[k, p, y], planes, p1, v_out
@@ -230,91 +298,206 @@
             )
     slots = lhs_ref.shape[1]
     build_partners(dims, (p0, p1, p2), (c0, c1, c2), None, lhs_ref, None)
+    build_rights(dims, p1, c1, None, right_ref)
+    gap = jnp.zeros((slots - KDIM, slots), BF)
+    side = jnp.zeros((slots, slots), BF)
+
+    def right_of(cell):
+        one = jnp.concatenate([right_ref[cell], gap], axis=0)
+        return jnp.concatenate(
+            [jnp.concatenate([one, side], axis=1), jnp.concatenate([side, one], axis=1)], axis=0
+        )
+
+    def left_of(tiles):
+        return jnp.concatenate([load_tile(lhs_ref, t) for t in tiles], axis=1)
+
+    def work(tiles, value, acc):
+        for r in range(TILE // 8):
+            for h in range(2):
+                t = jnp.maximum(value[r * 8 : r * 8 + 8, h * slots : (h + 1) * slots], 0.0)
+                acc[r] = acc[r] + t * t * t
+
+    def emit(cell, acc):
+        res_ref[cell] = (acc[0] + acc[1]) + (acc[2] + acc[3])
+
+    run_items(dims, slots, list_ref, GROUP, 2, 4, right_of, left_of, work, emit)
     lane = lax.broadcasted_iota(jnp.int32, (1, slots), 1)
     for p in range(planes):
 
-        def cell_step(i, _):
-            y, z = i // gz, i % gz
-            x3 = [p1[k, p, y, pl.ds(z, 1), :] for k in range(3)]
-            count = c1[p, y, z]
-            right = build_center(dims, p, y, z, x3, count, None)
-            cell = p * gy * gz + i
-            acc = [jnp.zeros((8, slots), F32) for _ in range(4)]
-            for slot in range(27):
-                u = jnp.dot(lhs_ref[list_ref[cell * 27 + slot]], right, preferred_element_type=F32)
-                for r in range(slots // 8):
-                    t = jnp.maximum(u[r * 8 : r * 8 + 8], 0.0)
-                    acc[r % 4] = acc[r % 4] + t * t * t
-            total = jnp.sum((acc[0] + acc[1]) + (acc[2] + acc[3]), axis=0, keepdims=True)
-            total = total - jnp.where(lane < count, 1.0, 0.0)
-            emb = -lax.rsqrt(1.0 + total / slots)
-            emb_ref[p, y, pl.ds(z, 1), :] = emb
-            if p == 0:
-                lo_ref[0, y, pl.ds(z, 1), :] = emb
-            if p == planes - 1:
-                hi_ref[0, y, pl.ds(z, 1), :] = emb
+        def row(y, _):
+            for z in range(gz):
+                total = jnp.sum(res_ref[(p * gy + y) * gz + z], axis=0, keepdims=True)
+                total = total - jnp.where(lane < c1[p, y, z], 1.0, 0.0)
+                emb = -lax.rsqrt(1.0 + total / slots)
+                emb_ref[p, y, z : z + 1, :] = emb
+                if p == 0:
+                    lo_ref[0, y, z : z + 1, :] = emb
+                if p == planes - 1:
+                    hi_ref[0, y, z : z + 1, :] = emb
             return 0
 
-        lax.fori_loop(0, gy * gz, cell_step, 0)
+        lax.fori_loop(0, gy, row, 0)
+
+
+def load_tile(ref, index):
+    per = ref.shape[1] // TILE
+    return ref[index // per, pl.ds(pl.multiple_of((index % per) * TILE, TILE), TILE), :]
+
+
+def build_rights(dims, pos, cnt, emb, right_ref):
+    planes, gy, gz = dims
+    for p in range(planes):
+
+        def row(y, _):
+            for z in range(gz):
+                x3 = [pos[k, p, y, z : z + 1, :] for k in range(3)]
+                e_row = None if emb is None else emb[p, y, z : z + 1, :]
+                right_ref[(p * gy + y) * gz + z] = build_center(
+                    dims, p, y, jnp.int32(z), x3, cnt[p, y, z], e_row
+                )
+            return 0
+
+        lax.fori_loop(0, gy, row, 0)
+
+
+def run_items(dims, slots, list_ref, group, width, chains, right_of, left_of, work, emit):
+    head, items, _ = list_sizes(dims, slots)
+    tiles_at = head + items
+    turns = ITEM // (2 * width)
+
+    def inner(*flat):
+        accs = [
+            [[flat[(i * 2 + m) * turns + t] for t in range(turns)] for m in range(2)]
+            for i in range(group)
+        ]
+
+        def tile_ids(item, m, t):
+            return [list_ref[tiles_at + item * ITEM + (t * 2 + m) * width + w] for w in range(width)]
+
+        def load_right(item):
+            right = right_of(list_ref[head + item])
+            for m in range(2):
+                pltpu.matmul_push_rhs(right, staging_register=0, mxu_index=m)
+
+        def send(item, i, m, t):
+            pltpu.matmul_acc_lhs(
+                accs[i][m][t],
+                left_of(tile_ids(item, m, t)),
+                load_staged_rhs=0 if t == 0 else None,
+            )
+
+        for i in range(group):
+            load_right(i)
+            for t in range(turns):
+                for m in range(2):
+                    send(i, i, m, t)
+
+        def step(turn, carry):
+            acc = list(carry)
+            for i in range(group):
+                item = turn * group + i
+                cell = list_ref[head + item]
+                same = cell == list_ref[head + jnp.maximum(item - 1, 0)]
+                keep = same.astype(F32)
+                acc = [value * keep for value in acc]
+                load_right(item + group)
+                for t in range(turns):
+                    for m in range(2):
+                        value = pltpu.matmul_pop(accs[i][m][t])
+                        send(item + group, i, m, t)
+                        work(tile_ids(item, m, t), value, acc)
+                emit(cell, acc)
+            return tuple(acc)
+
+        zero = jnp.zeros((8, slots), F32)
+        lax.fori_loop(0, list_ref[0] // group, step, (zero,) * chains)
+        for i in range(group):
+            for t in range(turns):
+                for m in range(2):
+                    pltpu.matmul_pop(accs[i][m][t])
+
+    pl.run_scoped(
+        inner,
+        *[
+            pltpu.ACC(m)((TILE, 2 * slots), F32)
+            for _ in range(group)
+            for m in range(2)
+            for _ in range(turns)
+        ],
+    )
 
 
 def force_kernel(dims, *refs):
-    (p0, p1, p2, c0, c1, c2, e0, e1, e2, vel, list_ref) = refs[:11]
-    (f_ref, v_ref, s_ref) = refs[11:14]
-    edges = refs[14:-2]
-    (lhs_ref, yb_ref) = refs[-2:]
+    (p0, p1, p2, c0, c1, c2, e0, e1, e2, vel, list_ref, table_ref) = refs[:12]
+    (f_ref, v_ref, s_ref) = refs[12:15]
+    edges = refs[15:-6]
+    (lhs_ref, right_ref, res_ref, *wide_refs) = refs[-6:]
     planes, gy, gz = dims
     slots = lhs_ref.shape[1]
-    build_partners(dims, (p0, p1, p2), (c0, c1, c2), (e0, e1, e2), lhs_ref, yb_ref)
+    pl.run_scoped(
+        functools.partial(build_partners, dims, (p0, p1, p2), (c0, c1, c2), (e0, e1, e2), lhs_ref, wide_refs),
+        *[pltpu.ACC(m)((slots, 2 * slots), F32) for m in range(2) for _ in range(gz + 2 * m)],
+    )
+    build_rights(dims, p1, c1, e1, right_ref)
+    gap = jnp.zeros((2 * slots - KDIM, 2 * slots), BF)
+    side = jnp.zeros((TILE, slots), BF)
+
+    def right_of(cell):
+        return jnp.concatenate([right_ref[cell], gap], axis=0)
+
+    def left_of(tiles):
+        return jnp.concatenate([load_tile(lhs_ref, tiles[0]), side], axis=1)
+
+    def work(tiles, value, acc):
+        where = table_ref[tiles[0]]
+        spots = (where & 1023, (where >> 10) & 1023, where >> 20)
+        wides = [load_tile(ref, spot) for ref, spot in zip(wide_refs, spots)]
+        for r in range(TILE // 8):
+            here = slice(r * 8, r * 8 + 8)
+            t = jnp.maximum(value[here, :slots], 0.0)
+            g = t * t * value[here, slots:]
+            half = (r % 2) * 4
+            acc[half] = acc[half] + g
+            for k in range(3):
+                acc[half + 1 + k] = acc[half + 1 + k] + g * wides[k][here]
+
+    def emit(cell, acc):
+        for k in range(4):
+            res_ref[cell, k] = acc[k] + acc[k + 4]
+
+    run_items(dims, slots, list_ref, 2, 1, 8, right_of, left_of, work, emit)
     lane = lax.broadcasted_iota(jnp.int32, (1, slots), 1)
     sums = (jnp.zeros((1, slots), F32), jnp.zeros((1, slots), F32))
     for p in range(planes):
 
-        def cell_step(i, sums):
-            y, z = i // gz, i % gz
-            x3 = [p1[k, p, y, pl.ds(z, 1), :] for k in range(3)]
-            count = c1[p, y, z]
-            right = build_center(dims, p, y, z, x3, count, e1[p, y, pl.ds(z, 1), :])
-            cell = p * gy * gz + i
-            zero = jnp.zeros((8, slots), F32)
-            s0, s1, extra = zero, [zero] * 3, [zero] * 3
-            for slot, offset in enumerate(OFFSETS):
-                both = jnp.dot(lhs_ref[list_ref[cell * 27 + slot]], right, preferred_element_type=F32)
-                base = ((p + 1 + offset[0]) * gy + wrap(y + offset[1], gy)) * gz + wrap(z + offset[2], gz)
-                part = None
-                for r in range(slots // 8):
-                    here = slice(r * 8, r * 8 + 8)
-                    t = jnp.maximum(both[here, :slots], 0.0)
-                    g = t * t * both[here, slots:]
-                    part = g if part is None else part + g
-                    for k in range(3):
-                        s1[k] = s1[k] + g * yb_ref[base, k, here, :]
-                s0 = s0 + part
+        def row(y, sums):
+            ff, vv = sums
+            for z in range(gz):
+                cell = (p * gy + y) * gz + z
+                one = slice(z, z + 1)
+                center = (
+                    p + 0.5 - (planes + 1) / 2,
+                    y.astype(F32) + 0.5 - (gy + 1) / 2,
+                    z + 0.5 - (gz + 1) / 2,
+                )
+                total = jnp.sum(res_ref[cell, 0], axis=0, keepdims=True)
                 for k in range(3):
-                    if offset[k] == 1:
-                        extra[k] = extra[k] + part
-                    elif offset[k] == -1:
-                        extra[k] = extra[k] - part
-            total = jnp.sum(s0, axis=0, keepdims=True)
-            ff, vv = sums
-            for k in range(3):
-                f = (24.0 / slots) * (
-                    x3[k] * total - jnp.sum(s1[k] + extra[k], axis=0, keepdims=True)
-                )
-                f_ref[k, p, y, pl.ds(z, 1), :] = f
-                v = jnp.where(lane < count, vel[k, p, y, pl.ds(z, 1), :], 0.0) + STEP_SIZE * f
-                v_ref[k, p, y, pl.ds(z, 1), :] = v
-                if edges and p == 0:
-                    edges[0][k, 0, y, pl.ds(z, 1), :] = f
-                    edges[0][k + 3, 0, y, pl.ds(z, 1), :] = v
-                if edges and p == planes - 1:
-                    edges[1][k, 0, y, pl.ds(z, 1), :] = f
-                    edges[1][k + 3, 0, y, pl.ds(z, 1), :] = v
-                ff = ff + f * f
-                vv = vv + v * v
+                    x = p1[k, p, y, one, :] + center[k]
+                    f = (24.0 / slots) * (x * total - jnp.sum(res_ref[cell, k + 1], axis=0, keepdims=True))
+                    f_ref[k, p, y, one, :] = f
+                    v = jnp.where(lane < c1[p, y, z], vel[k, p, y, one, :], 0.0) + STEP_SIZE * f
+                    v_ref[k, p, y, one, :] = v
+                    if edges and p == 0:
+                        edges[0][k, 0, y, one, :] = f
+                        edges[0][k + 3, 0, y, one, :] = v
+                    if edges and p == planes - 1:
+                        edges[1][k, 0, y, one, :] = f
+                        edges[1][k + 3, 0, y, one, :] = v
+                    ff = ff + f * f
+                    vv = vv + v * v
             return ff, vv
 
-        sums = lax.fori_loop(0, gy * gz, cell_step, sums)
+        sums = lax.fori_loop(0, gy, row, sums)
     s_ref[...] = jnp.concatenate([sums[0], sums[1], jnp.zeros((6, slots), F32)], axis=0)
 
 
@@ -368,7 +551,9 @@
     vmem = pl.BlockSpec(memory_space=pltpu.VMEM)
     smem = pl.BlockSpec(memory_space=pltpu.SMEM)
     ext = (planes + 2) * (gy + 2) * (gz + 2) + 1
-    entries = planes * gy * gz * 27
+    cells = planes * gy * gz
+    entries = list_sizes(dims, slots)[2]
+    table = jnp.asarray(wide_table(dims, slots))
     pairs = planes * gy * gz * 27 * slots * slots
 
     def shaped(*shape):
@@ -383,7 +568,16 @@
     flags_lo = lax.ppermute(lax.slice_in_dim(pair_flags, planes - 1, planes, axis=1), "space", up)
     count_lo, count_hi = halo(*planes_of(counts, 0))
     pos_lo, pos_hi = halo(*planes_of(start_pos, 1))
-    lhs_scratch = pltpu.VMEM((ext, slots, KDIM), BF)
+    lhs_scratch = pltpu.VMEM((ext, slots, slots), BF)
+    scratch_d = [lhs_scratch, pltpu.VMEM((cells, KDIM, slots), BF), pltpu.VMEM((cells, 8, slots), F32)]
+    scratch_f = [
+        lhs_scratch,
+        pltpu.VMEM((cells, KDIM, 2 * slots), BF),
+        pltpu.VMEM((cells, 4, 8, slots), F32),
+        pltpu.VMEM(((planes + 2) * gy * gz, slots, slots), F32),
+        pltpu.VMEM(((planes + 2) * (gy + 2) * gz, slots, slots), F32),
+        pltpu.VMEM(((planes + 2) * gy * (gz + 2), slots, slots), F32),
+    ]
     emb_shape = [shaped(planes, gy, gz, slots), shaped(1, gy, gz, slots), shaped(1, gy, gz, slots)]
     vec, edge = shaped(3, planes, gy, gz, slots), shaped(3, 1, gy, gz, slots)
     pack = shaped(6, 1, gy, gz, slots)
@@ -417,7 +611,7 @@
                 out_shape=(*emb_shape, jax.ShapeDtypeStruct((entries,), jnp.int32)),
                 in_specs=specs + [smem, smem],
                 out_specs=(vmem, vmem, vmem, smem),
-                scratch_shapes=[lhs_scratch],
+                scratch_shapes=scratch_d,
                 compiler_params=pltpu.CompilerParams(vmem_limit_bytes=12 * 2**20),
                 cost_estimate=cost_d,
                 name="density_first",
@@ -428,7 +622,7 @@
                 out_shape=(*emb_shape, edge, vec, edge, vec),
                 in_specs=specs + [smem] + [vmem] * (4 + space),
                 out_specs=(vmem,) * 7,
-                scratch_shapes=[lhs_scratch],
+                scratch_shapes=scratch_d,
                 compiler_params=pltpu.CompilerParams(vmem_limit_bytes=12 * 2**20),
                 cost_estimate=cost_d,
                 name="density_next",
@@ -439,16 +633,13 @@
         forces, pushed, part, *edges = pl.pallas_call(
             functools.partial(force_kernel, dims),
             out_shape=(vec, vec, shaped(8, slots), *(() if last else (pack, pack))),
-            in_specs=specs + [vmem] * 4 + [smem],
+            in_specs=specs + [vmem] * 4 + [smem] * 2,
             out_specs=(vmem,) * (3 if last else 5),
-            scratch_shapes=[
-                lhs_scratch,
-                pltpu.VMEM(((planes + 2) * gy * gz, 3, slots, slots), F32),
-            ],
-            compiler_params=pltpu.CompilerParams(vmem_limit_bytes=26 * 2**20),
+            scratch_shapes=scratch_f,
+            compiler_params=pltpu.CompilerParams(vmem_limit_bytes=34 * 2**20),
             cost_estimate=cost_f,
             name="force",
-        )(*args, emb_lo, emb, emb_hi, motion, blocks)
+        )(*args, emb_lo, emb, emb_hi, motion, blocks, table)
         sums = [part] + [lax.ppermute(part, "space", ring("space", s)) for s in range(1, space)]
         if not last:
             packs = halo(*edges)

time: 148 us -> 247 us (1.67)
  Pallas kernels: 111 us -> 208 us
  starting transfers between devices: 20.4 us -> 23.9 us
    pallas_call x2, Pallas kernels: 70.6 us -> 144 us  [body(): pl.pallas_call(functools.partial(force_kernel, dims), out_shape=(vec, vec...]
    pallas_call x1, Pallas kernels: 21.5 us -> 36.8 us  [body(): pl.pallas_call(functools.partial(density_kernel, dims, True), out_shape=(...]
    pallas_call x1, Pallas kernels: 17.9 us -> 25.8 us  [body(): pl.pallas_call(functools.partial(density_kernel, dims, False), out_shape=...]
    ppermute x6, starting transfers between devices: 3.06 us -> 5.79 us  [body(): lax.ppermute(part, 'space', ring('space', s))]
  transfers between devices with their start and end apart: 21 -> 21, of which waited for: 12 -> 11; matrix products, arithmetic and copies ran while one was open for 0% -> 0% of each run, Pallas kernels for 36% -> 40%
where the time goes in v3:
time: 247 us; the launch traced here: 246 us
  Pallas kernels  208 us (84%)
  starting transfers between devices  23.9 us (10%)
  waiting for transfers between devices  11.2 us (5%)
    pallas_call x2, Pallas kernels, body(): pl.pallas_call(functools.partial(force_kernel, dims), out_shape=(vec, vec...  144 us
    pallas_call x1, Pallas kernels, body(): pl.pallas_call(functools.partial(density_kernel, dims, True), out_shape=(...  36.8 us
    pallas_call x1, Pallas kernels, body(): pl.pallas_call(functools.partial(density_kernel, dims, False), out_shape=...  25.8 us
    ppermute x10, starting transfers between devices, halo(): return (lax.ppermute(last, 'space', up), lax.ppermute(first, 'space', down))  10.5 us
    ppermute x4, starting transfers between devices, hop(): options.append(lax.ppermute(held, 'rep', pairs))  6.3 us
    ppermute x6, starting transfers between devices, body(): lax.ppermute(part, 'space', ring('space', s))  5.79 us
    ppermute x6, waiting for transfers between devices, body(): lax.ppermute(part, 'space', ring('space', s))  5.09 us
  transfers between devices with their start and end apart: 21, of which 11 were waited for; matrix products, arithmetic and copies ran while one was open for 0% of the time, Pallas kernels for 40%

profile of v3, /device:TPU:0, one launch (start us, length us, event | category | flops | bytes accessed | tf_op | source)
XLA Modules:
  0.0 246.4 jit_solution(7714936707189670590)
XLA Ops:
  0.6 0.8 fusion
  1.4 0.5 collective-permute-start
  1.9 2.0 collective-permute-start.1
  4.0 1.4 collective-permute-start.4
  5.4 1.1 collective-permute-start.2
  6.4 0.7 collective-permute-start.3
  7.3 1.1 collective-permute-done.2.refs_3_
  8.5 36.8 %density_first.1 = (f32[2,4,4,128]{3,2,1,0:T(4,128)S(1)}, f32[1,4,4,128]{3,2,1,0:T(4,128)S(1)}, f32[1,4,4,128]{3,2,1,0:T(4,128)S(1)}, s32[3880]{0:T(1024)S(1)}) custom-call(f32[3,1,4,4,128]{4,3,2,1,0:T(4,128)S(1)} %collective-permute-done.refs_0_, f32[3,2,4,4,128]{4,3,2,1,0:T(4,128)S(1)} %bitcast.11, ...), custom_call_target="tpu_custom_call" | custom-call | flops 141557760 | bytes 1048576 | tf_op jit(solution)/shard_map/density_first/pallas_call | solution.py:609
  45.3 2.0 collective-permute-start.5
  47.2 1.2 collective-permute-done.5.refs_6_
  48.6 72.2 %force.2 = (f32[3,2,4,4,128]{4,3,2,1,0:T(4,128)S(1)}, f32[3,2,4,4,128]{4,3,2,1,0:T(4,128)S(1)}, f32[8,128]{1,0:T(8,128)S(1)}, f32[6,1,4,4,128]{4,3,2,1,0:T(4,128)S(1)}, f32[6,1,4,4,128]{4,3,2,1,0:T(4,128)S(1)}) custom-call(f32[3,1,4,4,128]{4,3,2,1,0:T(4,128)S(1)} %collective-permute-done.refs_0_, f32[3,2,4,4,128]{4,3,2,1,0:T(4,128)S(1)} %bitcast.12, ...), custom_call_target="tpu_custom_call" | custom-call | flops 353894400 | bytes 1048576 | tf_op jit(solution)/shard_map/force/pallas_call | solution.py:633
  120.8 2.5 %collective-permute-start.14 = (f32[6,2,4,4,128]{4,3,2,1,0:T(4,128)S(1)}, f32[6,2,4,4,128]{4,3,2,1,0:T(4,128)S(1)}, u32[]{:S(2)}, u32[]{:S(2)}) collective-permute-start(f32[6,2,4,4,128]{4,3,2,1,0:T(4,128)S(1)} %pad_maximum_fusion), channel_id=1, source_target_pairs={{0,12},{4,0},{8,4},{12,8},{16,28},{20,16},{24,20},{28,24},{1,13},{... | collective-permute-start | bytes 294920 | tf_op jit(solution)/shard_map/ppermute | solution.py:600
  123.4 0.4 collective-permute-start.15
  123.8 0.7 collective-permute-start.16
  124.5 0.7 copy-done.6
  125.3 2.1 collective-permute-start.7
  127.4 1.2 collective-permute-done.15
  128.6 1.1 collective-permute-done.16
  129.7 2.6 %collective-permute-start.17 = (f32[6,2,4,4,128]{4,3,2,1,0:T(4,128)S(1)}, f32[6,2,4,4,128]{4,3,2,1,0:T(4,128)S(1)}, u32[]{:S(2)}, u32[]{:S(2)}) collective-permute-start(f32[6,2,4,4,128]{4,3,2,1,0:T(4,128)S(1)} %select_select_fusion.refs_6_), channel_id=1, source_target_pairs={{0,16},{4,20},{8,24},{12,28},{16,0},{20,4},{24,8},{28,12},{1,17},{... | collective-permute-start | bytes 294920 | tf_op jit(solution)/shard_map/ppermute | solution.py:600
  132.4 0.6 collective-permute-start.9
  133.0 0.7 collective-permute-start.10
  133.7 1.7 collective-permute-done.9.refs_12_
  135.4 1.2 collective-permute-done.10.refs_13_
  136.8 25.8 %density_next.1 = (f32[2,4,4,128]{3,2,1,0:T(4,128)S(1)}, f32[1,4,4,128]{3,2,1,0:T(4,128)S(1)}, f32[1,4,4,128]{3,2,1,0:T(4,128)S(1)}, f32[3,1,4,4,128]{4,3,2,1,0:...) custom-call(f32[3,1,4,4,128]{4,3,2,1,0:T(4,128)S(1)} %collective-per, ...), custom_call_target="tpu_custom_call" | custom-call | flops 141557760 | bytes 1048576 | tf_op jit(solution)/shard_map/density_next/pallas_call | solution.py:620
  162.5 2.1 collective-permute-start.12
  164.7 1.0 collective-permute-done.12.refs_6_
  165.7 0.4 collective-permute-done.13.refs_8_
  166.1 72.3 %force.3 = (f32[3,2,4,4,128]{4,3,2,1,0:T(4,128)S(1)}, f32[3,2,4,4,128]{4,3,2,1,0:T(4,128)S(1)}, f32[8,128]{1,0:T(8,128)S(1)}) custom-call(f32[3,1,4,4,128]{4,3,2,1,0:T(4,128)S(1)} %get-tuple-element.37.refs_0_, f32[3,2,4,4,128]{4,3,2,1,0:T(4,128)S(1)} %get-tuple-element.36.refs_1_.refs_0_, f32[3,1,4,4,128]{4,3,2,1,0:T(4,128)S(1)} %get-tuple-element.38.refs_2_, ...), custom_call_target="tpu_custom_call" | custom-call | flops 353894400 | bytes 1048576 | tf_op jit(solution)/shard_map/force/pallas_call | solution.py:633
  238.4 3.0 %collective-permute-start.18 = (f32[8,128]{1,0:T(8,128)S(1)}, f32[8,128]{1,0:T(8,128)S(1)}, u32[]{:S(2)}, u32[]{:S(2)}) collective-permute-start(f32[8,128]{1,0:T(8,128)S(1)} %get-tuple-element.45.refs_8_), channel_id=1, source_target_pairs={{0,1},{1,2},{2,3},{3,0},{4,5},{5,6},{6,7},{7,4},{8,9},{9,10},{10,1... | collective-permute-start | bytes 12296 | tf_op jit(solution)/shard_map/ppermute | solution.py:643
  241.4 1.4 collective-permute-start.20
  242.9 2.1 collective-permute-done.19.refs_10_
  245.0 1.4 finish.1
  (37 shorter events, 0.8 us)
Async XLA Ops:
  1.4 7.0 %collective-permute-start = (f32[3,1,4,4,128]{4,3,2,1,0:T(4,128)S(1)}, f32[3,1,4,4,128]{4,3,2,1,0:T(4,128)S(1)}, u32[]{:S(2)}, u32[]{:S(2)}) collective-permute-start(f32[3,1,4,4,128]{4,3,2,1,0:T(4,128)S(1)} %get-tuple-element.51), channel_id=1, source_target_pairs={{0,1},{1,2},{2,3},{3,0},{4,5},{5,6},{6,7},{7,4},{8,9},{9,10},{10,1... | collective-permute-start | bytes 73736 | tf_op jit(solution)/shard_map/ppermute | solution.py:566
  1.9 2.0 slice-start
  1.9 6.6 %collective-permute-start.1 = (f32[3,1,4,4,128]{4,3,2,1,0:T(4,128)S(1)}, f32[3,1,4,4,128]{4,3,2,1,0:T(4,128)S(1)}, u32[]{:S(2)}, u32[]{:S(2)}) collective-permute-start(f32[3,1,4,4,128]{4,3,2,1,0:T(4,128)S(1)} %get-tuple-element.50), channel_id=1, source_target_pairs={{0,3},{1,0},{2,1},{3,2},{4,7},{5,4},{6,5},{7,6},{8,11},{9,8},{10,9... | collective-permute-start | bytes 73736 | tf_op jit(solution)/shard_map/ppermute | solution.py:566
  3.9 1.5 copy-start.2
  3.9 3.2 %copy-start.5 = (s32[13,2,4,4]{0,3,2,1:T(4,128)S(1)}, s32[13,2,4,4]{0,3,2,1:T(4,128)}, u32[]{:S(2)}) copy-start(s32[13,2,4,4]{0,3,2,1:T(4,128)} %param.11) | copy-start | bytes 4996
  4.0 4.4 %copy-start = (f32[1,3,2,4,4,128]{5,4,3,2,1,0:T(4,128)S(1)}, f32[1,3,2,4,4,128]{5,4,3,2,1,0:T(4,128)}, u32[]{:S(2)}) copy-start(f32[1,3,2,4,4,128]{5,4,3,2,1,0:T(4,128)} %param.7) | copy-start | bytes 147460
  4.0 4.4 %collective-permute-start.4 = (s32[13,1,4,4]{3,2,1,0:T(4,128)S(1)}, s32[13,1,4,4]{3,2,1,0:T(4,128)S(1)}, u32[]{:S(2)}, u32[]{:S(2)}) collective-permute-start(s32[13,1,4,4]{3,2,1,0:T(4,128)S(1)} %copy.11), channel_id=1, source_target_pairs={{0,1},{1,2},{2,3},{3,0},{4,5},{5,6},{6,7},{7,4},{8,9},{9,10},{10,1... | collective-permute-start | bytes 2504 | tf_op jit(solution)/shard_map/ppermute | solution.py:568
  5.4 3.0 %collective-permute-start.2 = (s32[1,4,4]{2,1,0:T(4,128)S(1)}, s32[1,4,4]{2,1,0:T(4,128)S(1)}, u32[]{:S(2)}, u32[]{:S(2)}) collective-permute-start(s32[1,4,4]{2,1,0:T(4,128)S(1)} %get-tuple-element.53), channel_id=1, source_target_pairs={{0,1},{1,2},{2,3},{3,0},{4,5},{5,6},{6,7},{7,4},{8,9},{9,10},{10,1... | collective-permute-start | bytes 200 | tf_op jit(solution)/shard_map/ppermute | solution.py:566
  6.4 2.0 collective-permute-start.3
  7.3 41.3 %copy-start.3 = (f32[1,3,2,4,4,128]{5,4,3,2,1,0:T(4,128)S(1)}, f32[1,3,2,4,4,128]{5,4,3,2,1,0:T(4,128)}, u32[]{:S(2)}) copy-start(f32[1,3,2,4,4,128]{5,4,3,2,1,0:T(4,128)} %param.8) | copy-start | bytes 147460
  45.3 3.3 %copy-start.4 = (s32[580]{0:T(1024)S(1)}, s32[580]{0:T(1024)}, u32[]{:S(2)}) copy-start(s32[580]{0:T(1024)} %constant.82.clone.refs_11_) | copy-start | bytes 6964
  45.3 3.1 %collective-permute-start.5 = (f32[1,4,4,128]{3,2,1,0:T(4,128)S(1)}, f32[1,4,4,128]{3,2,1,0:T(4,128)S(1)}, u32[]{:S(2)}, u32[]{:S(2)}) collective-permute-start(f32[1,4,4,128]{3,2,1,0:T(4,128)S(1)} %get-tuple-element.28), channel_id=1, source_target_pairs={{0,1},{1,2},{2,3},{3,0},{4,5},{5,6},{6,7},{7,4},{8,9},{9,10},{10,1... | collective-permute-start | bytes 24584 | tf_op jit(solution)/shard_map/ppermute | solution.py:566
  47.2 1.4 collective-permute-start.6
  120.8 6.6 %collective-permute-start.14 = (f32[6,2,4,4,128]{4,3,2,1,0:T(4,128)S(1)}, f32[6,2,4,4,128]{4,3,2,1,0:T(4,128)S(1)}, u32[]{:S(2)}, u32[]{:S(2)}) collective-permute-start(f32[6,2,4,4,128]{4,3,2,1,0:T(4,128)S(1)} %pad_maximum_fusion), channel_id=1, source_target_pairs={{0,12},{4,0},{8,4},{12,8},{16,28},{20,16},{24,20},{28,24},{1,13},{... | collective-permute-start | bytes 294920 | tf_op jit(solution)/shard_map/ppermute | solution.py:600
  123.4 5.3 %collective-permute-start.15 = (f32[6,2,4,4,128]{4,3,2,1,0:T(4,128)S(1)}, f32[6,2,4,4,128]{4,3,2,1,0:T(4,128)S(1)}, u32[]{:S(2)}, u32[]{:S(2)}) collective-permute-start(f32[6,2,4,4,128]{4,3,2,1,0:T(4,128)S(1)} %pad_maximum_fusion), channel_id=1, source_target_pairs={{0,8},{4,12},{8,0},{12,4},{16,24},{20,28},{24,16},{28,20},{1,9},{5... | collective-permute-start | bytes 294920 | tf_op jit(solution)/shard_map/ppermute | solution.py:600
  123.8 5.9 %collective-permute-start.16 = (f32[6,2,4,4,128]{4,3,2,1,0:T(4,128)S(1)}, f32[6,2,4,4,128]{4,3,2,1,0:T(4,128)S(1)}, u32[]{:S(2)}, u32[]{:S(2)}) collective-permute-start(f32[6,2,4,4,128]{4,3,2,1,0:T(4,128)S(1)} %pad_maximum_fusion), channel_id=1, source_target_pairs={{0,4},{4,8},{8,12},{12,0},{16,20},{20,24},{24,28},{28,16},{1,5},{5... | collective-permute-start | bytes 294920 | tf_op jit(solution)/shard_map/ppermute | solution.py:600
  124.5 0.7 copy-start.6
  125.3 11.5 %collective-permute-start.7 = (f32[6,1,4,4,128]{4,3,2,1,0:T(4,128)S(1)}, f32[6,1,4,4,128]{4,3,2,1,0:T(4,128)S(1)}, u32[]{:S(2)}, u32[]{:S(2)}) collective-permute-start(f32[6,1,4,4,128]{4,3,2,1,0:T(4,128)S(1)} %get-tuple-element.33), channel_id=1, source_target_pairs={{0,1},{1,2},{2,3},{3,0},{4,5},{5,6},{6,7},{7,4},{8,9},{9,10},{10,1... | collective-permute-start | bytes 147464 | tf_op jit(solution)/shard_map/ppermute | solution.py:566
  127.4 9.3 %collective-permute-start.8 = (f32[6,1,4,4,128]{4,3,2,1,0:T(4,128)S(1)}, f32[6,1,4,4,128]{4,3,2,1,0:T(4,128)S(1)}, u32[]{:S(2)}, u32[]{:S(2)}) collective-permute-start(f32[6,1,4,4,128]{4,3,2,1,0:T(4,128)S(1)} %get-tuple-element.34), channel_id=1, source_target_pairs={{0,3},{1,0},{2,1},{3,2},{4,7},{5,4},{6,5},{7,6},{8,11},{9,8},{10,9... | collective-permute-start | bytes 147464 | tf_op jit(solution)/shard_map/ppermute | solution.py:566
  129.7 115.2 %collective-permute-start.17 = (f32[6,2,4,4,128]{4,3,2,1,0:T(4,128)S(1)}, f32[6,2,4,4,128]{4,3,2,1,0:T(4,128)S(1)}, u32[]{:S(2)}, u32[]{:S(2)}) collective-permute-start(f32[6,2,4,4,128]{4,3,2,1,0:T(4,128)S(1)} %select_select_fusion.refs_6_), channel_id=1, source_target_pairs={{0,16},{4,20},{8,24},{12,28},{16,0},{20,4},{24,8},{28,12},{1,17},{... | collective-permute-start | bytes 294920 | tf_op jit(solution)/shard_map/ppermute | solution.py:600
  132.4 3.0 %collective-permute-start.9 = (f32[8,128]{1,0:T(8,128)S(1)}, f32[8,128]{1,0:T(8,128)S(1)}, u32[]{:S(2)}, u32[]{:S(2)}) collective-permute-start(f32[8,128]{1,0:T(8,128)S(1)} %get-tuple-element.35.refs_11_), channel_id=1, source_target_pairs={{0,1},{1,2},{2,3},{3,0},{4,5},{5,6},{6,7},{7,4},{8,9},{9,10},{10,1... | collective-permute-start | bytes 12296 | tf_op jit(solution)/shard_map/ppermute | solution.py:643
  133.0 3.6 %collective-permute-start.10 = (f32[8,128]{1,0:T(8,128)S(1)}, f32[8,128]{1,0:T(8,128)S(1)}, u32[]{:S(2)}, u32[]{:S(2)}) collective-permute-start(f32[8,128]{1,0:T(8,128)S(1)} %get-tuple-element.35.refs_11_), channel_id=1, source_target_pairs={{0,2},{1,3},{2,0},{3,1},{4,6},{5,7},{6,4},{7,5},{8,10},{9,11},{10,... | collective-permute-start | bytes 12296 | tf_op jit(solution)/shard_map/ppermute | solution.py:643
  135.4 1.3 collective-permute-start.11
  162.5 3.1 %collective-permute-start.12 = (f32[1,4,4,128]{3,2,1,0:T(4,128)S(1)}, f32[1,4,4,128]{3,2,1,0:T(4,128)S(1)}, u32[]{:S(2)}, u32[]{:S(2)}) collective-permute-start(f32[1,4,4,128]{3,2,1,0:T(4,128)S(1)} %get-tuple-element.39), channel_id=1, source_target_pairs={{0,1},{1,2},{2,3},{3,0},{4,5},{5,6},{6,7},{7,4},{8,9},{9,10},{10,1... | collective-permute-start | bytes 24584 | tf_op jit(solution)/shard_map/ppermute | solution.py:566
  164.7 1.4 collective-permute-start.13
  238.4 4.5 %collective-permute-start.18 = (f32[8,128]{1,0:T(8,128)S(1)}, f32[8,128]{1,0:T(8,128)S(1)}, u32[]{:S(2)}, u32[]{:S(2)}) collective-permute-start(f32[8,128]{1,0:T(8,128)S(1)} %get-tuple-element.45.refs_8_), channel_id=1, source_target_pairs={{0,1},{1,2},{2,3},{3,0},{4,5},{5,6},{6,7},{7,4},{8,9},{9,10},{10,1... | collective-permute-start | bytes 12296 | tf_op jit(solution)/shard_map/ppermute | solution.py:643
  241.4 3.6 %collective-permute-start.19 = (f32[8,128]{1,0:T(8,128)S(1)}, f32[8,128]{1,0:T(8,128)S(1)}, u32[]{:S(2)}, u32[]{:S(2)}) collective-permute-start(f32[8,128]{1,0:T(8,128)S(1)} %get-tuple-element.45.refs_8_), channel_id=1, source_target_pairs={{0,2},{1,3},{2,0},{3,1},{4,6},{5,7},{6,4},{7,5},{8,10},{9,11},{10,... | collective-permute-start | bytes 12296 | tf_op jit(solution)/shard_map/ppermute | solution.py:643
  241.4 3.6 %collective-permute-start.20 = (f32[8,128]{1,0:T(8,128)S(1)}, f32[8,128]{1,0:T(8,128)S(1)}, u32[]{:S(2)}, u32[]{:S(2)}) collective-permute-start(f32[8,128]{1,0:T(8,128)S(1)} %get-tuple-element.45.refs_8_), channel_id=1, source_target_pairs={{0,3},{1,0},{2,1},{3,2},{4,7},{5,4},{6,5},{7,6},{8,11},{9,8},{10,9... | collective-permute-start | bytes 12296 | tf_op jit(solution)/shard_map/ppermute | solution.py:643
  242.8 2.2 copy-start.1

commit v4 on v3

--- a/solution.py
+++ b/solution.py
@@ -3,7 +3,6 @@
 
 import jax
 import jax.numpy as jnp
-import numpy as np
 from jax import lax
 from jax.experimental import pallas as pl
 from jax.experimental.pallas import tpu as pltpu
@@ -26,8 +25,7 @@
 BF = jnp.bfloat16
 F32 = jnp.float32
 KDIM = 64
-TILE = 32
-ITEM = 12
+ITEM = 3
 GROUP = 4
 
 
@@ -57,47 +55,39 @@
     return jnp.where(index >= size, index - size, index)
 
 
-def list_sizes(dims, slots):
-    cells = math.prod(dims)
-    most = cells * (-(-27 * (slots // TILE) // ITEM))
+def list_sizes(dims):
+    most = math.prod(dims) * -(-27 // ITEM)
     head = 8
     return head, most + 2 * GROUP, head + (most + 2 * GROUP) * (ITEM + 1) + 2 * ITEM
 
 
-def build_list(dims, slots, cnt, flags, flags_lo, list_ref):
+def build_list(dims, flags, flags_lo, list_ref):
     planes, gy, gz = dims
     ey, ez = gy + 2, gz + 2
-    per = slots // TILE
-    dummy = (planes + 2) * ey * ez * per
-    head, items, _ = list_sizes(dims, slots)
-    tiles = head + items
-    bound = -(-27 * per // ITEM)
-
-    def count_at(j, y, z):
-        which, at = (0, 0) if j == 0 else ((2, 0) if j == planes + 1 else (1, j - 1))
-        return cnt[which][at, y, z]
+    dummy = (planes + 2) * ey * ez
+    head, items, _ = list_sizes(dims)
+    entries = head + items
+    bound = -(-27 // ITEM)
 
     def cell_list(p, y, z, item):
         at = item * ITEM
         for ox, oy, oz in OFFSETS:
-            ext = ((p + 1 + ox) * ey + (y + 1 + oy)) * ez + (z + 1 + oz)
+            list_ref[entries + at] = ((p + 1 + ox) * ey + (y + 1 + oy)) * ez + (z + 1 + oz)
+            found = flag_of((ox, oy, oz))
+            if found is None:
+                at = at + 1
+                continue
+            index, forward = found
             jy, jz = wrap(y + oy, gy), (z + oz) % gz
-            number = (count_at(p + 1 + ox, jy, jz) + (TILE - 1)) // TILE
-            found = flag_of((ox, oy, oz))
-            if found is not None:
-                index, forward = found
-                if forward:
-                    flag = flags[index, p, y, z]
-                elif p + ox < 0:
-                    flag = flags_lo[index, 0, jy, jz]
-                else:
-                    flag = flags[index, p + ox, jy, jz]
-                number = number * flag
-            for t in range(per):
-                list_ref[tiles + at + t] = ext * per + t
-            at = at + number
+            if forward:
+                flag = flags[index, p, y, z]
+            elif p + ox < 0:
+                flag = flags_lo[index, 0, jy, jz]
+            else:
+                flag = flags[index, p + ox, jy, jz]
+            at = at + flag
         for t in range(ITEM):
-            list_ref[tiles + at + t] = dummy
+            list_ref[entries + at + t] = dummy
         for t in range(bound):
             list_ref[head + item + t] = (p * gy + y) * gz + z
         return (at + (ITEM - 1)) // ITEM
@@ -116,13 +106,13 @@
     def rest(i, _):
         list_ref[head + item + i] = planes * gy * gz - 1
         for t in range(ITEM):
-            list_ref[tiles + (item + i) * ITEM + t] = dummy
+            list_ref[entries + (item + i) * ITEM + t] = dummy
         return 0
 
     lax.fori_loop(0, 2 * GROUP - 1, rest, 0)
 
 
-def build_partners(dims, pos, cnt, emb, lhs_ref, wide_refs, *accs):
+def build_partners(dims, pos, cnt, emb, lhs_ref, wide_ref, *accs):
     planes, gy, gz = dims
     ey, ez = gy + 2, gz + 2
     slots = lhs_ref.shape[1]
@@ -137,21 +127,26 @@
         lhs_ref[ext] = tall
         return tall
 
-    if wide_refs is not None:
+    if wide_ref is not None:
         row = lax.broadcasted_iota(jnp.int32, (2 * slots, 2 * slots), 0)
         col = lax.broadcasted_iota(jnp.int32, (2 * slots, 2 * slots), 1) // slots
-        used = (row < 8) | ((row >= 24) & (row < 32)) | ((row >= 48) & (row < 56))
+        line_row = row % slots
+        used = (line_row < 8) | ((line_row >= 24) & (line_row < 32)) | ((line_row >= 48) & (line_row < 56))
         side = jnp.zeros((slots, slots), BF)
-        wide_x, wide_y, wide_z = wide_refs
+        half = slots // 2
         acc_xy, acc_z = accs[:gz], accs[gz:]
-        for m, base in enumerate((0, 2)):
-            pick = jnp.where(used & (row % 8 == col + base) & (col + base < 3), 1.0, 0.0)
+        for m in range(2):
+            if m == 0:
+                chosen = used & (row < slots) & (line_row % 8 == col)
+            else:
+                chosen = used & (row // slots == col) & (line_row % 8 == 2)
+            pick = jnp.where(chosen, 1.0, 0.0)
             pltpu.matmul_push_rhs(pick.astype(BF), staging_register=0, mxu_index=m)
         for m in range(2):
             for index, acc in enumerate((acc_xy, acc_z)[m]):
                 pltpu.matmul_acc_lhs(
                     acc,
-                    jnp.zeros((slots, 2 * slots), BF),
+                    jnp.zeros((slots if m == 0 else half, 2 * slots), BF),
                     load_staged_rhs=0 if index == 0 else None,
                 )
 
@@ -173,51 +168,40 @@
         return store((j * ey + y) * ez + z, value)
 
     def put(spot):
-        at_x, at_y, at_z = spot
-        for z in range(gz):
-            both = pltpu.matmul_pop(acc_xy[z])
-            wide_x[at_x + z] = both[:, :slots]
-            wide_y[at_y + z] = both[:, slots:]
+        for z in range(1, gz + 1):
+            both = pltpu.matmul_pop(acc_xy[z - 1])
+            for at in [z] + [0] * (z == gz) + [gz + 1] * (z == 1):
+                wide_ref[spot + at, 0] = both[:, :slots]
+                wide_ref[spot + at, 1] = both[:, slots:]
         for z in range(ez):
-            wide_z[at_z + z] = pltpu.matmul_pop(acc_z[z])[:, :slots]
-
-    spot = (jnp.int32(0),) * 3
+            both = pltpu.matmul_pop(acc_z[z])
+            wide_ref[spot + z, 2, :half, :] = both[:, :slots]
+            wide_ref[spot + z, 2, half:, :] = both[:, slots:]
+
+    spot = jnp.int32(0)
     for j in range(planes + 2):
         which, at = (0, 0) if j == 0 else ((2, 0) if j == planes + 1 else (1, j - 1))
 
         def line(y, spot):
             by = wrap(y - 1, gy)
             talls = [one(j, which, at, y, z, by, (z - 1) % gz) for z in range(ez)]
-            if wide_refs is None:
+            if wide_ref is None:
                 return spot
             put(spot)
             for z in range(ez):
-                left = jnp.concatenate([talls[z], side], axis=1)
                 if 1 <= z <= gz:
-                    pltpu.matmul_acc_lhs(acc_xy[z - 1], left)
-                pltpu.matmul_acc_lhs(acc_z[z], left)
-            return ((j * gy + by) * gz, (j * ey + y) * gz, (j * gy + by) * ez)
+                    pltpu.matmul_acc_lhs(acc_xy[z - 1], jnp.concatenate([talls[z], side], axis=1))
+                pltpu.matmul_acc_lhs(
+                    acc_z[z], jnp.concatenate([talls[z][:half], talls[z][half:]], axis=1)
+                )
+            return (j * ey + y) * ez
 
         spot = lax.fori_loop(0, ey, line, spot)
-    if wide_refs is not None:
+    if wide_ref is not None:
         put(spot)
+        for k in range(3):
+            wide_ref[(planes + 2) * ey * ez, k] = jnp.zeros((slots, slots), F32)
     store((planes + 2) * ey * ez, jnp.where(rows == 3, FAR, jnp.where(rows >= 4, 1.0, 0.0)))
-
-
-def wide_table(dims, slots):
-    planes, gy, gz = dims
-    ey, ez = gy + 2, gz + 2
-    per = slots // TILE
-    table = np.zeros(((planes + 2) * ey * ez + 1) * per, np.int32)
-    for j in range(planes + 2):
-        for y in range(ey):
-            for z in range(ez):
-                by, bz = (y - 1) % gy, (z - 1) % gz
-                where = ((j * gy + by) * gz + bz, (j * ey + y) * gz + bz, (j * gy + by) * ez + z)
-                for t in range(per):
-                    x0, y0, z0 = (w * per + t for w in where)
-                    table[((j * ey + y) * ez + z) * per + t] = x0 | (y0 << 10) | (z0 << 20)
-    return table
 
 
 def build_center(dims, p, y, z, x3, count, e_row):
@@ -283,7 +267,7 @@
     planes, gy, gz = dims
     if first:
         (p0, p1, p2, c0, c1, c2, fl, fl_lo, emb_ref, lo_ref, hi_ref, list_ref, lhs_ref, right_ref, res_ref) = refs
-        build_list(dims, lhs_ref.shape[1], (c0, c1, c2), fl, fl_lo, list_ref)
+        build_list(dims, fl, fl_lo, list_ref)
     else:
         (q0, q1, q2, c0, c1, c2, list_ref, f_ref, v_ref, b0, b2) = refs[:11]
         sum_refs = refs[11:-10]
@@ -308,19 +292,24 @@
             [jnp.concatenate([one, side], axis=1), jnp.concatenate([side, one], axis=1)], axis=0
         )
 
-    def left_of(tiles):
-        return jnp.concatenate([load_tile(lhs_ref, t) for t in tiles], axis=1)
-
-    def work(tiles, value, acc):
-        for r in range(TILE // 8):
+    quarter = slots // 4
+
+    def left_of(entry, m):
+        start = m * 2 * quarter
+        return jnp.concatenate(
+            [lhs_ref[entry, start + h * quarter : start + (h + 1) * quarter, :] for h in range(2)], axis=1
+        )
+
+    def work(entry, m, value, acc):
+        for r in range(quarter // 8):
             for h in range(2):
                 t = jnp.maximum(value[r * 8 : r * 8 + 8, h * slots : (h + 1) * slots], 0.0)
-                acc[r] = acc[r] + t * t * t
+                acc[r % 4] = acc[r % 4] + t * t * t
 
     def emit(cell, acc):
         res_ref[cell] = (acc[0] + acc[1]) + (acc[2] + acc[3])
 
-    run_items(dims, slots, list_ref, GROUP, 2, 4, right_of, left_of, work, emit)
+    run_items(dims, slots, list_ref, GROUP, quarter, 4, right_of, left_of, work, emit)
     lane = lax.broadcasted_iota(jnp.int32, (1, slots), 1)
     for p in range(planes):
 
@@ -339,11 +328,6 @@
         lax.fori_loop(0, gy, row, 0)
 
 
-def load_tile(ref, index):
-    per = ref.shape[1] // TILE
-    return ref[index // per, pl.ds(pl.multiple_of((index % per) * TILE, TILE), TILE), :]
-
-
 def build_rights(dims, pos, cnt, emb, right_ref):
     planes, gy, gz = dims
     for p in range(planes):
@@ -360,10 +344,10 @@
         lax.fori_loop(0, gy, row, 0)
 
 
-def run_items(dims, slots, list_ref, group, width, chains, right_of, left_of, work, emit):
-    head, items, _ = list_sizes(dims, slots)
-    tiles_at = head + items
-    turns = ITEM // (2 * width)
+def run_items(dims, slots, list_ref, group, height, chains, right_of, left_of, work, emit):
+    head, items, _ = list_sizes(dims)
+    entries = head + items
+    turns = ITEM
 
     def inner(*flat):
         accs = [
@@ -371,8 +355,8 @@
             for i in range(group)
         ]
 
-        def tile_ids(item, m, t):
-            return [list_ref[tiles_at + item * ITEM + (t * 2 + m) * width + w] for w in range(width)]
+        def entry_of(item, t):
+            return list_ref[entries + item * ITEM + t]
 
         def load_right(item):
             right = right_of(list_ref[head + item])
@@ -382,7 +366,7 @@
         def send(item, i, m, t):
             pltpu.matmul_acc_lhs(
                 accs[i][m][t],
-                left_of(tile_ids(item, m, t)),
+                left_of(entry_of(item, t), m),
                 load_staged_rhs=0 if t == 0 else None,
             )
 
@@ -405,7 +389,7 @@
                     for m in range(2):
                         value = pltpu.matmul_pop(accs[i][m][t])
                         send(item + group, i, m, t)
-                        work(tile_ids(item, m, t), value, acc)
+                        work(entry_of(item, t), m, value, acc)
                 emit(cell, acc)
             return tuple(acc)
 
@@ -419,7 +403,7 @@
     pl.run_scoped(
         inner,
         *[
-            pltpu.ACC(m)((TILE, 2 * slots), F32)
+            pltpu.ACC(m)((height, 2 * slots), F32)
             for _ in range(group)
             for m in range(2)
             for _ in range(turns)
@@ -428,44 +412,43 @@
 
 
 def force_kernel(dims, *refs):
-    (p0, p1, p2, c0, c1, c2, e0, e1, e2, vel, list_ref, table_ref) = refs[:12]
-    (f_ref, v_ref, s_ref) = refs[12:15]
-    edges = refs[15:-6]
-    (lhs_ref, right_ref, res_ref, *wide_refs) = refs[-6:]
+    (p0, p1, p2, c0, c1, c2, e0, e1, e2, vel, list_ref) = refs[:11]
+    (f_ref, v_ref, s_ref) = refs[11:14]
+    edges = refs[14:-4]
+    (lhs_ref, right_ref, res_ref, wide_ref) = refs[-4:]
     planes, gy, gz = dims
     slots = lhs_ref.shape[1]
     pl.run_scoped(
-        functools.partial(build_partners, dims, (p0, p1, p2), (c0, c1, c2), (e0, e1, e2), lhs_ref, wide_refs),
-        *[pltpu.ACC(m)((slots, 2 * slots), F32) for m in range(2) for _ in range(gz + 2 * m)],
+        functools.partial(build_partners, dims, (p0, p1, p2), (c0, c1, c2), (e0, e1, e2), lhs_ref, wide_ref),
+        *[pltpu.ACC(0)((slots, 2 * slots), F32) for _ in range(gz)],
+        *[pltpu.ACC(1)((slots // 2, 2 * slots), F32) for _ in range(gz + 2)],
     )
     build_rights(dims, p1, c1, e1, right_ref)
     gap = jnp.zeros((2 * slots - KDIM, 2 * slots), BF)
-    side = jnp.zeros((TILE, slots), BF)
+    half = slots // 2
+    side = jnp.zeros((half, slots), BF)
 
     def right_of(cell):
         return jnp.concatenate([right_ref[cell], gap], axis=0)
 
-    def left_of(tiles):
-        return jnp.concatenate([load_tile(lhs_ref, tiles[0]), side], axis=1)
-
-    def work(tiles, value, acc):
-        where = table_ref[tiles[0]]
-        spots = (where & 1023, (where >> 10) & 1023, where >> 20)
-        wides = [load_tile(ref, spot) for ref, spot in zip(wide_refs, spots)]
-        for r in range(TILE // 8):
+    def left_of(entry, m):
+        return jnp.concatenate([lhs_ref[entry, m * half : (m + 1) * half, :], side], axis=1)
+
+    def work(entry, m, value, acc):
+        for r in range(half // 8):
             here = slice(r * 8, r * 8 + 8)
             t = jnp.maximum(value[here, :slots], 0.0)
             g = t * t * value[here, slots:]
-            half = (r % 2) * 4
-            acc[half] = acc[half] + g
+            at = (r % 2) * 4
+            acc[at] = acc[at] + g
             for k in range(3):
-                acc[half + 1 + k] = acc[half + 1 + k] + g * wides[k][here]
+                acc[at + 1 + k] = acc[at + 1 + k] + g * wide_ref[entry, k, m * half + r * 8 : m * half + r * 8 + 8, :]
 
     def emit(cell, acc):
         for k in range(4):
             res_ref[cell, k] = acc[k] + acc[k + 4]
 
-    run_items(dims, slots, list_ref, 2, 1, 8, right_of, left_of, work, emit)
+    run_items(dims, slots, list_ref, 2, half, 8, right_of, left_of, work, emit)
     lane = lax.broadcasted_iota(jnp.int32, (1, slots), 1)
     sums = (jnp.zeros((1, slots), F32), jnp.zeros((1, slots), F32))
     for p in range(planes):
@@ -552,8 +535,7 @@
     smem = pl.BlockSpec(memory_space=pltpu.SMEM)
     ext = (planes + 2) * (gy + 2) * (gz + 2) + 1
     cells = planes * gy * gz
-    entries = list_sizes(dims, slots)[2]
-    table = jnp.asarray(wide_table(dims, slots))
+    entries = list_sizes(dims)[2]
     pairs = planes * gy * gz * 27 * slots * slots
 
     def shaped(*shape):
@@ -574,9 +556,7 @@
         lhs_scratch,
         pltpu.VMEM((cells, KDIM, 2 * slots), BF),
         pltpu.VMEM((cells, 4, 8, slots), F32),
-        pltpu.VMEM(((planes + 2) * gy * gz, slots, slots), F32),
-        pltpu.VMEM(((planes + 2) * (gy + 2) * gz, slots, slots), F32),
-        pltpu.VMEM(((planes + 2) * gy * (gz + 2), slots, slots), F32),
+        pltpu.VMEM((ext, 3, slots, slots), F32),
     ]
     emb_shape = [shaped(planes, gy, gz, slots), shaped(1, gy, gz, slots), shaped(1, gy, gz, slots)]
     vec, edge = shaped(3, planes, gy, gz, slots), shaped(3, 1, gy, gz, slots)
@@ -633,13 +613,13 @@
         forces, pushed, part, *edges = pl.pallas_call(
             functools.partial(force_kernel, dims),
             out_shape=(vec, vec, shaped(8, slots), *(() if last else (pack, pack))),
-            in_specs=specs + [vmem] * 4 + [smem] * 2,
+            in_specs=specs + [vmem] * 4 + [smem],
             out_specs=(vmem,) * (3 if last else 5),
             scratch_shapes=scratch_f,
-            compiler_params=pltpu.CompilerParams(vmem_limit_bytes=34 * 2**20),
+            compiler_params=pltpu.CompilerParams(vmem_limit_bytes=42 * 2**20),
             cost_estimate=cost_f,
             name="force",
-        )(*args, emb_lo, emb, emb_hi, motion, blocks, table)
+        )(*args, emb_lo, emb, emb_hi, motion, blocks)
         sums = [part] + [lax.ppermute(part, "space", ring("space", s)) for s in range(1, space)]
         if not last:
             packs = halo(*edges)

time: 247 us -> 130 us (0.53)
  Pallas kernels: 208 us -> 93.3 us
    pallas_call x2, Pallas kernels: 144 us -> 54 us  [body(): pl.pallas_call(functools.partial(force_kernel, dims), out_shape=(vec, vec...]
    pallas_call x1, Pallas kernels: 36.8 us -> 21.1 us  [body(): pl.pallas_call(functools.partial(density_kernel, dims, True), out_shape=(...]
    pallas_call x1, Pallas kernels: 25.8 us -> 16.8 us  [body(): pl.pallas_call(functools.partial(density_kernel, dims, False), out_shape=...]
  transfers between devices with their start and end apart: 21 -> 21, of which waited for: 11 -> 11; matrix products, arithmetic and copies ran while one was open for 0% -> 0% of each run, Pallas kernels for 40% -> 34%
where the time goes in v4:
time: 130 us
  Pallas kernels  93.3 us (72%)
  starting transfers between devices  21.8 us (17%)
  waiting for transfers between devices  12 us (9%)
  local copies, waits for them, and re-layouts  1.7 us (1%)
    pallas_call x2, Pallas kernels, body(): pl.pallas_call(functools.partial(force_kernel, dims), out_shape=(vec, vec...  54 us
    pallas_call x1, Pallas kernels, body(): pl.pallas_call(functools.partial(density_kernel, dims, True), out_shape=(...  21.1 us
    pallas_call x1, Pallas kernels, body(): pl.pallas_call(functools.partial(density_kernel, dims, False), out_shape=...  16.8 us
    ppermute x10, starting transfers between devices, halo(): return (lax.ppermute(last, 'space', up), lax.ppermute(first, 'space', down))  9.68 us
    ppermute x4, starting transfers between devices, hop(): options.append(lax.ppermute(held, 'rep', pairs))  6.31 us
    ppermute x6, waiting for transfers between devices, body(): lax.ppermute(part, 'space', ring('space', s))  5.29 us
    ppermute x6, starting transfers between devices, body(): lax.ppermute(part, 'space', ring('space', s))  4.4 us
    ppermute x10, waiting for transfers between devices, halo(): return (lax.ppermute(last, 'space', up), lax.ppermute(first, 'space', down))  3.9 us
  transfers between devices with their start and end apart: 21, of which 11 were waited for; matrix products, arithmetic and copies ran while one was open for 0% of the time, Pallas kernels for 34%

profile of v4, /device:TPU:0, one launch (start us, length us, event | category | flops | bytes accessed | tf_op | source)
XLA Modules:
  0.0 129.8 jit_solution(10122346869752439593)
XLA Ops:
  0.6 0.8 fusion
  1.4 0.5 collective-permute-start
  1.9 2.0 %collective-permute-start.1 = (f32[3,1,4,4,128]{4,3,2,1,0:T(4,128)S(1)}, f32[3,1,4,4,128]{4,3,2,1,0:T(4,128)S(1)}, u32[]{:S(2)}, u32[]{:S(2)}) collective-permute-start(f32[3,1,4,4,128]{4,3,2,1,0:T(4,128)S(1)} %get-tuple-element.50), channel_id=1, source_target_pairs={{0,3},{1,0},{2,1},{3,2},{4,7},{5,4},{6,5},{7,6},{8,11},{9,8},{10,9... | collective-permute-start | bytes 73736 | tf_op jit(solution)/shard_map/ppermute | solution.py:548
  4.0 1.4 %collective-permute-start.4 = (s32[13,1,4,4]{3,2,1,0:T(4,128)S(1)}, s32[13,1,4,4]{3,2,1,0:T(4,128)S(1)}, u32[]{:S(2)}, u32[]{:S(2)}) collective-permute-start(s32[13,1,4,4]{3,2,1,0:T(4,128)S(1)} %copy.10), channel_id=1, source_target_pairs={{0,1},{1,2},{2,3},{3,0},{4,5},{5,6},{6,7},{7,4},{8,9},{9,10},{10,1... | collective-permute-start | bytes 2504 | tf_op jit(solution)/shard_map/ppermute | solution.py:550
  5.4 1.1 collective-permute-start.2
  6.4 0.7 collective-permute-start.3
  7.3 1.1 collective-permute-done.2.refs_3_
  8.5 21.1 %density_first.1 = (f32[2,4,4,128]{3,2,1,0:T(4,128)S(1)}, f32[1,4,4,128]{3,2,1,0:T(4,128)S(1)}, f32[1,4,4,128]{3,2,1,0:T(4,128)S(1)}, s32[1198]{0:T(1024)S(1)}) custom-call(f32[3,1,4,4,128]{4,3,2,1,0:T(4,128)S(1)} %collective-permute-done.refs_0_, f32[3,2,4,4,128]{4,3,2,1,0:T(4,128)S(1)} %bitcast.11, ...), custom_call_target="tpu_custom_call" | custom-call | flops 141557760 | bytes 1048576 | tf_op jit(solution)/shard_map/density_first/pallas_call | solution.py:589
  29.5 1.8 %collective-permute-start.5 = (f32[1,4,4,128]{3,2,1,0:T(4,128)S(1)}, f32[1,4,4,128]{3,2,1,0:T(4,128)S(1)}, u32[]{:S(2)}, u32[]{:S(2)}) collective-permute-start(f32[1,4,4,128]{3,2,1,0:T(4,128)S(1)} %get-tuple-element.28), channel_id=1, source_target_pairs={{0,1},{1,2},{2,3},{3,0},{4,5},{5,6},{6,7},{7,4},{8,9},{9,10},{10,1... | collective-permute-start | bytes 24584 | tf_op jit(solution)/shard_map/ppermute | solution.py:548
  31.3 1.3 %collective-permute-done.5.refs_6_ = f32[1,4,4,128]{3,2,1,0:T(4,128)S(1)} collective-permute-done((f32[1,4,4,128]{3,2,1,0:T(4,128)S(1)}, f32[1,4,4,128]{3,2,1,0:T(4,128)S(1)}, u32[]{:S(2)}, u32[]{:S(2)}) %collective-permute-start.5) | collective-permute-done | bytes 8224 | tf_op jit(solution)/shard_map/ppermute | solution.py:548
  32.7 27.0 %force.2 = (f32[3,2,4,4,128]{4,3,2,1,0:T(4,128)S(1)}, f32[3,2,4,4,128]{4,3,2,1,0:T(4,128)S(1)}, f32[8,128]{1,0:T(8,128)S(1)}, f32[6,1,4,4,128]{4,3,2,1,0:T(4,128)S(1)}, f32[6,1,4,4,128]{4,3,2,1,0:T(4,128)S(1)}) custom-call(f32[3,1,4,4,128]{4,3,2,1,0:T(4,128)S(1)} %collective-permute-done.refs_0_, f32[3,2,4,4,128]{4,3,2,1,0:T(4,128)S(1)} %bitcast.12, ...), custom_call_target="tpu_custom_call" | custom-call | flops 353894400 | bytes 1048576 | tf_op jit(solution)/shard_map/force/pallas_call | solution.py:613
  59.8 2.6 %collective-permute-start.14 = (f32[6,2,4,4,128]{4,3,2,1,0:T(4,128)S(1)}, f32[6,2,4,4,128]{4,3,2,1,0:T(4,128)S(1)}, u32[]{:S(2)}, u32[]{:S(2)}) collective-permute-start(f32[6,2,4,4,128]{4,3,2,1,0:T(4,128)S(1)} %pad_maximum_fusion), channel_id=1, source_target_pairs={{0,12},{4,0},{8,4},{12,8},{16,28},{20,16},{24,20},{28,24},{1,13},{... | collective-permute-start | bytes 294920 | tf_op jit(solution)/shard_map/ppermute | solution.py:580
  62.3 0.5 collective-permute-start.15
  62.8 0.7 collective-permute-start.16
  63.4 0.7 copy-done.5
  64.2 1.3 collective-permute-start.7
  65.5 0.5 collective-permute-start.8
  66.0 1.9 %collective-permute-done.15 = f32[6,2,4,4,128]{4,3,2,1,0:T(4,128)S(1)} collective-permute-done((f32[6,2,4,4,128]{4,3,2,1,0:T(4,128)S(1)}, f32[6,2,4,4,128]{4,3,2,1,0:T(4,128)S(1)}, u32[]{:S(2)}, u32[]{:S(2)}) %collective-permute-start.15) | collective-permute-done | bytes 98336 | tf_op jit(solution)/shard_map/ppermute | solution.py:580
  68.0 0.8 collective-permute-done.16
  68.9 2.6 %collective-permute-start.17 = (f32[6,2,4,4,128]{4,3,2,1,0:T(4,128)S(1)}, f32[6,2,4,4,128]{4,3,2,1,0:T(4,128)S(1)}, u32[]{:S(2)}, u32[]{:S(2)}) collective-permute-start(f32[6,2,4,4,128]{4,3,2,1,0:T(4,128)S(1)} %select_select_fusion.refs_6_), channel_id=1, source_target_pairs={{0,16},{4,20},{8,24},{12,28},{16,0},{20,4},{24,8},{28,12},{1,17},{... | collective-permute-start | bytes 294920 | tf_op jit(solution)/shard_map/ppermute | solution.py:580
  71.6 1.1 collective-permute-start.10
  72.7 1.9 %collective-permute-done.9.refs_12_ = f32[8,128]{1,0:T(8,128)S(1)} collective-permute-done((f32[8,128]{1,0:T(8,128)S(1)}, f32[8,128]{1,0:T(8,128)S(1)}, u32[]{:S(2)}, u32[]{:S(2)}) %collective-permute-start.9) | collective-permute-done | bytes 4128 | tf_op jit(solution)/shard_map/ppermute | solution.py:623
  74.6 0.7 collective-permute-done.10.refs_13_
  75.2 0.7 collective-permute-done.11.refs_14_
  75.9 16.8 %density_next.1 = (f32[2,4,4,128]{3,2,1,0:T(4,128)S(1)}, f32[1,4,4,128]{3,2,1,0:T(4,128)S(1)}, f32[1,4,4,128]{3,2,1,0:T(4,128)S(1)}, f32[3,1,4,4,128]{4,3,2,1,0:...) custom-call(f32[3,1,4,4,128]{4,3,2,1,0:T(4,128)S(1)} %collective-per, ...), custom_call_target="tpu_custom_call" | custom-call | flops 141557760 | bytes 1048576 | tf_op jit(solution)/shard_map/density_next/pallas_call | solution.py:600
  92.7 1.5 %collective-permute-start.12 = (f32[1,4,4,128]{3,2,1,0:T(4,128)S(1)}, f32[1,4,4,128]{3,2,1,0:T(4,128)S(1)}, u32[]{:S(2)}, u32[]{:S(2)}) collective-permute-start(f32[1,4,4,128]{3,2,1,0:T(4,128)S(1)} %get-tuple-element.39), channel_id=1, source_target_pairs={{0,1},{1,2},{2,3},{3,0},{4,5},{5,6},{6,7},{7,4},{8,9},{9,10},{10,1... | collective-permute-start | bytes 24584 | tf_op jit(solution)/shard_map/ppermute | solution.py:548
  94.6 1.3 collective-permute-done.12.refs_6_
  95.9 27.0 %force.3 = (f32[3,2,4,4,128]{4,3,2,1,0:T(4,128)S(1)}, f32[3,2,4,4,128]{4,3,2,1,0:T(4,128)S(1)}, f32[8,128]{1,0:T(8,128)S(1)}) custom-call(f32[3,1,4,4,128]{4,3,2,1,0:T(4,128)S(1)} %get-tuple-element.37.refs_0_, f32[3,2,4,4,128]{4,3,2,1,0:T(4,128)S(1)} %get-tuple-element.36.refs_1_.refs_0_, f32[3,1,4,4,128]{4,3,2,1,0:T(4,128)S(1)} %get-tuple-element.38.refs_2_, ...), custom_call_target="tpu_custom_call" | custom-call | flops 353894400 | bytes 1048576 | tf_op jit(solution)/shard_map/force/pallas_call | solution.py:613
  123.0 1.8 %collective-permute-start.18 = (f32[8,128]{1,0:T(8,128)S(1)}, f32[8,128]{1,0:T(8,128)S(1)}, u32[]{:S(2)}, u32[]{:S(2)}) collective-permute-start(f32[8,128]{1,0:T(8,128)S(1)} %get-tuple-element.45.refs_8_), channel_id=1, source_target_pairs={{0,1},{1,2},{2,3},{3,0},{4,5},{5,6},{6,7},{7,4},{8,9},{9,10},{10,1... | collective-permute-start | bytes 12296 | tf_op jit(solution)/shard_map/ppermute | solution.py:623
  125.1 1.1 collective-permute-start.20
  126.3 2.1 %collective-permute-done.19.refs_10_ = f32[8,128]{1,0:T(8,128)S(1)} collective-permute-done((f32[8,128]{1,0:T(8,128)S(1)}, f32[8,128]{1,0:T(8,128)S(1)}, u32[]{:S(2)}, u32[]{:S(2)}) %collective-permute-start.19) | collective-permute-done | bytes 4128 | tf_op jit(solution)/shard_map/ppermute | solution.py:623
  128.4 1.4 %finish.1 = (f32[3,2,4,4,128]{4,3,2,1,0:T(4,128)}, f32[3,2,4,4,128]{4,3,2,1,0:T(4,128)}, f32[3,2,4,4,128]{4,3,2,1,0:T(4,128)}, f32[3,2,4,4,128]{4,3,2,1,0:T(4,128)}) custom-call(f32[3,2,4,4,128]{4,3,2,1,0:T(4,128)S(1)} %get-tuple-element.36.refs_1_.refs_0_, f32[3,2,4,4,128]{4,3,2,1,0:T(4,128)S(1)} %get-tuple-element.43.refs_1_, ...), custom_call_target="tpu_custom_call" | custom-call | tf_op jit(solution)/shard_map/finish/pallas_call | solution.py:635
  (35 shorter events, 1.4 us)
Async XLA Ops:
  1.4 7.0 %collective-permute-start = (f32[3,1,4,4,128]{4,3,2,1,0:T(4,128)S(1)}, f32[3,1,4,4,128]{4,3,2,1,0:T(4,128)S(1)}, u32[]{:S(2)}, u32[]{:S(2)}) collective-permute-start(f32[3,1,4,4,128]{4,3,2,1,0:T(4,128)S(1)} %get-tuple-element.51), channel_id=1, source_target_pairs={{0,1},{1,2},{2,3},{3,0},{4,5},{5,6},{6,7},{7,4},{8,9},{9,10},{10,1... | collective-permute-start | bytes 73736 | tf_op jit(solution)/shard_map/ppermute | solution.py:548
  1.9 2.0 %slice-start = ((s32[13,2,4,4]{0,3,2,1:T(4,128)}), s32[13,1,4,4]{0,3,2,1:T(4,128)S(1)}, s32[]{:S(2)}) async-start(s32[13,2,4,4]{0,3,2,1:T(4,128)} %param.10), calls=%async_computation | async-start | bytes 16384 | tf_op jit(solution)/shard_map/slice | solution.py:550
  1.9 6.6 %collective-permute-start.1 = (f32[3,1,4,4,128]{4,3,2,1,0:T(4,128)S(1)}, f32[3,1,4,4,128]{4,3,2,1,0:T(4,128)S(1)}, u32[]{:S(2)}, u32[]{:S(2)}) collective-permute-start(f32[3,1,4,4,128]{4,3,2,1,0:T(4,128)S(1)} %get-tuple-element.50), channel_id=1, source_target_pairs={{0,3},{1,0},{2,1},{3,2},{4,7},{5,4},{6,5},{7,6},{8,11},{9,8},{10,9... | collective-permute-start | bytes 73736 | tf_op jit(solution)/shard_map/ppermute | solution.py:548
  3.9 1.5 %copy-start.2 = (s32[2,4,4]{2,1,0:T(4,128)S(1)}, s32[2,4,4]{2,1,0:T(4,128)}, u32[]{:S(2)}) copy-start(s32[2,4,4]{2,1,0:T(4,128)} %refs_4_.9) | copy-start | bytes 388
  3.9 3.2 %copy-start.4 = (s32[13,2,4,4]{0,3,2,1:T(4,128)S(1)}, s32[13,2,4,4]{0,3,2,1:T(4,128)}, u32[]{:S(2)}) copy-start(s32[13,2,4,4]{0,3,2,1:T(4,128)} %param.10) | copy-start | bytes 4996
  4.0 4.4 %copy-start = (f32[1,3,2,4,4,128]{5,4,3,2,1,0:T(4,128)S(1)}, f32[1,3,2,4,4,128]{5,4,3,2,1,0:T(4,128)}, u32[]{:S(2)}) copy-start(f32[1,3,2,4,4,128]{5,4,3,2,1,0:T(4,128)} %param.6) | copy-start | bytes 147460
  4.0 4.4 %collective-permute-start.4 = (s32[13,1,4,4]{3,2,1,0:T(4,128)S(1)}, s32[13,1,4,4]{3,2,1,0:T(4,128)S(1)}, u32[]{:S(2)}, u32[]{:S(2)}) collective-permute-start(s32[13,1,4,4]{3,2,1,0:T(4,128)S(1)} %copy.10), channel_id=1, source_target_pairs={{0,1},{1,2},{2,3},{3,0},{4,5},{5,6},{6,7},{7,4},{8,9},{9,10},{10,1... | collective-permute-start | bytes 2504 | tf_op jit(solution)/shard_map/ppermute | solution.py:550
  5.4 3.0 %collective-permute-start.2 = (s32[1,4,4]{2,1,0:T(4,128)S(1)}, s32[1,4,4]{2,1,0:T(4,128)S(1)}, u32[]{:S(2)}, u32[]{:S(2)}) collective-permute-start(s32[1,4,4]{2,1,0:T(4,128)S(1)} %get-tuple-element.53), channel_id=1, source_target_pairs={{0,1},{1,2},{2,3},{3,0},{4,5},{5,6},{6,7},{7,4},{8,9},{9,10},{10,1... | collective-permute-start | bytes 200 | tf_op jit(solution)/shard_map/ppermute | solution.py:548
  6.4 2.0 %collective-permute-start.3 = (s32[1,4,4]{2,1,0:T(4,128)S(1)}, s32[1,4,4]{2,1,0:T(4,128)S(1)}, u32[]{:S(2)}, u32[]{:S(2)}) collective-permute-start(s32[1,4,4]{2,1,0:T(4,128)S(1)} %get-tuple-element.52), channel_id=1, source_target_pairs={{0,3},{1,0},{2,1},{3,2},{4,7},{5,4},{6,5},{7,6},{8,11},{9,8},{10,9... | collective-permute-start | bytes 200 | tf_op jit(solution)/shard_map/ppermute | solution.py:548
  7.3 25.4 %copy-start.3 = (f32[1,3,2,4,4,128]{5,4,3,2,1,0:T(4,128)S(1)}, f32[1,3,2,4,4,128]{5,4,3,2,1,0:T(4,128)}, u32[]{:S(2)}) copy-start(f32[1,3,2,4,4,128]{5,4,3,2,1,0:T(4,128)} %param.7) | copy-start | bytes 147460
  29.5 3.1 %collective-permute-start.5 = (f32[1,4,4,128]{3,2,1,0:T(4,128)S(1)}, f32[1,4,4,128]{3,2,1,0:T(4,128)S(1)}, u32[]{:S(2)}, u32[]{:S(2)}) collective-permute-start(f32[1,4,4,128]{3,2,1,0:T(4,128)S(1)} %get-tuple-element.28), channel_id=1, source_target_pairs={{0,1},{1,2},{2,3},{3,0},{4,5},{5,6},{6,7},{7,4},{8,9},{9,10},{10,1... | collective-permute-start | bytes 24584 | tf_op jit(solution)/shard_map/ppermute | solution.py:548
  31.3 1.4 %collective-permute-start.6 = (f32[1,4,4,128]{3,2,1,0:T(4,128)S(1)}, f32[1,4,4,128]{3,2,1,0:T(4,128)S(1)}, u32[]{:S(2)}, u32[]{:S(2)}) collective-permute-start(f32[1,4,4,128]{3,2,1,0:T(4,128)S(1)} %get-tuple-element.30), channel_id=1, source_target_pairs={{0,3},{1,0},{2,1},{3,2},{4,7},{5,4},{6,5},{7,6},{8,11},{9,8},{10,9... | collective-permute-start | bytes 24584 | tf_op jit(solution)/shard_map/ppermute | solution.py:548
  59.8 6.3 %collective-permute-start.14 = (f32[6,2,4,4,128]{4,3,2,1,0:T(4,128)S(1)}, f32[6,2,4,4,128]{4,3,2,1,0:T(4,128)S(1)}, u32[]{:S(2)}, u32[]{:S(2)}) collective-permute-start(f32[6,2,4,4,128]{4,3,2,1,0:T(4,128)S(1)} %pad_maximum_fusion), channel_id=1, source_target_pairs={{0,12},{4,0},{8,4},{12,8},{16,28},{20,16},{24,20},{28,24},{1,13},{... | collective-permute-start | bytes 294920 | tf_op jit(solution)/shard_map/ppermute | solution.py:580
  62.3 5.7 %collective-permute-start.15 = (f32[6,2,4,4,128]{4,3,2,1,0:T(4,128)S(1)}, f32[6,2,4,4,128]{4,3,2,1,0:T(4,128)S(1)}, u32[]{:S(2)}, u32[]{:S(2)}) collective-permute-start(f32[6,2,4,4,128]{4,3,2,1,0:T(4,128)S(1)} %pad_maximum_fusion), channel_id=1, source_target_pairs={{0,8},{4,12},{8,0},{12,4},{16,24},{20,28},{24,16},{28,20},{1,9},{5... | collective-permute-start | bytes 294920 | tf_op jit(solution)/shard_map/ppermute | solution.py:580
  62.8 6.0 %collective-permute-start.16 = (f32[6,2,4,4,128]{4,3,2,1,0:T(4,128)S(1)}, f32[6,2,4,4,128]{4,3,2,1,0:T(4,128)S(1)}, u32[]{:S(2)}, u32[]{:S(2)}) collective-permute-start(f32[6,2,4,4,128]{4,3,2,1,0:T(4,128)S(1)} %pad_maximum_fusion), channel_id=1, source_target_pairs={{0,4},{4,8},{8,12},{12,0},{16,20},{20,24},{24,28},{28,16},{1,5},{5... | collective-permute-start | bytes 294920 | tf_op jit(solution)/shard_map/ppermute | solution.py:580
  63.4 0.7 copy-start.5
  64.2 11.7 %collective-permute-start.7 = (f32[6,1,4,4,128]{4,3,2,1,0:T(4,128)S(1)}, f32[6,1,4,4,128]{4,3,2,1,0:T(4,128)S(1)}, u32[]{:S(2)}, u32[]{:S(2)}) collective-permute-start(f32[6,1,4,4,128]{4,3,2,1,0:T(4,128)S(1)} %get-tuple-element.33), channel_id=1, source_target_pairs={{0,1},{1,2},{2,3},{3,0},{4,5},{5,6},{6,7},{7,4},{8,9},{9,10},{10,1... | collective-permute-start | bytes 147464 | tf_op jit(solution)/shard_map/ppermute | solution.py:548
  65.5 10.4 %collective-permute-start.8 = (f32[6,1,4,4,128]{4,3,2,1,0:T(4,128)S(1)}, f32[6,1,4,4,128]{4,3,2,1,0:T(4,128)S(1)}, u32[]{:S(2)}, u32[]{:S(2)}) collective-permute-start(f32[6,1,4,4,128]{4,3,2,1,0:T(4,128)S(1)} %get-tuple-element.34), channel_id=1, source_target_pairs={{0,3},{1,0},{2,1},{3,2},{4,7},{5,4},{6,5},{7,6},{8,11},{9,8},{10,9... | collective-permute-start | bytes 147464 | tf_op jit(solution)/shard_map/ppermute | solution.py:548
  68.9 59.5 %collective-permute-start.17 = (f32[6,2,4,4,128]{4,3,2,1,0:T(4,128)S(1)}, f32[6,2,4,4,128]{4,3,2,1,0:T(4,128)S(1)}, u32[]{:S(2)}, u32[]{:S(2)}) collective-permute-start(f32[6,2,4,4,128]{4,3,2,1,0:T(4,128)S(1)} %select_select_fusion.refs_6_), channel_id=1, source_target_pairs={{0,16},{4,20},{8,24},{12,28},{16,0},{20,4},{24,8},{28,12},{1,17},{... | collective-permute-start | bytes 294920 | tf_op jit(solution)/shard_map/ppermute | solution.py:580
  71.5 3.0 %collective-permute-start.9 = (f32[8,128]{1,0:T(8,128)S(1)}, f32[8,128]{1,0:T(8,128)S(1)}, u32[]{:S(2)}, u32[]{:S(2)}) collective-permute-start(f32[8,128]{1,0:T(8,128)S(1)} %get-tuple-element.35.refs_11_), channel_id=1, source_target_pairs={{0,1},{1,2},{2,3},{3,0},{4,5},{5,6},{6,7},{7,4},{8,9},{9,10},{10,1... | collective-permute-start | bytes 12296 | tf_op jit(solution)/shard_map/ppermute | solution.py:623
  71.6 3.6 %collective-permute-start.10 = (f32[8,128]{1,0:T(8,128)S(1)}, f32[8,128]{1,0:T(8,128)S(1)}, u32[]{:S(2)}, u32[]{:S(2)}) collective-permute-start(f32[8,128]{1,0:T(8,128)S(1)} %get-tuple-element.35.refs_11_), channel_id=1, source_target_pairs={{0,2},{1,3},{2,0},{3,1},{4,6},{5,7},{6,4},{7,5},{8,10},{9,11},{10,... | collective-permute-start | bytes 12296 | tf_op jit(solution)/shard_map/ppermute | solution.py:623
  74.6 1.3 %collective-permute-start.11 = (f32[8,128]{1,0:T(8,128)S(1)}, f32[8,128]{1,0:T(8,128)S(1)}, u32[]{:S(2)}, u32[]{:S(2)}) collective-permute-start(f32[8,128]{1,0:T(8,128)S(1)} %get-tuple-element.35.refs_11_), channel_id=1, source_target_pairs={{0,3},{1,0},{2,1},{3,2},{4,7},{5,4},{6,5},{7,6},{8,11},{9,8},{10,9... | collective-permute-start | bytes 12296 | tf_op jit(solution)/shard_map/ppermute | solution.py:623
  92.7 3.1 %collective-permute-start.12 = (f32[1,4,4,128]{3,2,1,0:T(4,128)S(1)}, f32[1,4,4,128]{3,2,1,0:T(4,128)S(1)}, u32[]{:S(2)}, u32[]{:S(2)}) collective-permute-start(f32[1,4,4,128]{3,2,1,0:T(4,128)S(1)} %get-tuple-element.39), channel_id=1, source_target_pairs={{0,1},{1,2},{2,3},{3,0},{4,5},{5,6},{6,7},{7,4},{8,9},{9,10},{10,1... | collective-permute-start | bytes 24584 | tf_op jit(solution)/shard_map/ppermute | solution.py:548
  94.2 1.7 %collective-permute-start.13 = (f32[1,4,4,128]{3,2,1,0:T(4,128)S(1)}, f32[1,4,4,128]{3,2,1,0:T(4,128)S(1)}, u32[]{:S(2)}, u32[]{:S(2)}) collective-permute-start(f32[1,4,4,128]{3,2,1,0:T(4,128)S(1)} %get-tuple-element.41), channel_id=1, source_target_pairs={{0,3},{1,0},{2,1},{3,2},{4,7},{5,4},{6,5},{7,6},{8,11},{9,8},{10,9... | collective-permute-start | bytes 24584 | tf_op jit(solution)/shard_map/ppermute | solution.py:548
  123.0 3.4 %collective-permute-start.18 = (f32[8,128]{1,0:T(8,128)S(1)}, f32[8,128]{1,0:T(8,128)S(1)}, u32[]{:S(2)}, u32[]{:S(2)}) collective-permute-start(f32[8,128]{1,0:T(8,128)S(1)} %get-tuple-element.45.refs_8_), channel_id=1, source_target_pairs={{0,1},{1,2},{2,3},{3,0},{4,5},{5,6},{6,7},{7,4},{8,9},{9,10},{10,1... | collective-permute-start | bytes 12296 | tf_op jit(solution)/shard_map/ppermute | solution.py:623
  124.8 3.6 %collective-permute-start.19 = (f32[8,128]{1,0:T(8,128)S(1)}, f32[8,128]{1,0:T(8,128)S(1)}, u32[]{:S(2)}, u32[]{:S(2)}) collective-permute-start(f32[8,128]{1,0:T(8,128)S(1)} %get-tuple-element.45.refs_8_), channel_id=1, source_target_pairs={{0,2},{1,3},{2,0},{3,1},{4,6},{5,7},{6,4},{7,5},{8,10},{9,11},{10,... | collective-permute-start | bytes 12296 | tf_op jit(solution)/shard_map/ppermute | solution.py:623
  125.1 3.3 %collective-permute-start.20 = (f32[8,128]{1,0:T(8,128)S(1)}, f32[8,128]{1,0:T(8,128)S(1)}, u32[]{:S(2)}, u32[]{:S(2)}) collective-permute-start(f32[8,128]{1,0:T(8,128)S(1)} %get-tuple-element.45.refs_8_), channel_id=1, source_target_pairs={{0,3},{1,0},{2,1},{3,2},{4,7},{5,4},{6,5},{7,6},{8,11},{9,8},{10,9... | collective-permute-start | bytes 12296 | tf_op jit(solution)/shard_map/ppermute | solution.py:623
  126.2 2.2 %copy-start.1 = (f32[1,1,3,2,4,4,128]{6,5,4,3,2,1,0:T(4,128)S(1)}, f32[1,1,3,2,4,4,128]{6,5,4,3,2,1,0:T(4,128)}, u32[]{:S(2)}) copy-start(f32[1,1,3,2,4,4,128]{6,5,4,3,2,1,0:T(4,128)} %param.8) | copy-start | bytes 147460

commit v5 on v4

--- a/solution.py
+++ b/solution.py
@@ -25,7 +25,8 @@
 BF = jnp.bfloat16
 F32 = jnp.float32
 KDIM = 64
-ITEM = 3
+TILE = 32
+ITEM = 12
 GROUP = 4
 
 
@@ -43,6 +44,12 @@
     return None
 
 
+def rows_of(cell, slots):
+    if isinstance(cell, int):
+        return pl.ds(cell * slots, slots)
+    return pl.ds(pl.multiple_of(cell * slots, slots), slots)
+
+
 def split3(value):
     high = value.astype(BF).astype(F32)
     rest = value - high
@@ -55,67 +62,83 @@
     return jnp.where(index >= size, index - size, index)
 
 
-def list_sizes(dims):
-    most = math.prod(dims) * -(-27 // ITEM)
+def list_sizes(dims, slots):
+    most = math.prod(dims) * -(-27 * (slots // TILE) // ITEM)
     head = 8
     return head, most + 2 * GROUP, head + (most + 2 * GROUP) * (ITEM + 1) + 2 * ITEM
 
 
-def build_list(dims, flags, flags_lo, list_ref):
+class ListBuilder:
+    def __init__(self, dims, slots, cnt, flags, flags_lo, list_ref, size_ref):
+        self.dims, self.slots, self.flags, self.flags_lo = dims, slots, flags, flags_lo
+        self.list_ref, self.size_ref = list_ref, size_ref
+        planes, gy, gz = dims
+        self.head, items, _ = list_sizes(dims, slots)
+        self.entries = self.head + items
+        self.dummy = (planes + 2) * (gy + 2) * (gz + 2) * slots
+        cells = [(p, z) for p in range(planes) for z in range(gz)]
+        self.shares = [cells[j :: planes + 2] for j in range(planes + 2)]
+        for j in range(planes + 2):
+            which, at = (0, 0) if j == 0 else ((2, 0) if j == planes + 1 else (1, j - 1))
+
+            def row(y, _):
+                for z in range(gz):
+                    size_ref[(j * gy + y) * gz + z] = (cnt[which][at, y, z] + (TILE - 1)) >> (
+                        TILE.bit_length() - 1
+                    )
+                return 0
+
+            lax.fori_loop(0, gy, row, 0)
+
+    def add_cell(self, p, y, z, item):
+        _, gy, gz = self.dims
+        ey, ez = gy + 2, gz + 2
+        at = self.entries + item * ITEM
+        for ox, oy, oz in OFFSETS:
+            ext = ((p + 1 + ox) * ey + (y + 1 + oy)) * ez + (z + 1 + oz)
+            jy, jz = wrap(y + oy, gy), (z + oz) % gz
+            number = self.size_ref[((p + 1 + ox) * gy + jy) * gz + jz]
+            for t in range(self.slots // TILE):
+                self.list_ref[at + t] = ext * self.slots + t * TILE
+            found = flag_of((ox, oy, oz))
+            if found is not None:
+                index, forward = found
+                if forward:
+                    flag = self.flags[index, p, y, z]
+                elif p + ox < 0:
+                    flag = self.flags_lo[index, 0, jy, jz]
+                else:
+                    flag = self.flags[index, p + ox, jy, jz]
+                number = number * flag
+            at = at + number
+        for t in range(ITEM):
+            self.list_ref[at + t] = self.dummy
+        for t in range(-(-27 * (self.slots // TILE) // ITEM)):
+            self.list_ref[self.head + item + t] = (p * gy + y) * gz + z
+        return lax.div(at - self.entries + (ITEM - 1), jnp.int32(ITEM))
+
+    def add_row(self, j, y, item):
+        for p, z in self.shares[j]:
+            item = self.add_cell(p, y, z, item)
+        return item
+
+    def close(self, item):
+        self.list_ref[0] = (item + (GROUP - 1)) // GROUP * GROUP
+        last = self.list_ref[self.head + item - 1]
+
+        def rest(i, _):
+            self.list_ref[self.head + item + i] = last
+            for t in range(ITEM):
+                self.list_ref[self.entries + (item + i) * ITEM + t] = self.dummy
+            return 0
+
+        lax.fori_loop(0, 2 * GROUP - 1, rest, 0)
+
+
+def build_partners(dims, pos, cnt, emb, lister, lhs_ref, wide_ref, *accs):
     planes, gy, gz = dims
     ey, ez = gy + 2, gz + 2
-    dummy = (planes + 2) * ey * ez
-    head, items, _ = list_sizes(dims)
-    entries = head + items
-    bound = -(-27 // ITEM)
-
-    def cell_list(p, y, z, item):
-        at = item * ITEM
-        for ox, oy, oz in OFFSETS:
-            list_ref[entries + at] = ((p + 1 + ox) * ey + (y + 1 + oy)) * ez + (z + 1 + oz)
-            found = flag_of((ox, oy, oz))
-            if found is None:
-                at = at + 1
-                continue
-            index, forward = found
-            jy, jz = wrap(y + oy, gy), (z + oz) % gz
-            if forward:
-                flag = flags[index, p, y, z]
-            elif p + ox < 0:
-                flag = flags_lo[index, 0, jy, jz]
-            else:
-                flag = flags[index, p + ox, jy, jz]
-            at = at + flag
-        for t in range(ITEM):
-            list_ref[entries + at + t] = dummy
-        for t in range(bound):
-            list_ref[head + item + t] = (p * gy + y) * gz + z
-        return (at + (ITEM - 1)) // ITEM
-
-    item = 0
-    for p in range(planes):
-
-        def row(y, item):
-            for z in range(gz):
-                item = cell_list(p, y, z, item)
-            return item
-
-        item = lax.fori_loop(0, gy, row, item)
-    list_ref[0] = (item + (GROUP - 1)) // GROUP * GROUP
-
-    def rest(i, _):
-        list_ref[head + item + i] = planes * gy * gz - 1
-        for t in range(ITEM):
-            list_ref[entries + (item + i) * ITEM + t] = dummy
-        return 0
-
-    lax.fori_loop(0, 2 * GROUP - 1, rest, 0)
-
-
-def build_partners(dims, pos, cnt, emb, lhs_ref, wide_ref, *accs):
-    planes, gy, gz = dims
-    ey, ez = gy + 2, gz + 2
-    slots = lhs_ref.shape[1]
+    slots = lhs_ref.shape[-1]
     full = (8, slots)
     rows = lax.broadcasted_iota(jnp.int32, full, 0)
     lane = lax.broadcasted_iota(jnp.int32, full, 1)
@@ -124,7 +147,7 @@
     def store(ext, value):
         h, m, l = split3(value)
         tall = jnp.concatenate([h, h, h, m, m, m, l, l, blank], axis=0).T.astype(BF)
-        lhs_ref[ext] = tall
+        lhs_ref[rows_of(ext, slots), :] = tall
         return tall
 
     if wide_ref is not None:
@@ -171,14 +194,15 @@
         for z in range(1, gz + 1):
             both = pltpu.matmul_pop(acc_xy[z - 1])
             for at in [z] + [0] * (z == gz) + [gz + 1] * (z == 1):
-                wide_ref[spot + at, 0] = both[:, :slots]
-                wide_ref[spot + at, 1] = both[:, slots:]
+                wide_ref[0, rows_of(spot + at, slots), :] = both[:, :slots]
+                wide_ref[1, rows_of(spot + at, slots), :] = both[:, slots:]
         for z in range(ez):
             both = pltpu.matmul_pop(acc_z[z])
-            wide_ref[spot + z, 2, :half, :] = both[:, :slots]
-            wide_ref[spot + z, 2, half:, :] = both[:, slots:]
-
-    spot = jnp.int32(0)
+            wide_ref[2, rows_of(spot + z, slots), :] = jnp.concatenate(
+                [both[:, :slots], both[:, slots:]], axis=0
+            )
+
+    spot, item = jnp.int32(0), jnp.int32(0)
     for j in range(planes + 2):
         which, at = (0, 0) if j == 0 else ((2, 0) if j == planes + 1 else (1, j - 1))
 
@@ -196,11 +220,21 @@
                 )
             return (j * ey + y) * ez
 
-        spot = lax.fori_loop(0, ey, line, spot)
+        def line_and_list(y, item):
+            line(y, None)
+            return lister.add_row(j, y, item)
+
+        if lister is None:
+            spot = lax.fori_loop(0, ey, line, spot)
+        else:
+            item = lax.fori_loop(0, gy, line_and_list, item)
+            lax.fori_loop(gy, ey, lambda y, zero: line(y, None) or zero, 0)
+    if lister is not None:
+        lister.close(item)
     if wide_ref is not None:
         put(spot)
         for k in range(3):
-            wide_ref[(planes + 2) * ey * ez, k] = jnp.zeros((slots, slots), F32)
+            wide_ref[k, (planes + 2) * ey * ez * slots :, :] = jnp.zeros((slots, slots), F32)
     store((planes + 2) * ey * ez, jnp.where(rows == 3, FAR, jnp.where(rows >= 4, 1.0, 0.0)))
 
 
@@ -266,12 +300,13 @@
 def density_kernel(dims, first, *refs):
     planes, gy, gz = dims
     if first:
-        (p0, p1, p2, c0, c1, c2, fl, fl_lo, emb_ref, lo_ref, hi_ref, list_ref, lhs_ref, right_ref, res_ref) = refs
-        build_list(dims, fl, fl_lo, list_ref)
+        (p0, p1, p2, c0, c1, c2, fl, fl_lo, emb_ref, lo_ref, hi_ref, list_ref, lhs_ref, right_ref, res_ref, size_ref) = refs
+        lister = ListBuilder(dims, lhs_ref.shape[-1], (c0, c1, c2), fl, fl_lo, list_ref, size_ref)
     else:
         (q0, q1, q2, c0, c1, c2, list_ref, f_ref, v_ref, b0, b2) = refs[:11]
         sum_refs = refs[11:-10]
         (emb_ref, lo_ref, hi_ref, p0, p1, p2, v_out, lhs_ref, right_ref, res_ref) = refs[-10:]
+        lister = None
         mix = mix_factor(sum_refs)
         quench_update(
             dims, mix, q1, lambda k, p, y: f_ref[k, p, y], lambda k, p, y: v_ref[k, p, y], planes, p1, v_out
@@ -280,8 +315,8 @@
             quench_update(
                 dims, mix, q, lambda k, p, y, b=b: b[k, p, y], lambda k, p, y, b=b: b[k + 3, p, y], 1, out, None
             )
-    slots = lhs_ref.shape[1]
-    build_partners(dims, (p0, p1, p2), (c0, c1, c2), None, lhs_ref, None)
+    slots = lhs_ref.shape[-1]
+    build_partners(dims, (p0, p1, p2), (c0, c1, c2), None, lister, lhs_ref, None)
     build_rights(dims, p1, c1, None, right_ref)
     gap = jnp.zeros((slots - KDIM, slots), BF)
     side = jnp.zeros((slots, slots), BF)
@@ -292,16 +327,11 @@
             [jnp.concatenate([one, side], axis=1), jnp.concatenate([side, one], axis=1)], axis=0
         )
 
-    quarter = slots // 4
-
-    def left_of(entry, m):
-        start = m * 2 * quarter
-        return jnp.concatenate(
-            [lhs_ref[entry, start + h * quarter : start + (h + 1) * quarter, :] for h in range(2)], axis=1
-        )
-
-    def work(entry, m, value, acc):
-        for r in range(quarter // 8):
+    def left_of(starts):
+        return jnp.concatenate([lhs_ref[tile_at(start), :] for start in starts], axis=1)
+
+    def work(starts, value, acc):
+        for r in range(TILE // 8):
             for h in range(2):
                 t = jnp.maximum(value[r * 8 : r * 8 + 8, h * slots : (h + 1) * slots], 0.0)
                 acc[r % 4] = acc[r % 4] + t * t * t
@@ -309,7 +339,7 @@
     def emit(cell, acc):
         res_ref[cell] = (acc[0] + acc[1]) + (acc[2] + acc[3])
 
-    run_items(dims, slots, list_ref, GROUP, quarter, 4, right_of, left_of, work, emit)
+    run_items(dims, slots, list_ref, GROUP, 2, 4, right_of, left_of, work, emit)
     lane = lax.broadcasted_iota(jnp.int32, (1, slots), 1)
     for p in range(planes):
 
@@ -344,10 +374,14 @@
         lax.fori_loop(0, gy, row, 0)
 
 
-def run_items(dims, slots, list_ref, group, height, chains, right_of, left_of, work, emit):
-    head, items, _ = list_sizes(dims)
+def tile_at(start):
+    return pl.ds(pl.multiple_of(start, TILE), TILE)
+
+
+def run_items(dims, slots, list_ref, group, width, chains, right_of, left_of, work, emit):
+    head, items, _ = list_sizes(dims, slots)
     entries = head + items
-    turns = ITEM
+    turns = ITEM // (2 * width)
 
     def inner(*flat):
         accs = [
@@ -355,8 +389,8 @@
             for i in range(group)
         ]
 
-        def entry_of(item, t):
-            return list_ref[entries + item * ITEM + t]
+        def starts_of(item, m, t):
+            return [list_ref[entries + item * ITEM + (t * 2 + m) * width + w] for w in range(width)]
 
         def load_right(item):
             right = right_of(list_ref[head + item])
@@ -366,7 +400,7 @@
         def send(item, i, m, t):
             pltpu.matmul_acc_lhs(
                 accs[i][m][t],
-                left_of(entry_of(item, t), m),
+                left_of(starts_of(item, m, t)),
                 load_staged_rhs=0 if t == 0 else None,
             )
 
@@ -389,7 +423,7 @@
                     for m in range(2):
                         value = pltpu.matmul_pop(accs[i][m][t])
                         send(item + group, i, m, t)
-                        work(entry_of(item, t), m, value, acc)
+                        work(starts_of(item, m, t), value, acc)
                 emit(cell, acc)
             return tuple(acc)
 
@@ -403,7 +437,7 @@
     pl.run_scoped(
         inner,
         *[
-            pltpu.ACC(m)((height, 2 * slots), F32)
+            pltpu.ACC(m)((TILE, 2 * slots), F32)
             for _ in range(group)
             for m in range(2)
             for _ in range(turns)
@@ -417,38 +451,38 @@
     edges = refs[14:-4]
     (lhs_ref, right_ref, res_ref, wide_ref) = refs[-4:]
     planes, gy, gz = dims
-    slots = lhs_ref.shape[1]
+    slots = lhs_ref.shape[-1]
     pl.run_scoped(
-        functools.partial(build_partners, dims, (p0, p1, p2), (c0, c1, c2), (e0, e1, e2), lhs_ref, wide_ref),
+        functools.partial(build_partners, dims, (p0, p1, p2), (c0, c1, c2), (e0, e1, e2), None, lhs_ref, wide_ref),
         *[pltpu.ACC(0)((slots, 2 * slots), F32) for _ in range(gz)],
         *[pltpu.ACC(1)((slots // 2, 2 * slots), F32) for _ in range(gz + 2)],
     )
     build_rights(dims, p1, c1, e1, right_ref)
     gap = jnp.zeros((2 * slots - KDIM, 2 * slots), BF)
-    half = slots // 2
-    side = jnp.zeros((half, slots), BF)
+    side = jnp.zeros((TILE, slots), BF)
 
     def right_of(cell):
         return jnp.concatenate([right_ref[cell], gap], axis=0)
 
-    def left_of(entry, m):
-        return jnp.concatenate([lhs_ref[entry, m * half : (m + 1) * half, :], side], axis=1)
-
-    def work(entry, m, value, acc):
-        for r in range(half // 8):
+    def left_of(starts):
+        return jnp.concatenate([lhs_ref[tile_at(starts[0]), :], side], axis=1)
+
+    def work(starts, value, acc):
+        wides = [wide_ref[k, tile_at(starts[0]), :] for k in range(3)]
+        for r in range(TILE // 8):
             here = slice(r * 8, r * 8 + 8)
             t = jnp.maximum(value[here, :slots], 0.0)
             g = t * t * value[here, slots:]
             at = (r % 2) * 4
             acc[at] = acc[at] + g
             for k in range(3):
-                acc[at + 1 + k] = acc[at + 1 + k] + g * wide_ref[entry, k, m * half + r * 8 : m * half + r * 8 + 8, :]
+                acc[at + 1 + k] = acc[at + 1 + k] + g * wides[k][here]
 
     def emit(cell, acc):
         for k in range(4):
             res_ref[cell, k] = acc[k] + acc[k + 4]
 
-    run_items(dims, slots, list_ref, 2, half, 8, right_of, left_of, work, emit)
+    run_items(dims, slots, list_ref, 2, 1, 8, right_of, left_of, work, emit)
     lane = lax.broadcasted_iota(jnp.int32, (1, slots), 1)
     sums = (jnp.zeros((1, slots), F32), jnp.zeros((1, slots), F32))
     for p in range(planes):
@@ -535,7 +569,7 @@
     smem = pl.BlockSpec(memory_space=pltpu.SMEM)
     ext = (planes + 2) * (gy + 2) * (gz + 2) + 1
     cells = planes * gy * gz
-    entries = list_sizes(dims)[2]
+    entries = list_sizes(dims, slots)[2]
     pairs = planes * gy * gz * 27 * slots * slots
 
     def shaped(*shape):
@@ -550,13 +584,13 @@
     flags_lo = lax.ppermute(lax.slice_in_dim(pair_flags, planes - 1, planes, axis=1), "space", up)
     count_lo, count_hi = halo(*planes_of(counts, 0))
     pos_lo, pos_hi = halo(*planes_of(start_pos, 1))
-    lhs_scratch = pltpu.VMEM((ext, slots, slots), BF)
+    lhs_scratch = pltpu.VMEM((ext * slots, slots), BF)
     scratch_d = [lhs_scratch, pltpu.VMEM((cells, KDIM, slots), BF), pltpu.VMEM((cells, 8, slots), F32)]
     scratch_f = [
         lhs_scratch,
         pltpu.VMEM((cells, KDIM, 2 * slots), BF),
         pltpu.VMEM((cells, 4, 8, slots), F32),
-        pltpu.VMEM((ext, 3, slots, slots), F32),
+        pltpu.VMEM((3, ext * slots, slots), F32),
     ]
     emb_shape = [shaped(planes, gy, gz, slots), shaped(1, gy, gz, slots), shaped(1, gy, gz, slots)]
     vec, edge = shaped(3, planes, gy, gz, slots), shaped(3, 1, gy, gz, slots)
@@ -591,7 +625,7 @@
                 out_shape=(*emb_shape, jax.ShapeDtypeStruct((entries,), jnp.int32)),
                 in_specs=specs + [smem, smem],
                 out_specs=(vmem, vmem, vmem, smem),
-                scratch_shapes=scratch_d,
+                scratch_shapes=scratch_d + [pltpu.SMEM(((planes + 2) * gy * gz,), jnp.int32)],
                 compiler_params=pltpu.CompilerParams(vmem_limit_bytes=12 * 2**20),
                 cost_estimate=cost_d,
                 name="density_first",

time: 130 us -> 129 us (level)
  transfers between devices with their start and end apart: 21 -> 21, of which waited for: 11 -> 9; matrix products, arithmetic and copies ran while one was open for 0% -> 0% of each run, Pallas kernels for 34% -> 33%
where the time goes in v5:
time: 129 us
  Pallas kernels  92.6 us (72%)
  starting transfers between devices  21.7 us (17%)
  waiting for transfers between devices  11.9 us (9%)
  local copies, waits for them, and re-layouts  1.7 us (1%)
    pallas_call x2, Pallas kernels, body(): pl.pallas_call(functools.partial(force_kernel, dims), out_shape=(vec, vec...  53 us
    pallas_call x1, Pallas kernels, body(): pl.pallas_call(functools.partial(density_kernel, dims, True), out_shape=(...  22.1 us
    pallas_call x1, Pallas kernels, body(): pl.pallas_call(functools.partial(density_kernel, dims, False), out_shape=...  16.1 us
    ppermute x10, starting transfers between devices, halo(): return (lax.ppermute(last, 'space', up), lax.ppermute(first, 'space', down))  9.63 us
    ppermute x4, starting transfers between devices, hop(): options.append(lax.ppermute(held, 'rep', pairs))  6.31 us
    ppermute x6, waiting for transfers between devices, body(): lax.ppermute(part, 'space', ring('space', s))  5.28 us
    ppermute x6, starting transfers between devices, body(): lax.ppermute(part, 'space', ring('space', s))  4.38 us
    ppermute x10, waiting for transfers between devices, halo(): return (lax.ppermute(last, 'space', up), lax.ppermute(first, 'space', down))  3.9 us
  transfers between devices with their start and end apart: 21, of which 9 were waited for; matrix products, arithmetic and copies ran while one was open for 0% of the time, Pallas kernels for 33%

profile of v5, /device:TPU:0, one launch (start us, length us, event | category | flops | bytes accessed | tf_op | source)
XLA Modules:
  0.0 129.0 jit_solution(1155485991694115161)
XLA Ops:
  0.6 0.8 fusion
  1.4 0.5 collective-permute-start
  1.9 2.0 %collective-permute-start.1 = (f32[3,1,4,4,128]{4,3,2,1,0:T(4,128)S(1)}, f32[3,1,4,4,128]{4,3,2,1,0:T(4,128)S(1)}, u32[]{:S(2)}, u32[]{:S(2)}) collective-permute-start(f32[3,1,4,4,128]{4,3,2,1,0:T(4,128)S(1)} %get-tuple-element.50), channel_id=1, source_target_pairs={{0,3},{1,0},{2,1},{3,2},{4,7},{5,4},{6,5},{7,6},{8,11},{9,8},{10,9... | collective-permute-start | bytes 73736 | tf_op jit(solution)/shard_map/ppermute | solution.py:582
  4.0 1.4 %collective-permute-start.4 = (s32[13,1,4,4]{3,2,1,0:T(4,128)S(1)}, s32[13,1,4,4]{3,2,1,0:T(4,128)S(1)}, u32[]{:S(2)}, u32[]{:S(2)}) collective-permute-start(s32[13,1,4,4]{3,2,1,0:T(4,128)S(1)} %copy.10), channel_id=1, source_target_pairs={{0,1},{1,2},{2,3},{3,0},{4,5},{5,6},{6,7},{7,4},{8,9},{9,10},{10,1... | collective-permute-start | bytes 2504 | tf_op jit(solution)/shard_map/ppermute | solution.py:584
  5.4 1.1 collective-permute-start.2
  6.4 0.7 collective-permute-start.3
  7.3 1.1 collective-permute-done.2.refs_3_
  8.5 22.1 %density_first.1 = (f32[2,4,4,128]{3,2,1,0:T(4,128)S(1)}, f32[1,4,4,128]{3,2,1,0:T(4,128)S(1)}, f32[1,4,4,128]{3,2,1,0:T(4,128)S(1)}, s32[3880]{0:T(1024)S(1)}) custom-call(f32[3,1,4,4,128]{4,3,2,1,0:T(4,128)S(1)} %collective-permute-done.refs_0_, f32[3,2,4,4,128]{4,3,2,1,0:T(4,128)S(1)} %bitcast.11, ...), custom_call_target="tpu_custom_call" | custom-call | flops 141557760 | bytes 1048576 | tf_op jit(solution)/shard_map/density_first/pallas_call | solution.py:623
  30.6 1.8 %collective-permute-start.5 = (f32[1,4,4,128]{3,2,1,0:T(4,128)S(1)}, f32[1,4,4,128]{3,2,1,0:T(4,128)S(1)}, u32[]{:S(2)}, u32[]{:S(2)}) collective-permute-start(f32[1,4,4,128]{3,2,1,0:T(4,128)S(1)} %get-tuple-element.28), channel_id=1, source_target_pairs={{0,1},{1,2},{2,3},{3,0},{4,5},{5,6},{6,7},{7,4},{8,9},{9,10},{10,1... | collective-permute-start | bytes 24584 | tf_op jit(solution)/shard_map/ppermute | solution.py:582
  32.4 1.3 %collective-permute-done.5.refs_6_ = f32[1,4,4,128]{3,2,1,0:T(4,128)S(1)} collective-permute-done((f32[1,4,4,128]{3,2,1,0:T(4,128)S(1)}, f32[1,4,4,128]{3,2,1,0:T(4,128)S(1)}, u32[]{:S(2)}, u32[]{:S(2)}) %collective-permute-start.5) | collective-permute-done | bytes 8224 | tf_op jit(solution)/shard_map/ppermute | solution.py:582
  33.8 26.5 %force.2 = (f32[3,2,4,4,128]{4,3,2,1,0:T(4,128)S(1)}, f32[3,2,4,4,128]{4,3,2,1,0:T(4,128)S(1)}, f32[8,128]{1,0:T(8,128)S(1)}, f32[6,1,4,4,128]{4,3,2,1,0:T(4,128)S(1)}, f32[6,1,4,4,128]{4,3,2,1,0:T(4,128)S(1)}) custom-call(f32[3,1,4,4,128]{4,3,2,1,0:T(4,128)S(1)} %collective-permute-done.refs_0_, f32[3,2,4,4,128]{4,3,2,1,0:T(4,128)S(1)} %bitcast.12, ...), custom_call_target="tpu_custom_call" | custom-call | flops 353894400 | bytes 1048576 | tf_op jit(solution)/shard_map/force/pallas_call | solution.py:647
  60.3 2.6 %collective-permute-start.14 = (f32[6,2,4,4,128]{4,3,2,1,0:T(4,128)S(1)}, f32[6,2,4,4,128]{4,3,2,1,0:T(4,128)S(1)}, u32[]{:S(2)}, u32[]{:S(2)}) collective-permute-start(f32[6,2,4,4,128]{4,3,2,1,0:T(4,128)S(1)} %pad_maximum_fusion), channel_id=1, source_target_pairs={{0,12},{4,0},{8,4},{12,8},{16,28},{20,16},{24,20},{28,24},{1,13},{... | collective-permute-start | bytes 294920 | tf_op jit(solution)/shard_map/ppermute | solution.py:614
  62.9 0.4 collective-permute-start.15
  63.4 0.7 collective-permute-start.16
  64.0 0.7 copy-done.5
  64.8 1.3 collective-permute-start.7
  66.1 0.5 collective-permute-start.8
  66.6 2.0 %collective-permute-done.15 = f32[6,2,4,4,128]{4,3,2,1,0:T(4,128)S(1)} collective-permute-done((f32[6,2,4,4,128]{4,3,2,1,0:T(4,128)S(1)}, f32[6,2,4,4,128]{4,3,2,1,0:T(4,128)S(1)}, u32[]{:S(2)}, u32[]{:S(2)}) %collective-permute-start.15) | collective-permute-done | bytes 98336 | tf_op jit(solution)/shard_map/ppermute | solution.py:614
  68.6 0.8 collective-permute-done.16
  69.4 2.7 %collective-permute-start.17 = (f32[6,2,4,4,128]{4,3,2,1,0:T(4,128)S(1)}, f32[6,2,4,4,128]{4,3,2,1,0:T(4,128)S(1)}, u32[]{:S(2)}, u32[]{:S(2)}) collective-permute-start(f32[6,2,4,4,128]{4,3,2,1,0:T(4,128)S(1)} %select_select_fusion.refs_6_), channel_id=1, source_target_pairs={{0,16},{4,20},{8,24},{12,28},{16,0},{20,4},{24,8},{28,12},{1,17},{... | collective-permute-start | bytes 294920 | tf_op jit(solution)/shard_map/ppermute | solution.py:614
  72.2 1.1 collective-permute-start.10
  73.2 1.9 %collective-permute-done.9.refs_12_ = f32[8,128]{1,0:T(8,128)S(1)} collective-permute-done((f32[8,128]{1,0:T(8,128)S(1)}, f32[8,128]{1,0:T(8,128)S(1)}, u32[]{:S(2)}, u32[]{:S(2)}) %collective-permute-start.9) | collective-permute-done | bytes 4128 | tf_op jit(solution)/shard_map/ppermute | solution.py:657
  75.1 0.7 collective-permute-done.10.refs_13_
  75.8 0.7 collective-permute-done.11.refs_14_
  76.5 16.1 %density_next.1 = (f32[2,4,4,128]{3,2,1,0:T(4,128)S(1)}, f32[1,4,4,128]{3,2,1,0:T(4,128)S(1)}, f32[1,4,4,128]{3,2,1,0:T(4,128)S(1)}, f32[3,1,4,4,128]{4,3,2,1,0:...) custom-call(f32[3,1,4,4,128]{4,3,2,1,0:T(4,128)S(1)} %collective-per, ...), custom_call_target="tpu_custom_call" | custom-call | flops 141557760 | bytes 1048576 | tf_op jit(solution)/shard_map/density_next/pallas_call | solution.py:634
  92.5 1.5 %collective-permute-start.12 = (f32[1,4,4,128]{3,2,1,0:T(4,128)S(1)}, f32[1,4,4,128]{3,2,1,0:T(4,128)S(1)}, u32[]{:S(2)}, u32[]{:S(2)}) collective-permute-start(f32[1,4,4,128]{3,2,1,0:T(4,128)S(1)} %get-tuple-element.39), channel_id=1, source_target_pairs={{0,1},{1,2},{2,3},{3,0},{4,5},{5,6},{6,7},{7,4},{8,9},{9,10},{10,1... | collective-permute-start | bytes 24584 | tf_op jit(solution)/shard_map/ppermute | solution.py:582
  94.3 1.3 %collective-permute-done.12.refs_6_ = f32[1,4,4,128]{3,2,1,0:T(4,128)S(1)} collective-permute-done((f32[1,4,4,128]{3,2,1,0:T(4,128)S(1)}, f32[1,4,4,128]{3,2,1,0:T(4,128)S(1)}, u32[]{:S(2)}, u32[]{:S(2)}) %collective-permute-start.12) | collective-permute-done | bytes 8224 | tf_op jit(solution)/shard_map/ppermute | solution.py:582
  95.7 26.5 %force.3 = (f32[3,2,4,4,128]{4,3,2,1,0:T(4,128)S(1)}, f32[3,2,4,4,128]{4,3,2,1,0:T(4,128)S(1)}, f32[8,128]{1,0:T(8,128)S(1)}) custom-call(f32[3,1,4,4,128]{4,3,2,1,0:T(4,128)S(1)} %get-tuple-element.37.refs_0_, f32[3,2,4,4,128]{4,3,2,1,0:T(4,128)S(1)} %get-tuple-element.36.refs_1_.refs_0_, f32[3,1,4,4,128]{4,3,2,1,0:T(4,128)S(1)} %get-tuple-element.38.refs_2_, ...), custom_call_target="tpu_custom_call" | custom-call | flops 353894400 | bytes 1048576 | tf_op jit(solution)/shard_map/force/pallas_call | solution.py:647
  122.2 1.8 %collective-permute-start.18 = (f32[8,128]{1,0:T(8,128)S(1)}, f32[8,128]{1,0:T(8,128)S(1)}, u32[]{:S(2)}, u32[]{:S(2)}) collective-permute-start(f32[8,128]{1,0:T(8,128)S(1)} %get-tuple-element.45.refs_8_), channel_id=1, source_target_pairs={{0,1},{1,2},{2,3},{3,0},{4,5},{5,6},{6,7},{7,4},{8,9},{9,10},{10,1... | collective-permute-start | bytes 12296 | tf_op jit(solution)/shard_map/ppermute | solution.py:657
  124.0 1.4 %collective-permute-start.20 = (f32[8,128]{1,0:T(8,128)S(1)}, f32[8,128]{1,0:T(8,128)S(1)}, u32[]{:S(2)}, u32[]{:S(2)}) collective-permute-start(f32[8,128]{1,0:T(8,128)S(1)} %get-tuple-element.45.refs_8_), channel_id=1, source_target_pairs={{0,3},{1,0},{2,1},{3,2},{4,7},{5,4},{6,5},{7,6},{8,11},{9,8},{10,9... | collective-permute-start | bytes 12296 | tf_op jit(solution)/shard_map/ppermute | solution.py:657
  125.5 2.1 %collective-permute-done.19.refs_10_ = f32[8,128]{1,0:T(8,128)S(1)} collective-permute-done((f32[8,128]{1,0:T(8,128)S(1)}, f32[8,128]{1,0:T(8,128)S(1)}, u32[]{:S(2)}, u32[]{:S(2)}) %collective-permute-start.19) | collective-permute-done | bytes 4128 | tf_op jit(solution)/shard_map/ppermute | solution.py:657
  127.6 1.4 %finish.1 = (f32[3,2,4,4,128]{4,3,2,1,0:T(4,128)}, f32[3,2,4,4,128]{4,3,2,1,0:T(4,128)}, f32[3,2,4,4,128]{4,3,2,1,0:T(4,128)}, f32[3,2,4,4,128]{4,3,2,1,0:T(4,128)}) custom-call(f32[3,2,4,4,128]{4,3,2,1,0:T(4,128)S(1)} %get-tuple-element.36.refs_1_.refs_0_, f32[3,2,4,4,128]{4,3,2,1,0:T(4,128)S(1)} %get-tuple-element.43.refs_1_, ...), custom_call_target="tpu_custom_call" | custom-call | tf_op jit(solution)/shard_map/finish/pallas_call | solution.py:669
  (35 shorter events, 0.9 us)
Async XLA Ops:
  1.4 7.0 %collective-permute-start = (f32[3,1,4,4,128]{4,3,2,1,0:T(4,128)S(1)}, f32[3,1,4,4,128]{4,3,2,1,0:T(4,128)S(1)}, u32[]{:S(2)}, u32[]{:S(2)}) collective-permute-start(f32[3,1,4,4,128]{4,3,2,1,0:T(4,128)S(1)} %get-tuple-element.51), channel_id=1, source_target_pairs={{0,1},{1,2},{2,3},{3,0},{4,5},{5,6},{6,7},{7,4},{8,9},{9,10},{10,1... | collective-permute-start | bytes 73736 | tf_op jit(solution)/shard_map/ppermute | solution.py:582
  1.9 2.0 %slice-start = ((s32[13,2,4,4]{0,3,2,1:T(4,128)}), s32[13,1,4,4]{0,3,2,1:T(4,128)S(1)}, s32[]{:S(2)}) async-start(s32[13,2,4,4]{0,3,2,1:T(4,128)} %param.10), calls=%async_computation | async-start | bytes 16384 | tf_op jit(solution)/shard_map/slice | solution.py:584
  1.9 6.6 %collective-permute-start.1 = (f32[3,1,4,4,128]{4,3,2,1,0:T(4,128)S(1)}, f32[3,1,4,4,128]{4,3,2,1,0:T(4,128)S(1)}, u32[]{:S(2)}, u32[]{:S(2)}) collective-permute-start(f32[3,1,4,4,128]{4,3,2,1,0:T(4,128)S(1)} %get-tuple-element.50), channel_id=1, source_target_pairs={{0,3},{1,0},{2,1},{3,2},{4,7},{5,4},{6,5},{7,6},{8,11},{9,8},{10,9... | collective-permute-start | bytes 73736 | tf_op jit(solution)/shard_map/ppermute | solution.py:582
  3.9 1.5 %copy-start.2 = (s32[2,4,4]{2,1,0:T(4,128)S(1)}, s32[2,4,4]{2,1,0:T(4,128)}, u32[]{:S(2)}) copy-start(s32[2,4,4]{2,1,0:T(4,128)} %refs_4_.9) | copy-start | bytes 388
  3.9 3.2 %copy-start.4 = (s32[13,2,4,4]{0,3,2,1:T(4,128)S(1)}, s32[13,2,4,4]{0,3,2,1:T(4,128)}, u32[]{:S(2)}) copy-start(s32[13,2,4,4]{0,3,2,1:T(4,128)} %param.10) | copy-start | bytes 4996
  4.0 4.4 %copy-start = (f32[1,3,2,4,4,128]{5,4,3,2,1,0:T(4,128)S(1)}, f32[1,3,2,4,4,128]{5,4,3,2,1,0:T(4,128)}, u32[]{:S(2)}) copy-start(f32[1,3,2,4,4,128]{5,4,3,2,1,0:T(4,128)} %param.6) | copy-start | bytes 147460
  4.0 4.4 %collective-permute-start.4 = (s32[13,1,4,4]{3,2,1,0:T(4,128)S(1)}, s32[13,1,4,4]{3,2,1,0:T(4,128)S(1)}, u32[]{:S(2)}, u32[]{:S(2)}) collective-permute-start(s32[13,1,4,4]{3,2,1,0:T(4,128)S(1)} %copy.10), channel_id=1, source_target_pairs={{0,1},{1,2},{2,3},{3,0},{4,5},{5,6},{6,7},{7,4},{8,9},{9,10},{10,1... | collective-permute-start | bytes 2504 | tf_op jit(solution)/shard_map/ppermute | solution.py:584
  5.4 3.0 %collective-permute-start.2 = (s32[1,4,4]{2,1,0:T(4,128)S(1)}, s32[1,4,4]{2,1,0:T(4,128)S(1)}, u32[]{:S(2)}, u32[]{:S(2)}) collective-permute-start(s32[1,4,4]{2,1,0:T(4,128)S(1)} %get-tuple-element.53), channel_id=1, source_target_pairs={{0,1},{1,2},{2,3},{3,0},{4,5},{5,6},{6,7},{7,4},{8,9},{9,10},{10,1... | collective-permute-start | bytes 200 | tf_op jit(solution)/shard_map/ppermute | solution.py:582
  6.4 2.0 %collective-permute-start.3 = (s32[1,4,4]{2,1,0:T(4,128)S(1)}, s32[1,4,4]{2,1,0:T(4,128)S(1)}, u32[]{:S(2)}, u32[]{:S(2)}) collective-permute-start(s32[1,4,4]{2,1,0:T(4,128)S(1)} %get-tuple-element.52), channel_id=1, source_target_pairs={{0,3},{1,0},{2,1},{3,2},{4,7},{5,4},{6,5},{7,6},{8,11},{9,8},{10,9... | collective-permute-start | bytes 200 | tf_op jit(solution)/shard_map/ppermute | solution.py:582
  7.3 26.5 %copy-start.3 = (f32[1,3,2,4,4,128]{5,4,3,2,1,0:T(4,128)S(1)}, f32[1,3,2,4,4,128]{5,4,3,2,1,0:T(4,128)}, u32[]{:S(2)}) copy-start(f32[1,3,2,4,4,128]{5,4,3,2,1,0:T(4,128)} %param.7) | copy-start | bytes 147460
  30.6 3.1 %collective-permute-start.5 = (f32[1,4,4,128]{3,2,1,0:T(4,128)S(1)}, f32[1,4,4,128]{3,2,1,0:T(4,128)S(1)}, u32[]{:S(2)}, u32[]{:S(2)}) collective-permute-start(f32[1,4,4,128]{3,2,1,0:T(4,128)S(1)} %get-tuple-element.28), channel_id=1, source_target_pairs={{0,1},{1,2},{2,3},{3,0},{4,5},{5,6},{6,7},{7,4},{8,9},{9,10},{10,1... | collective-permute-start | bytes 24584 | tf_op jit(solution)/shard_map/ppermute | solution.py:582
  32.4 1.4 %collective-permute-start.6 = (f32[1,4,4,128]{3,2,1,0:T(4,128)S(1)}, f32[1,4,4,128]{3,2,1,0:T(4,128)S(1)}, u32[]{:S(2)}, u32[]{:S(2)}) collective-permute-start(f32[1,4,4,128]{3,2,1,0:T(4,128)S(1)} %get-tuple-element.30), channel_id=1, source_target_pairs={{0,3},{1,0},{2,1},{3,2},{4,7},{5,4},{6,5},{7,6},{8,11},{9,8},{10,9... | collective-permute-start | bytes 24584 | tf_op jit(solution)/shard_map/ppermute | solution.py:582
  60.3 6.3 %collective-permute-start.14 = (f32[6,2,4,4,128]{4,3,2,1,0:T(4,128)S(1)}, f32[6,2,4,4,128]{4,3,2,1,0:T(4,128)S(1)}, u32[]{:S(2)}, u32[]{:S(2)}) collective-permute-start(f32[6,2,4,4,128]{4,3,2,1,0:T(4,128)S(1)} %pad_maximum_fusion), channel_id=1, source_target_pairs={{0,12},{4,0},{8,4},{12,8},{16,28},{20,16},{24,20},{28,24},{1,13},{... | collective-permute-start | bytes 294920 | tf_op jit(solution)/shard_map/ppermute | solution.py:614
  62.9 5.7 %collective-permute-start.15 = (f32[6,2,4,4,128]{4,3,2,1,0:T(4,128)S(1)}, f32[6,2,4,4,128]{4,3,2,1,0:T(4,128)S(1)}, u32[]{:S(2)}, u32[]{:S(2)}) collective-permute-start(f32[6,2,4,4,128]{4,3,2,1,0:T(4,128)S(1)} %pad_maximum_fusion), channel_id=1, source_target_pairs={{0,8},{4,12},{8,0},{12,4},{16,24},{20,28},{24,16},{28,20},{1,9},{5... | collective-permute-start | bytes 294920 | tf_op jit(solution)/shard_map/ppermute | solution.py:614
  63.4 6.0 %collective-permute-start.16 = (f32[6,2,4,4,128]{4,3,2,1,0:T(4,128)S(1)}, f32[6,2,4,4,128]{4,3,2,1,0:T(4,128)S(1)}, u32[]{:S(2)}, u32[]{:S(2)}) collective-permute-start(f32[6,2,4,4,128]{4,3,2,1,0:T(4,128)S(1)} %pad_maximum_fusion), channel_id=1, source_target_pairs={{0,4},{4,8},{8,12},{12,0},{16,20},{20,24},{24,28},{28,16},{1,5},{5... | collective-permute-start | bytes 294920 | tf_op jit(solution)/shard_map/ppermute | solution.py:614
  64.0 0.7 copy-start.5
  64.8 11.6 %collective-permute-start.7 = (f32[6,1,4,4,128]{4,3,2,1,0:T(4,128)S(1)}, f32[6,1,4,4,128]{4,3,2,1,0:T(4,128)S(1)}, u32[]{:S(2)}, u32[]{:S(2)}) collective-permute-start(f32[6,1,4,4,128]{4,3,2,1,0:T(4,128)S(1)} %get-tuple-element.33), channel_id=1, source_target_pairs={{0,1},{1,2},{2,3},{3,0},{4,5},{5,6},{6,7},{7,4},{8,9},{9,10},{10,1... | collective-permute-start | bytes 147464 | tf_op jit(solution)/shard_map/ppermute | solution.py:582
  66.1 10.4 %collective-permute-start.8 = (f32[6,1,4,4,128]{4,3,2,1,0:T(4,128)S(1)}, f32[6,1,4,4,128]{4,3,2,1,0:T(4,128)S(1)}, u32[]{:S(2)}, u32[]{:S(2)}) collective-permute-start(f32[6,1,4,4,128]{4,3,2,1,0:T(4,128)S(1)} %get-tuple-element.34), channel_id=1, source_target_pairs={{0,3},{1,0},{2,1},{3,2},{4,7},{5,4},{6,5},{7,6},{8,11},{9,8},{10,9... | collective-permute-start | bytes 147464 | tf_op jit(solution)/shard_map/ppermute | solution.py:582
  69.4 58.2 %collective-permute-start.17 = (f32[6,2,4,4,128]{4,3,2,1,0:T(4,128)S(1)}, f32[6,2,4,4,128]{4,3,2,1,0:T(4,128)S(1)}, u32[]{:S(2)}, u32[]{:S(2)}) collective-permute-start(f32[6,2,4,4,128]{4,3,2,1,0:T(4,128)S(1)} %select_select_fusion.refs_6_), channel_id=1, source_target_pairs={{0,16},{4,20},{8,24},{12,28},{16,0},{20,4},{24,8},{28,12},{1,17},{... | collective-permute-start | bytes 294920 | tf_op jit(solution)/shard_map/ppermute | solution.py:614
  72.1 3.0 %collective-permute-start.9 = (f32[8,128]{1,0:T(8,128)S(1)}, f32[8,128]{1,0:T(8,128)S(1)}, u32[]{:S(2)}, u32[]{:S(2)}) collective-permute-start(f32[8,128]{1,0:T(8,128)S(1)} %get-tuple-element.35.refs_11_), channel_id=1, source_target_pairs={{0,1},{1,2},{2,3},{3,0},{4,5},{5,6},{6,7},{7,4},{8,9},{9,10},{10,1... | collective-permute-start | bytes 12296 | tf_op jit(solution)/shard_map/ppermute | solution.py:657
  72.2 3.6 %collective-permute-start.10 = (f32[8,128]{1,0:T(8,128)S(1)}, f32[8,128]{1,0:T(8,128)S(1)}, u32[]{:S(2)}, u32[]{:S(2)}) collective-permute-start(f32[8,128]{1,0:T(8,128)S(1)} %get-tuple-element.35.refs_11_), channel_id=1, source_target_pairs={{0,2},{1,3},{2,0},{3,1},{4,6},{5,7},{6,4},{7,5},{8,10},{9,11},{10,... | collective-permute-start | bytes 12296 | tf_op jit(solution)/shard_map/ppermute | solution.py:657
  75.1 1.3 %collective-permute-start.11 = (f32[8,128]{1,0:T(8,128)S(1)}, f32[8,128]{1,0:T(8,128)S(1)}, u32[]{:S(2)}, u32[]{:S(2)}) collective-permute-start(f32[8,128]{1,0:T(8,128)S(1)} %get-tuple-element.35.refs_11_), channel_id=1, source_target_pairs={{0,3},{1,0},{2,1},{3,2},{4,7},{5,4},{6,5},{7,6},{8,11},{9,8},{10,9... | collective-permute-start | bytes 12296 | tf_op jit(solution)/shard_map/ppermute | solution.py:657
  92.5 3.1 %collective-permute-start.12 = (f32[1,4,4,128]{3,2,1,0:T(4,128)S(1)}, f32[1,4,4,128]{3,2,1,0:T(4,128)S(1)}, u32[]{:S(2)}, u32[]{:S(2)}) collective-permute-start(f32[1,4,4,128]{3,2,1,0:T(4,128)S(1)} %get-tuple-element.39), channel_id=1, source_target_pairs={{0,1},{1,2},{2,3},{3,0},{4,5},{5,6},{6,7},{7,4},{8,9},{9,10},{10,1... | collective-permute-start | bytes 24584 | tf_op jit(solution)/shard_map/ppermute | solution.py:582
  94.0 1.7 %collective-permute-start.13 = (f32[1,4,4,128]{3,2,1,0:T(4,128)S(1)}, f32[1,4,4,128]{3,2,1,0:T(4,128)S(1)}, u32[]{:S(2)}, u32[]{:S(2)}) collective-permute-start(f32[1,4,4,128]{3,2,1,0:T(4,128)S(1)} %get-tuple-element.41), channel_id=1, source_target_pairs={{0,3},{1,0},{2,1},{3,2},{4,7},{5,4},{6,5},{7,6},{8,11},{9,8},{10,9... | collective-permute-start | bytes 24584 | tf_op jit(solution)/shard_map/ppermute | solution.py:582
  122.2 3.3 %collective-permute-start.18 = (f32[8,128]{1,0:T(8,128)S(1)}, f32[8,128]{1,0:T(8,128)S(1)}, u32[]{:S(2)}, u32[]{:S(2)}) collective-permute-start(f32[8,128]{1,0:T(8,128)S(1)} %get-tuple-element.45.refs_8_), channel_id=1, source_target_pairs={{0,1},{1,2},{2,3},{3,0},{4,5},{5,6},{6,7},{7,4},{8,9},{9,10},{10,1... | collective-permute-start | bytes 12296 | tf_op jit(solution)/shard_map/ppermute | solution.py:657
  124.0 3.6 %collective-permute-start.19 = (f32[8,128]{1,0:T(8,128)S(1)}, f32[8,128]{1,0:T(8,128)S(1)}, u32[]{:S(2)}, u32[]{:S(2)}) collective-permute-start(f32[8,128]{1,0:T(8,128)S(1)} %get-tuple-element.45.refs_8_), channel_id=1, source_target_pairs={{0,2},{1,3},{2,0},{3,1},{4,6},{5,7},{6,4},{7,5},{8,10},{9,11},{10,... | collective-permute-start | bytes 12296 | tf_op jit(solution)/shard_map/ppermute | solution.py:657
  124.0 3.6 %collective-permute-start.20 = (f32[8,128]{1,0:T(8,128)S(1)}, f32[8,128]{1,0:T(8,128)S(1)}, u32[]{:S(2)}, u32[]{:S(2)}) collective-permute-start(f32[8,128]{1,0:T(8,128)S(1)} %get-tuple-element.45.refs_8_), channel_id=1, source_target_pairs={{0,3},{1,0},{2,1},{3,2},{4,7},{5,4},{6,5},{7,6},{8,11},{9,8},{10,9... | collective-permute-start | bytes 12296 | tf_op jit(solution)/shard_map/ppermute | solution.py:657
  125.4 2.2 %copy-start.1 = (f32[1,1,3,2,4,4,128]{6,5,4,3,2,1,0:T(4,128)S(1)}, f32[1,1,3,2,4,4,128]{6,5,4,3,2,1,0:T(4,128)}, u32[]{:S(2)}) copy-start(f32[1,1,3,2,4,4,128]{6,5,4,3,2,1,0:T(4,128)} %param.8) | copy-start | bytes 147460

commit v6 on v5

--- a/solution.py
+++ b/solution.py
@@ -90,36 +90,40 @@
 
             lax.fori_loop(0, gy, row, 0)
 
-    def add_cell(self, p, y, z, item):
+    def add_cell(self, p, y, z, item, base, near, spots):
         _, gy, gz = self.dims
         ey, ez = gy + 2, gz + 2
         at = self.entries + item * ITEM
         for ox, oy, oz in OFFSETS:
-            ext = ((p + 1 + ox) * ey + (y + 1 + oy)) * ez + (z + 1 + oz)
-            jy, jz = wrap(y + oy, gy), (z + oz) % gz
-            number = self.size_ref[((p + 1 + ox) * gy + jy) * gz + jz]
+            first = (((p + 1 + ox) * ey + 1 + oy) * ez + (z + 1 + oz)) * self.slots
+            jz = (z + oz) % gz
+            number = self.size_ref[spots[oy] + ((p + 1 + ox) * gy * gz + jz)]
             for t in range(self.slots // TILE):
-                self.list_ref[at + t] = ext * self.slots + t * TILE
+                self.list_ref[at + t] = base + (first + t * TILE)
             found = flag_of((ox, oy, oz))
             if found is not None:
                 index, forward = found
                 if forward:
                     flag = self.flags[index, p, y, z]
                 elif p + ox < 0:
-                    flag = self.flags_lo[index, 0, jy, jz]
+                    flag = self.flags_lo[index, 0, near[oy], jz]
                 else:
-                    flag = self.flags[index, p + ox, jy, jz]
+                    flag = self.flags[index, p + ox, near[oy], jz]
                 number = number * flag
             at = at + number
         for t in range(ITEM):
             self.list_ref[at + t] = self.dummy
         for t in range(-(-27 * (self.slots // TILE) // ITEM)):
-            self.list_ref[self.head + item + t] = (p * gy + y) * gz + z
+            self.list_ref[self.head + item + t] = y * gz + (p * gy * gz + z)
         return lax.div(at - self.entries + (ITEM - 1), jnp.int32(ITEM))
 
     def add_row(self, j, y, item):
+        gy, gz = self.dims[1:]
+        base = y * ((gz + 2) * self.slots)
+        near = {oy: wrap(y + oy, gy) for oy in (-1, 0, 1)}
+        spots = {oy: near[oy] * gz for oy in (-1, 0, 1)}
         for p, z in self.shares[j]:
-            item = self.add_cell(p, y, z, item)
+            item = self.add_cell(p, y, z, item, base, near, spots)
         return item
 
     def close(self, item):
@@ -165,13 +169,9 @@
                 chosen = used & (row // slots == col) & (line_row % 8 == 2)
             pick = jnp.where(chosen, 1.0, 0.0)
             pltpu.matmul_push_rhs(pick.astype(BF), staging_register=0, mxu_index=m)
-        for m in range(2):
-            for index, acc in enumerate((acc_xy, acc_z)[m]):
-                pltpu.matmul_acc_lhs(
-                    acc,
-                    jnp.zeros((slots if m == 0 else half, 2 * slots), BF),
-                    load_staged_rhs=0 if index == 0 else None,
-                )
+        for acc, height in ((acc_xy[0], slots), (acc_z[0], half)):
+            pltpu.matmul_acc_lhs(acc, jnp.zeros((height, 2 * slots), BF), load_staged_rhs=0)
+            pltpu.matmul_pop(acc)
 
     def one(j, which, at, y, z, by, bz):
         raw = [
@@ -190,49 +190,64 @@
             value = jnp.where(rows == 6, e, value)
         return store((j * ey + y) * ez + z, value)
 
-    def put(spot):
+    def put(spot, images=()):
         for z in range(1, gz + 1):
             both = pltpu.matmul_pop(acc_xy[z - 1])
-            for at in [z] + [0] * (z == gz) + [gz + 1] * (z == 1):
-                wide_ref[0, rows_of(spot + at, slots), :] = both[:, :slots]
-                wide_ref[1, rows_of(spot + at, slots), :] = both[:, slots:]
-        for z in range(ez):
-            both = pltpu.matmul_pop(acc_z[z])
-            wide_ref[2, rows_of(spot + z, slots), :] = jnp.concatenate(
-                [both[:, :slots], both[:, slots:]], axis=0
-            )
-
-    spot, item = jnp.int32(0), jnp.int32(0)
+            deep = pltpu.matmul_pop(acc_z[z - 1])
+            deep = jnp.concatenate([deep[:, :slots], deep[:, slots:]], axis=0)
+            wide_x, wide_y = both[:, :slots], both[:, slots:]
+            for line, shift in ((spot, 0.0), *images):
+                here = wide_y + shift if shift else wide_y
+                for at, turn in [(z, 0.0)] + [(0, -1.0 * gz)] * (z == gz) + [(gz + 1, 1.0 * gz)] * (z == 1):
+                    rows_at = rows_of(line + at, slots)
+                    wide_ref[0, rows_at, :] = wide_x
+                    wide_ref[1, rows_at, :] = here
+                    wide_ref[2, rows_at, :] = deep + turn if turn else deep
+
+    def send(talls):
+        for z in range(1, gz + 1):
+            pltpu.matmul_acc_lhs(acc_xy[z - 1], jnp.concatenate([talls[z], side], axis=1))
+            pltpu.matmul_acc_lhs(acc_z[z - 1], jnp.concatenate([talls[z][:half], talls[z][half:]], axis=1))
+
+    item = jnp.int32(0)
     for j in range(planes + 2):
         which, at = (0, 0) if j == 0 else ((2, 0) if j == planes + 1 else (1, j - 1))
 
-        def line(y, spot):
-            by = wrap(y - 1, gy)
-            talls = [one(j, which, at, y, z, by, (z - 1) % gz) for z in range(ez)]
-            if wide_ref is None:
-                return spot
-            put(spot)
-            for z in range(ez):
-                if 1 <= z <= gz:
-                    pltpu.matmul_acc_lhs(acc_xy[z - 1], jnp.concatenate([talls[z], side], axis=1))
-                pltpu.matmul_acc_lhs(
-                    acc_z[z], jnp.concatenate([talls[z][:half], talls[z][half:]], axis=1)
-                )
-            return (j * ey + y) * ez
+        def line(y, by):
+            return [one(j, which, at, y, z, by, (z - 1) % gz) for z in range(ez)]
+
+        def wide_line(y, _):
+            talls = line(y, y - 1)
+            put((j * ey + y - 1) * ez)
+            send(talls)
+            return 0
 
         def line_and_list(y, item):
-            line(y, None)
+            line(y, wrap(y - 1, gy))
             return lister.add_row(j, y, item)
 
-        if lister is None:
-            spot = lax.fori_loop(0, ey, line, spot)
+        def plain(y, _):
+            line(y, wrap(y - 1, gy))
+            return 0
+
+        if wide_ref is not None:
+            base = j * ey * ez
+            line(0, gy - 1)
+            send(line(1, 0))
+            talls = line(2, 1)
+            put(base + ez, [(base + (gy + 1) * ez, 1.0 * gy)])
+            send(talls)
+            lax.fori_loop(3, gy + 1, wide_line, 0)
+            line(gy + 1, 0)
+            put(base + gy * ez, [(base, -1.0 * gy)])
+        elif lister is None:
+            lax.fori_loop(0, ey, plain, 0)
         else:
             item = lax.fori_loop(0, gy, line_and_list, item)
-            lax.fori_loop(gy, ey, lambda y, zero: line(y, None) or zero, 0)
+            lax.fori_loop(gy, ey, plain, 0)
     if lister is not None:
         lister.close(item)
     if wide_ref is not None:
-        put(spot)
         for k in range(3):
             wide_ref[k, (planes + 2) * ey * ez * slots :, :] = jnp.zeros((slots, slots), F32)
     store((planes + 2) * ey * ez, jnp.where(rows == 3, FAR, jnp.where(rows >= 4, 1.0, 0.0)))
@@ -455,7 +470,7 @@
     pl.run_scoped(
         functools.partial(build_partners, dims, (p0, p1, p2), (c0, c1, c2), (e0, e1, e2), None, lhs_ref, wide_ref),
         *[pltpu.ACC(0)((slots, 2 * slots), F32) for _ in range(gz)],
-        *[pltpu.ACC(1)((slots // 2, 2 * slots), F32) for _ in range(gz + 2)],
+        *[pltpu.ACC(1)((slots // 2, 2 * slots), F32) for _ in range(gz)],
     )
     build_rights(dims, p1, c1, e1, right_ref)
     gap = jnp.zeros((2 * slots - KDIM, 2 * slots), BF)

time: 129 us -> 125 us (0.969)
  Pallas kernels: 92.6 us -> 88.4 us
    pallas_call x2, Pallas kernels: 53 us -> 49.2 us  [body(): pl.pallas_call(functools.partial(force_kernel, dims), out_shape=(vec, vec...]
where the time goes in v6:
time: 125 us
  Pallas kernels  88.4 us (71%)
  starting transfers between devices  21.6 us (17%)
  waiting for transfers between devices  12 us (10%)
  local copies, waits for them, and re-layouts  1.7 us (1%)
    pallas_call x2, Pallas kernels, body(): pl.pallas_call(functools.partial(force_kernel, dims), out_shape=(vec, vec...  49.2 us
    pallas_call x1, Pallas kernels, body(): pl.pallas_call(functools.partial(density_kernel, dims, True), out_shape=(...  21.8 us
    pallas_call x1, Pallas kernels, body(): pl.pallas_call(functools.partial(density_kernel, dims, False), out_shape=...  16.1 us
    ppermute x10, starting transfers between devices, halo(): return (lax.ppermute(last, 'space', up), lax.ppermute(first, 'space', down))  9.63 us
    ppermute x4, starting transfers between devices, hop(): options.append(lax.ppermute(held, 'rep', pairs))  6.32 us
    ppermute x6, waiting for transfers between devices, body(): lax.ppermute(part, 'space', ring('space', s))  5.32 us
    ppermute x6, starting transfers between devices, body(): lax.ppermute(part, 'space', ring('space', s))  4.34 us
    ppermute x10, waiting for transfers between devices, halo(): return (lax.ppermute(last, 'space', up), lax.ppermute(first, 'space', down))  3.9 us
  transfers between devices with their start and end apart: 21, of which 9 were waited for; matrix products, arithmetic and copies ran while one was open for 0% of the time, Pallas kernels for 33%

profile of v6, /device:TPU:0, one launch (start us, length us, event | category | flops | bytes accessed | tf_op | source)
XLA Modules:
  0.0 124.8 jit_solution(15808456808137431927)
XLA Ops:
  0.6 0.8 fusion
  1.4 0.5 collective-permute-start
  1.9 2.0 %collective-permute-start.1 = (f32[3,1,4,4,128]{4,3,2,1,0:T(4,128)S(1)}, f32[3,1,4,4,128]{4,3,2,1,0:T(4,128)S(1)}, u32[]{:S(2)}, u32[]{:S(2)}) collective-permute-start(f32[3,1,4,4,128]{4,3,2,1,0:T(4,128)S(1)} %get-tuple-element.50), channel_id=1, source_target_pairs={{0,3},{1,0},{2,1},{3,2},{4,7},{5,4},{6,5},{7,6},{8,11},{9,8},{10,9... | collective-permute-start | bytes 73736 | tf_op jit(solution)/shard_map/ppermute | solution.py:597
  4.0 1.4 %collective-permute-start.4 = (s32[13,1,4,4]{3,2,1,0:T(4,128)S(1)}, s32[13,1,4,4]{3,2,1,0:T(4,128)S(1)}, u32[]{:S(2)}, u32[]{:S(2)}) collective-permute-start(s32[13,1,4,4]{3,2,1,0:T(4,128)S(1)} %copy.10), channel_id=1, source_target_pairs={{0,1},{1,2},{2,3},{3,0},{4,5},{5,6},{6,7},{7,4},{8,9},{9,10},{10,1... | collective-permute-start | bytes 2504 | tf_op jit(solution)/shard_map/ppermute | solution.py:599
  5.4 1.1 collective-permute-start.2
  6.4 0.7 collective-permute-start.3
  7.3 1.1 collective-permute-done.2.refs_3_
  8.5 21.8 %density_first.1 = (f32[2,4,4,128]{3,2,1,0:T(4,128)S(1)}, f32[1,4,4,128]{3,2,1,0:T(4,128)S(1)}, f32[1,4,4,128]{3,2,1,0:T(4,128)S(1)}, s32[3880]{0:T(1024)S(1)}) custom-call(f32[3,1,4,4,128]{4,3,2,1,0:T(4,128)S(1)} %collective-permute-done.refs_0_, f32[3,2,4,4,128]{4,3,2,1,0:T(4,128)S(1)} %bitcast.11, ...), custom_call_target="tpu_custom_call" | custom-call | flops 141557760 | bytes 1048576 | tf_op jit(solution)/shard_map/density_first/pallas_call | solution.py:638
  30.2 1.8 %collective-permute-start.5 = (f32[1,4,4,128]{3,2,1,0:T(4,128)S(1)}, f32[1,4,4,128]{3,2,1,0:T(4,128)S(1)}, u32[]{:S(2)}, u32[]{:S(2)}) collective-permute-start(f32[1,4,4,128]{3,2,1,0:T(4,128)S(1)} %get-tuple-element.28), channel_id=1, source_target_pairs={{0,1},{1,2},{2,3},{3,0},{4,5},{5,6},{6,7},{7,4},{8,9},{9,10},{10,1... | collective-permute-start | bytes 24584 | tf_op jit(solution)/shard_map/ppermute | solution.py:597
  32.0 1.3 %collective-permute-done.5.refs_6_ = f32[1,4,4,128]{3,2,1,0:T(4,128)S(1)} collective-permute-done((f32[1,4,4,128]{3,2,1,0:T(4,128)S(1)}, f32[1,4,4,128]{3,2,1,0:T(4,128)S(1)}, u32[]{:S(2)}, u32[]{:S(2)}) %collective-permute-start.5) | collective-permute-done | bytes 8224 | tf_op jit(solution)/shard_map/ppermute | solution.py:597
  33.4 24.6 %force.2 = (f32[3,2,4,4,128]{4,3,2,1,0:T(4,128)S(1)}, f32[3,2,4,4,128]{4,3,2,1,0:T(4,128)S(1)}, f32[8,128]{1,0:T(8,128)S(1)}, f32[6,1,4,4,128]{4,3,2,1,0:T(4,128)S(1)}, f32[6,1,4,4,128]{4,3,2,1,0:T(4,128)S(1)}) custom-call(f32[3,1,4,4,128]{4,3,2,1,0:T(4,128)S(1)} %collective-permute-done.refs_0_, f32[3,2,4,4,128]{4,3,2,1,0:T(4,128)S(1)} %bitcast.12, ...), custom_call_target="tpu_custom_call" | custom-call | flops 353894400 | bytes 1048576 | tf_op jit(solution)/shard_map/force/pallas_call | solution.py:662
  58.1 2.6 %collective-permute-start.14 = (f32[6,2,4,4,128]{4,3,2,1,0:T(4,128)S(1)}, f32[6,2,4,4,128]{4,3,2,1,0:T(4,128)S(1)}, u32[]{:S(2)}, u32[]{:S(2)}) collective-permute-start(f32[6,2,4,4,128]{4,3,2,1,0:T(4,128)S(1)} %pad_maximum_fusion), channel_id=1, source_target_pairs={{0,12},{4,0},{8,4},{12,8},{16,28},{20,16},{24,20},{28,24},{1,13},{... | collective-permute-start | bytes 294920 | tf_op jit(solution)/shard_map/ppermute | solution.py:629
  60.6 0.4 collective-permute-start.15
  61.1 0.7 collective-permute-start.16
  61.7 0.7 copy-done.5
  62.5 1.3 %collective-permute-start.7 = (f32[6,1,4,4,128]{4,3,2,1,0:T(4,128)S(1)}, f32[6,1,4,4,128]{4,3,2,1,0:T(4,128)S(1)}, u32[]{:S(2)}, u32[]{:S(2)}) collective-permute-start(f32[6,1,4,4,128]{4,3,2,1,0:T(4,128)S(1)} %get-tuple-element.33), channel_id=1, source_target_pairs={{0,1},{1,2},{2,3},{3,0},{4,5},{5,6},{6,7},{7,4},{8,9},{9,10},{10,1... | collective-permute-start | bytes 147464 | tf_op jit(solution)/shard_map/ppermute | solution.py:597
  63.8 0.5 collective-permute-start.8
  64.3 2.0 %collective-permute-done.15 = f32[6,2,4,4,128]{4,3,2,1,0:T(4,128)S(1)} collective-permute-done((f32[6,2,4,4,128]{4,3,2,1,0:T(4,128)S(1)}, f32[6,2,4,4,128]{4,3,2,1,0:T(4,128)S(1)}, u32[]{:S(2)}, u32[]{:S(2)}) %collective-permute-start.15) | collective-permute-done | bytes 98336 | tf_op jit(solution)/shard_map/ppermute | solution.py:629
  66.3 0.8 collective-permute-done.16
  67.2 2.7 %collective-permute-start.17 = (f32[6,2,4,4,128]{4,3,2,1,0:T(4,128)S(1)}, f32[6,2,4,4,128]{4,3,2,1,0:T(4,128)S(1)}, u32[]{:S(2)}, u32[]{:S(2)}) collective-permute-start(f32[6,2,4,4,128]{4,3,2,1,0:T(4,128)S(1)} %select_select_fusion.refs_6_), channel_id=1, source_target_pairs={{0,16},{4,20},{8,24},{12,28},{16,0},{20,4},{24,8},{28,12},{1,17},{... | collective-permute-start | bytes 294920 | tf_op jit(solution)/shard_map/ppermute | solution.py:629
  69.9 1.0 collective-permute-start.10
  70.9 1.9 %collective-permute-done.9.refs_12_ = f32[8,128]{1,0:T(8,128)S(1)} collective-permute-done((f32[8,128]{1,0:T(8,128)S(1)}, f32[8,128]{1,0:T(8,128)S(1)}, u32[]{:S(2)}, u32[]{:S(2)}) %collective-permute-start.9) | collective-permute-done | bytes 4128 | tf_op jit(solution)/shard_map/ppermute | solution.py:672
  72.9 0.6 collective-permute-done.10.refs_13_
  73.5 0.7 collective-permute-done.11.refs_14_
  74.2 16.1 %density_next.1 = (f32[2,4,4,128]{3,2,1,0:T(4,128)S(1)}, f32[1,4,4,128]{3,2,1,0:T(4,128)S(1)}, f32[1,4,4,128]{3,2,1,0:T(4,128)S(1)}, f32[3,1,4,4,128]{4,3,2,1,0:...) custom-call(f32[3,1,4,4,128]{4,3,2,1,0:T(4,128)S(1)} %collective-per, ...), custom_call_target="tpu_custom_call" | custom-call | flops 141557760 | bytes 1048576 | tf_op jit(solution)/shard_map/density_next/pallas_call | solution.py:649
  90.3 1.5 %collective-permute-start.12 = (f32[1,4,4,128]{3,2,1,0:T(4,128)S(1)}, f32[1,4,4,128]{3,2,1,0:T(4,128)S(1)}, u32[]{:S(2)}, u32[]{:S(2)}) collective-permute-start(f32[1,4,4,128]{3,2,1,0:T(4,128)S(1)} %get-tuple-element.39), channel_id=1, source_target_pairs={{0,1},{1,2},{2,3},{3,0},{4,5},{5,6},{6,7},{7,4},{8,9},{9,10},{10,1... | collective-permute-start | bytes 24584 | tf_op jit(solution)/shard_map/ppermute | solution.py:597
  92.1 1.3 %collective-permute-done.12.refs_6_ = f32[1,4,4,128]{3,2,1,0:T(4,128)S(1)} collective-permute-done((f32[1,4,4,128]{3,2,1,0:T(4,128)S(1)}, f32[1,4,4,128]{3,2,1,0:T(4,128)S(1)}, u32[]{:S(2)}, u32[]{:S(2)}) %collective-permute-start.12) | collective-permute-done | bytes 8224 | tf_op jit(solution)/shard_map/ppermute | solution.py:597
  93.4 24.5 %force.3 = (f32[3,2,4,4,128]{4,3,2,1,0:T(4,128)S(1)}, f32[3,2,4,4,128]{4,3,2,1,0:T(4,128)S(1)}, f32[8,128]{1,0:T(8,128)S(1)}) custom-call(f32[3,1,4,4,128]{4,3,2,1,0:T(4,128)S(1)} %get-tuple-element.37.refs_0_, f32[3,2,4,4,128]{4,3,2,1,0:T(4,128)S(1)} %get-tuple-element.36.refs_1_.refs_0_, f32[3,1,4,4,128]{4,3,2,1,0:T(4,128)S(1)} %get-tuple-element.38.refs_2_, ...), custom_call_target="tpu_custom_call" | custom-call | flops 353894400 | bytes 1048576 | tf_op jit(solution)/shard_map/force/pallas_call | solution.py:662
  118.0 1.8 %collective-permute-start.18 = (f32[8,128]{1,0:T(8,128)S(1)}, f32[8,128]{1,0:T(8,128)S(1)}, u32[]{:S(2)}, u32[]{:S(2)}) collective-permute-start(f32[8,128]{1,0:T(8,128)S(1)} %get-tuple-element.45.refs_8_), channel_id=1, source_target_pairs={{0,1},{1,2},{2,3},{3,0},{4,5},{5,6},{6,7},{7,4},{8,9},{9,10},{10,1... | collective-permute-start | bytes 12296 | tf_op jit(solution)/shard_map/ppermute | solution.py:672
  119.8 1.4 %collective-permute-start.20 = (f32[8,128]{1,0:T(8,128)S(1)}, f32[8,128]{1,0:T(8,128)S(1)}, u32[]{:S(2)}, u32[]{:S(2)}) collective-permute-start(f32[8,128]{1,0:T(8,128)S(1)} %get-tuple-element.45.refs_8_), channel_id=1, source_target_pairs={{0,3},{1,0},{2,1},{3,2},{4,7},{5,4},{6,5},{7,6},{8,11},{9,8},{10,9... | collective-permute-start | bytes 12296 | tf_op jit(solution)/shard_map/ppermute | solution.py:672
  121.3 2.1 %collective-permute-done.19.refs_10_ = f32[8,128]{1,0:T(8,128)S(1)} collective-permute-done((f32[8,128]{1,0:T(8,128)S(1)}, f32[8,128]{1,0:T(8,128)S(1)}, u32[]{:S(2)}, u32[]{:S(2)}) %collective-permute-start.19) | collective-permute-done | bytes 4128 | tf_op jit(solution)/shard_map/ppermute | solution.py:672
  123.4 1.4 %finish.1 = (f32[3,2,4,4,128]{4,3,2,1,0:T(4,128)}, f32[3,2,4,4,128]{4,3,2,1,0:T(4,128)}, f32[3,2,4,4,128]{4,3,2,1,0:T(4,128)}, f32[3,2,4,4,128]{4,3,2,1,0:T(4,128)}) custom-call(f32[3,2,4,4,128]{4,3,2,1,0:T(4,128)S(1)} %get-tuple-element.36.refs_1_.refs_0_, f32[3,2,4,4,128]{4,3,2,1,0:T(4,128)S(1)} %get-tuple-element.43.refs_1_, ...), custom_call_target="tpu_custom_call" | custom-call | tf_op jit(solution)/shard_map/finish/pallas_call | solution.py:684
  (35 shorter events, 1.0 us)
Async XLA Ops:
  1.4 7.0 %collective-permute-start = (f32[3,1,4,4,128]{4,3,2,1,0:T(4,128)S(1)}, f32[3,1,4,4,128]{4,3,2,1,0:T(4,128)S(1)}, u32[]{:S(2)}, u32[]{:S(2)}) collective-permute-start(f32[3,1,4,4,128]{4,3,2,1,0:T(4,128)S(1)} %get-tuple-element.51), channel_id=1, source_target_pairs={{0,1},{1,2},{2,3},{3,0},{4,5},{5,6},{6,7},{7,4},{8,9},{9,10},{10,1... | collective-permute-start | bytes 73736 | tf_op jit(solution)/shard_map/ppermute | solution.py:597
  1.9 2.0 %slice-start = ((s32[13,2,4,4]{0,3,2,1:T(4,128)}), s32[13,1,4,4]{0,3,2,1:T(4,128)S(1)}, s32[]{:S(2)}) async-start(s32[13,2,4,4]{0,3,2,1:T(4,128)} %param.10), calls=%async_computation | async-start | bytes 16384 | tf_op jit(solution)/shard_map/slice | solution.py:599
  1.9 6.6 %collective-permute-start.1 = (f32[3,1,4,4,128]{4,3,2,1,0:T(4,128)S(1)}, f32[3,1,4,4,128]{4,3,2,1,0:T(4,128)S(1)}, u32[]{:S(2)}, u32[]{:S(2)}) collective-permute-start(f32[3,1,4,4,128]{4,3,2,1,0:T(4,128)S(1)} %get-tuple-element.50), channel_id=1, source_target_pairs={{0,3},{1,0},{2,1},{3,2},{4,7},{5,4},{6,5},{7,6},{8,11},{9,8},{10,9... | collective-permute-start | bytes 73736 | tf_op jit(solution)/shard_map/ppermute | solution.py:597
  3.9 1.5 %copy-start.2 = (s32[2,4,4]{2,1,0:T(4,128)S(1)}, s32[2,4,4]{2,1,0:T(4,128)}, u32[]{:S(2)}) copy-start(s32[2,4,4]{2,1,0:T(4,128)} %refs_4_.9) | copy-start | bytes 388
  3.9 3.2 %copy-start.4 = (s32[13,2,4,4]{0,3,2,1:T(4,128)S(1)}, s32[13,2,4,4]{0,3,2,1:T(4,128)}, u32[]{:S(2)}) copy-start(s32[13,2,4,4]{0,3,2,1:T(4,128)} %param.10) | copy-start | bytes 4996
  4.0 4.4 %copy-start = (f32[1,3,2,4,4,128]{5,4,3,2,1,0:T(4,128)S(1)}, f32[1,3,2,4,4,128]{5,4,3,2,1,0:T(4,128)}, u32[]{:S(2)}) copy-start(f32[1,3,2,4,4,128]{5,4,3,2,1,0:T(4,128)} %param.6) | copy-start | bytes 147460
  4.0 4.4 %collective-permute-start.4 = (s32[13,1,4,4]{3,2,1,0:T(4,128)S(1)}, s32[13,1,4,4]{3,2,1,0:T(4,128)S(1)}, u32[]{:S(2)}, u32[]{:S(2)}) collective-permute-start(s32[13,1,4,4]{3,2,1,0:T(4,128)S(1)} %copy.10), channel_id=1, source_target_pairs={{0,1},{1,2},{2,3},{3,0},{4,5},{5,6},{6,7},{7,4},{8,9},{9,10},{10,1... | collective-permute-start | bytes 2504 | tf_op jit(solution)/shard_map/ppermute | solution.py:599
  5.4 3.0 %collective-permute-start.2 = (s32[1,4,4]{2,1,0:T(4,128)S(1)}, s32[1,4,4]{2,1,0:T(4,128)S(1)}, u32[]{:S(2)}, u32[]{:S(2)}) collective-permute-start(s32[1,4,4]{2,1,0:T(4,128)S(1)} %get-tuple-element.53), channel_id=1, source_target_pairs={{0,1},{1,2},{2,3},{3,0},{4,5},{5,6},{6,7},{7,4},{8,9},{9,10},{10,1... | collective-permute-start | bytes 200 | tf_op jit(solution)/shard_map/ppermute | solution.py:597
  6.4 2.0 %collective-permute-start.3 = (s32[1,4,4]{2,1,0:T(4,128)S(1)}, s32[1,4,4]{2,1,0:T(4,128)S(1)}, u32[]{:S(2)}, u32[]{:S(2)}) collective-permute-start(s32[1,4,4]{2,1,0:T(4,128)S(1)} %get-tuple-element.52), channel_id=1, source_target_pairs={{0,3},{1,0},{2,1},{3,2},{4,7},{5,4},{6,5},{7,6},{8,11},{9,8},{10,9... | collective-permute-start | bytes 200 | tf_op jit(solution)/shard_map/ppermute | solution.py:597
  7.3 26.1 %copy-start.3 = (f32[1,3,2,4,4,128]{5,4,3,2,1,0:T(4,128)S(1)}, f32[1,3,2,4,4,128]{5,4,3,2,1,0:T(4,128)}, u32[]{:S(2)}) copy-start(f32[1,3,2,4,4,128]{5,4,3,2,1,0:T(4,128)} %param.7) | copy-start | bytes 147460
  30.2 3.1 %collective-permute-start.5 = (f32[1,4,4,128]{3,2,1,0:T(4,128)S(1)}, f32[1,4,4,128]{3,2,1,0:T(4,128)S(1)}, u32[]{:S(2)}, u32[]{:S(2)}) collective-permute-start(f32[1,4,4,128]{3,2,1,0:T(4,128)S(1)} %get-tuple-element.28), channel_id=1, source_target_pairs={{0,1},{1,2},{2,3},{3,0},{4,5},{5,6},{6,7},{7,4},{8,9},{9,10},{10,1... | collective-permute-start | bytes 24584 | tf_op jit(solution)/shard_map/ppermute | solution.py:597
  32.0 1.4 %collective-permute-start.6 = (f32[1,4,4,128]{3,2,1,0:T(4,128)S(1)}, f32[1,4,4,128]{3,2,1,0:T(4,128)S(1)}, u32[]{:S(2)}, u32[]{:S(2)}) collective-permute-start(f32[1,4,4,128]{3,2,1,0:T(4,128)S(1)} %get-tuple-element.30), channel_id=1, source_target_pairs={{0,3},{1,0},{2,1},{3,2},{4,7},{5,4},{6,5},{7,6},{8,11},{9,8},{10,9... | collective-permute-start | bytes 24584 | tf_op jit(solution)/shard_map/ppermute | solution.py:597
  58.1 6.3 %collective-permute-start.14 = (f32[6,2,4,4,128]{4,3,2,1,0:T(4,128)S(1)}, f32[6,2,4,4,128]{4,3,2,1,0:T(4,128)S(1)}, u32[]{:S(2)}, u32[]{:S(2)}) collective-permute-start(f32[6,2,4,4,128]{4,3,2,1,0:T(4,128)S(1)} %pad_maximum_fusion), channel_id=1, source_target_pairs={{0,12},{4,0},{8,4},{12,8},{16,28},{20,16},{24,20},{28,24},{1,13},{... | collective-permute-start | bytes 294920 | tf_op jit(solution)/shard_map/ppermute | solution.py:629
  60.6 5.7 %collective-permute-start.15 = (f32[6,2,4,4,128]{4,3,2,1,0:T(4,128)S(1)}, f32[6,2,4,4,128]{4,3,2,1,0:T(4,128)S(1)}, u32[]{:S(2)}, u32[]{:S(2)}) collective-permute-start(f32[6,2,4,4,128]{4,3,2,1,0:T(4,128)S(1)} %pad_maximum_fusion), channel_id=1, source_target_pairs={{0,8},{4,12},{8,0},{12,4},{16,24},{20,28},{24,16},{28,20},{1,9},{5... | collective-permute-start | bytes 294920 | tf_op jit(solution)/shard_map/ppermute | solution.py:629
  61.1 6.0 %collective-permute-start.16 = (f32[6,2,4,4,128]{4,3,2,1,0:T(4,128)S(1)}, f32[6,2,4,4,128]{4,3,2,1,0:T(4,128)S(1)}, u32[]{:S(2)}, u32[]{:S(2)}) collective-permute-start(f32[6,2,4,4,128]{4,3,2,1,0:T(4,128)S(1)} %pad_maximum_fusion), channel_id=1, source_target_pairs={{0,4},{4,8},{8,12},{12,0},{16,20},{20,24},{24,28},{28,16},{1,5},{5... | collective-permute-start | bytes 294920 | tf_op jit(solution)/shard_map/ppermute | solution.py:629
  61.7 0.7 copy-start.5
  62.5 11.7 %collective-permute-start.7 = (f32[6,1,4,4,128]{4,3,2,1,0:T(4,128)S(1)}, f32[6,1,4,4,128]{4,3,2,1,0:T(4,128)S(1)}, u32[]{:S(2)}, u32[]{:S(2)}) collective-permute-start(f32[6,1,4,4,128]{4,3,2,1,0:T(4,128)S(1)} %get-tuple-element.33), channel_id=1, source_target_pairs={{0,1},{1,2},{2,3},{3,0},{4,5},{5,6},{6,7},{7,4},{8,9},{9,10},{10,1... | collective-permute-start | bytes 147464 | tf_op jit(solution)/shard_map/ppermute | solution.py:597
  63.8 10.4 %collective-permute-start.8 = (f32[6,1,4,4,128]{4,3,2,1,0:T(4,128)S(1)}, f32[6,1,4,4,128]{4,3,2,1,0:T(4,128)S(1)}, u32[]{:S(2)}, u32[]{:S(2)}) collective-permute-start(f32[6,1,4,4,128]{4,3,2,1,0:T(4,128)S(1)} %get-tuple-element.34), channel_id=1, source_target_pairs={{0,3},{1,0},{2,1},{3,2},{4,7},{5,4},{6,5},{7,6},{8,11},{9,8},{10,9... | collective-permute-start | bytes 147464 | tf_op jit(solution)/shard_map/ppermute | solution.py:597
  67.2 56.2 %collective-permute-start.17 = (f32[6,2,4,4,128]{4,3,2,1,0:T(4,128)S(1)}, f32[6,2,4,4,128]{4,3,2,1,0:T(4,128)S(1)}, u32[]{:S(2)}, u32[]{:S(2)}) collective-permute-start(f32[6,2,4,4,128]{4,3,2,1,0:T(4,128)S(1)} %select_select_fusion.refs_6_), channel_id=1, source_target_pairs={{0,16},{4,20},{8,24},{12,28},{16,0},{20,4},{24,8},{28,12},{1,17},{... | collective-permute-start | bytes 294920 | tf_op jit(solution)/shard_map/ppermute | solution.py:629
  69.8 3.0 %collective-permute-start.9 = (f32[8,128]{1,0:T(8,128)S(1)}, f32[8,128]{1,0:T(8,128)S(1)}, u32[]{:S(2)}, u32[]{:S(2)}) collective-permute-start(f32[8,128]{1,0:T(8,128)S(1)} %get-tuple-element.35.refs_11_), channel_id=1, source_target_pairs={{0,1},{1,2},{2,3},{3,0},{4,5},{5,6},{6,7},{7,4},{8,9},{9,10},{10,1... | collective-permute-start | bytes 12296 | tf_op jit(solution)/shard_map/ppermute | solution.py:672
  69.9 3.6 %collective-permute-start.10 = (f32[8,128]{1,0:T(8,128)S(1)}, f32[8,128]{1,0:T(8,128)S(1)}, u32[]{:S(2)}, u32[]{:S(2)}) collective-permute-start(f32[8,128]{1,0:T(8,128)S(1)} %get-tuple-element.35.refs_11_), channel_id=1, source_target_pairs={{0,2},{1,3},{2,0},{3,1},{4,6},{5,7},{6,4},{7,5},{8,10},{9,11},{10,... | collective-permute-start | bytes 12296 | tf_op jit(solution)/shard_map/ppermute | solution.py:672
  72.9 1.3 %collective-permute-start.11 = (f32[8,128]{1,0:T(8,128)S(1)}, f32[8,128]{1,0:T(8,128)S(1)}, u32[]{:S(2)}, u32[]{:S(2)}) collective-permute-start(f32[8,128]{1,0:T(8,128)S(1)} %get-tuple-element.35.refs_11_), channel_id=1, source_target_pairs={{0,3},{1,0},{2,1},{3,2},{4,7},{5,4},{6,5},{7,6},{8,11},{9,8},{10,9... | collective-permute-start | bytes 12296 | tf_op jit(solution)/shard_map/ppermute | solution.py:672
  90.3 3.1 %collective-permute-start.12 = (f32[1,4,4,128]{3,2,1,0:T(4,128)S(1)}, f32[1,4,4,128]{3,2,1,0:T(4,128)S(1)}, u32[]{:S(2)}, u32[]{:S(2)}) collective-permute-start(f32[1,4,4,128]{3,2,1,0:T(4,128)S(1)} %get-tuple-element.39), channel_id=1, source_target_pairs={{0,1},{1,2},{2,3},{3,0},{4,5},{5,6},{6,7},{7,4},{8,9},{9,10},{10,1... | collective-permute-start | bytes 24584 | tf_op jit(solution)/shard_map/ppermute | solution.py:597
  91.7 1.7 %collective-permute-start.13 = (f32[1,4,4,128]{3,2,1,0:T(4,128)S(1)}, f32[1,4,4,128]{3,2,1,0:T(4,128)S(1)}, u32[]{:S(2)}, u32[]{:S(2)}) collective-permute-start(f32[1,4,4,128]{3,2,1,0:T(4,128)S(1)} %get-tuple-element.41), channel_id=1, source_target_pairs={{0,3},{1,0},{2,1},{3,2},{4,7},{5,4},{6,5},{7,6},{8,11},{9,8},{10,9... | collective-permute-start | bytes 24584 | tf_op jit(solution)/shard_map/ppermute | solution.py:597
  118.0 3.3 %collective-permute-start.18 = (f32[8,128]{1,0:T(8,128)S(1)}, f32[8,128]{1,0:T(8,128)S(1)}, u32[]{:S(2)}, u32[]{:S(2)}) collective-permute-start(f32[8,128]{1,0:T(8,128)S(1)} %get-tuple-element.45.refs_8_), channel_id=1, source_target_pairs={{0,1},{1,2},{2,3},{3,0},{4,5},{5,6},{6,7},{7,4},{8,9},{9,10},{10,1... | collective-permute-start | bytes 12296 | tf_op jit(solution)/shard_map/ppermute | solution.py:672
  119.8 3.6 %collective-permute-start.19 = (f32[8,128]{1,0:T(8,128)S(1)}, f32[8,128]{1,0:T(8,128)S(1)}, u32[]{:S(2)}, u32[]{:S(2)}) collective-permute-start(f32[8,128]{1,0:T(8,128)S(1)} %get-tuple-element.45.refs_8_), channel_id=1, source_target_pairs={{0,2},{1,3},{2,0},{3,1},{4,6},{5,7},{6,4},{7,5},{8,10},{9,11},{10,... | collective-permute-start | bytes 12296 | tf_op jit(solution)/shard_map/ppermute | solution.py:672
  119.8 3.6 %collective-permute-start.20 = (f32[8,128]{1,0:T(8,128)S(1)}, f32[8,128]{1,0:T(8,128)S(1)}, u32[]{:S(2)}, u32[]{:S(2)}) collective-permute-start(f32[8,128]{1,0:T(8,128)S(1)} %get-tuple-element.45.refs_8_), channel_id=1, source_target_pairs={{0,3},{1,0},{2,1},{3,2},{4,7},{5,4},{6,5},{7,6},{8,11},{9,8},{10,9... | collective-permute-start | bytes 12296 | tf_op jit(solution)/shard_map/ppermute | solution.py:672
  121.2 2.2 %copy-start.1 = (f32[1,1,3,2,4,4,128]{6,5,4,3,2,1,0:T(4,128)S(1)}, f32[1,1,3,2,4,4,128]{6,5,4,3,2,1,0:T(4,128)}, u32[]{:S(2)}) copy-start(f32[1,1,3,2,4,4,128]{6,5,4,3,2,1,0:T(4,128)} %param.8) | copy-start | bytes 147460
